TPU v7x, 256 devices: a whole 4x4x8 slice. The times are simulated.
256 devices in a mesh: illum: 32 (over z_hi, x, y), row: 8 (over z_lo, core).
Axes of the slice: x: 4, y: 4, z: 8 (z_hi: 2, z_lo: 4; z = z_hi * 4 + z_lo), core: 2. Of those that a mesh axis runs over, the one named last changes fastest.
Arguments:
- angles: int32 [128, 2], P('illum'), may hold values from -8 to 8
- depth_order: int32 [3], replicated, may hold values from 0 to 31, as said below
- slices: float32 [32, 64, 4096], P('illum', 'row'), may hold values from -4 to 4
- cotangent: float32 [128, 2, 64, 4096], P('illum', None, 'row'), may hold values from -0.6 to 0.6
Outputs:
- exit_field: float32 [128, 2, 64, 4096], P('illum', None, 'row')
- slice_grad: float32 [32, 64, 4096], P('illum', 'row')
Inputs may be any that keep to these rules, and one draw needn't show every extreme that they name: `depth_order`: 3 distinct slice numbers; slice 0 and the last slice are always among them.
All inputs are finite; a program needn't handle non-finite values.
Results may differ from a plain program's by a relative error of at most 0.0001.
Values sent between devices are 32-bit elements; how exact they have to be, the bound alone decides.
No kernel may reach another device: no remote copies, remote signals or barrier semaphores. Data moves between devices by JAX's collectives and lax.ppermute only.
A program may use at most 64 MiB of HBM per device.

v0:
```python
import math

import jax
import jax.numpy as jnp
from jax import lax
from jax.sharding import PartitionSpec as P

rate_scale = 0.3


def extended(array, sides, width):
    for axis, dim in sides:
        peers, length = (lax.axis_size(axis), array.shape[dim])
        up = [(i, (i + 1) % peers) for i in range(peers - 1)]
        down = [(j, i) for i, j in up]
        last = lax.slice_in_dim(array, length - width, length, axis=dim)
        initial = lax.slice_in_dim(array, 0, width, axis=dim)
        before = lax.ppermute(last, axis, up)
        after = lax.ppermute(initial, axis, down)
        array = jnp.concatenate([before, array, after], axis=dim)
    return array


def broadcast(block, axis, holder):
    block = jnp.where(lax.axis_index(axis) == holder, block, jnp.zeros_like(block))
    return lax.psum(block, axis)


def laplace_padded(padded):
    framed = jnp.pad(padded, ((0, 0), (0, 0), (0, 0), (1, 1)))
    centre = framed[:, :, 1:-1, 1:-1]
    return (
        framed[:, :, 2:, 1:-1]
        + framed[:, :, :-2, 1:-1]
        + (framed[:, :, 1:-1, 2:] + framed[:, :, 1:-1, :-2])
        - 4.0 * centre
    )


def forward_rate(field):
    padded = extended(field, (("row", 2),), 1)
    curved = laplace_padded(padded)
    return jnp.stack([-rate_scale * curved[:, 1], rate_scale * curved[:, 0]], axis=1)


def adjoint_rate(field):
    padded = extended(field, (("row", 2),), 1)
    curved = laplace_padded(padded)
    factor = -rate_scale
    return jnp.stack([-factor * curved[:, 1], factor * curved[:, 0]], axis=1)


def runge_step(field, rate_fn):
    slope_one = rate_fn(field)
    slope_two = rate_fn(field + 0.5 * slope_one)
    slope_three = rate_fn(field + 0.5 * slope_two)
    slope_four = rate_fn(field + slope_three)
    return field + (slope_one + 2.0 * slope_two + 2.0 * slope_three + slope_four) / 6.0


def rotate(field, phase):
    cosine = jnp.cos(phase)
    sine = jnp.sin(phase)
    real_part = field[:, 0]
    imag_part = field[:, 1]
    return jnp.stack(
        [cosine * real_part - sine * imag_part, sine * real_part + cosine * imag_part], axis=1
    )


def inner_term(adjoint, stored):
    return jnp.sum(-adjoint[:, 0] * stored[:, 1] + adjoint[:, 1] * stored[:, 0], axis=0)


def body(angles, depth_order, slices, cotangent):
    rows = slices.shape[1]
    cols = slices.shape[2]
    layers = depth_order.shape[0]
    owner_count = lax.axis_size("illum")
    total_rows = rows * lax.axis_size("row")
    first_row = lax.axis_index("row") * rows
    rows_idx = first_row + jnp.arange(rows, dtype=jnp.int32)
    cols_idx = jnp.arange(cols, dtype=jnp.int32)
    phase_rows = (
        2.0
        * math.pi
        * (angles[:, 0:1] * rows_idx[None, :] % total_rows).astype(jnp.float32)
        / total_rows
    )
    phase_cols = (
        2.0 * math.pi * (angles[:, 1:2] * cols_idx[None, :] % cols).astype(jnp.float32) / cols
    )
    phase = phase_rows[:, :, None] + phase_cols[:, None, :]
    field = jnp.stack([jnp.cos(phase), jnp.sin(phase)], axis=1)
    chosen = [broadcast(slices[0], "illum", depth_order[layer]) for layer in range(layers)]
    kept = [None] * layers
    terms = [None] * layers
    adjoint = cotangent
    for layer in range(layers):
        field = rotate(field, chosen[layer])
        kept[layer] = field
        field = runge_step(field, forward_rate)
    for layer in range(layers - 1, -1, -1):
        adjoint = runge_step(adjoint, adjoint_rate)
        terms[layer] = inner_term(adjoint, kept[layer])
        adjoint = rotate(adjoint, -chosen[layer])
    grads = jnp.stack(terms, axis=0)
    owners = jnp.arange(owner_count, dtype=jnp.int32)
    buffer = jnp.zeros((owner_count, rows, cols), jnp.float32)
    for layer in range(layers):
        picked = (owners == depth_order[layer]).astype(jnp.float32)
        buffer = buffer + picked[:, None, None] * grads[layer][None]
    slice_grad = lax.psum_scatter(buffer, "illum", scatter_dimension=0, tiled=True)
    return (field, slice_grad)


def solution(mesh):
    placed = (P("illum", None), P(), P("illum", "row", None), P("illum", None, "row", None))
    return jax.shard_map(
        body,
        mesh=mesh,
        in_specs=placed,
        out_specs=(P("illum", None, "row", None), P("illum", "row", None)),
        check_vma=False,
    )
```

profile of v0, /device:TPU:32, one launch (start us, length us, event | category | flops | bytes accessed | tf_op | source)
XLA Modules:
  0.0 844.7 jit_solution(2397940869130016920)
XLA Ops:
  7.2 1.9 copy.96
  9.2 1.9 collective-permute-start.24
  11.1 2.4 collective-permute-start.25
  21.2 2.8 collective-permute-start.26
  24.0 2.0 collective-permute-start.27
  26.5 3.8 collective-permute-done.27
  34.9 2.4 collective-permute-start.29
  39.2 2.0 collective-permute-done.29
  46.5 2.4 collective-permute-start.31
  48.9 386.7 %all-reduce.27.cloned.1.call-done = (f32[8,4096]{1,0:T(8,128)}, f32[8,4096]{1,0:T(8,128)}, f32[8,4096]{1,0:T(8,128)}) async-done(((f32[8,4096]{1,0:T(8,128)}, f32[8,4096]{1,0:T(8,128)}, f32[8,4096]{1,0:T(8,128)}), (f32[8,4096]{1,0:T(8,128)}, f32[8,4096]{1,0:T(8,128)}, f32[8,4096]{1,0:T(8,128)})) %all-reduce.27.cloned.1.call-update) | async-done | bytes 393232 | tf_op jit(solution)/shard_map/psum | solution.py:26
  437.0 4.2 fusion.105
  441.3 1.9 collective-permute-start
  443.2 2.6 collective-permute-start.1
  452.7 3.2 collective-permute-start.32
  455.8 1.9 collective-permute-start.33
  460.3 3.6 collective-permute-start.2
  468.5 3.6 collective-permute-start.34
  476.3 3.6 collective-permute-start.4
  479.9 2.3 collective-permute-start.5
  484.5 3.6 collective-permute-start.36
  492.2 3.6 collective-permute-start.6
  500.0 3.6 collective-permute-start.38
  503.6 1.9 collective-permute-start.39
  508.9 3.6 collective-permute-start.8
  512.5 2.1 collective-permute-start.9
  517.9 3.6 collective-permute-start.40
  526.1 3.6 collective-permute-start.10
  535.0 3.6 collective-permute-start.42
  538.6 1.9 collective-permute-start.43
  542.7 3.6 collective-permute-start.12
  546.4 2.1 collective-permute-start.13
  550.7 3.6 collective-permute-start.44
  558.5 3.6 collective-permute-start.14
  566.2 3.6 collective-permute-start.46
  569.9 1.9 collective-permute-start.47
  575.1 3.6 collective-permute-start.16
  578.8 2.2 collective-permute-start.17
  584.6 4.7 fusion.117
  592.6 3.6 collective-permute-start.18
  596.2 1.9 collective-permute-start.19
  598.1 2.9 multiply_add_fusion
  604.7 2.2 collective-permute-start.20
  607.0 2.1 collective-permute-start.21
  609.5 4.5 collective-permute-done.21
  616.1 1.9 collective-permute-start.22
  618.1 2.7 collective-permute-start.23
  620.8 6.2 collective-permute-done.23
  631.5 205.9 %reduce-scatter.2.cloned.1.call-done = f32[1,8,4096]{2,1,0:T(8,128)} async-done(((f32[32,8,4096]{2,1,0:T(8,128)}), f32[1,8,4096]{2,1,0:T(8,128)}) %reduce-scatter.2.cloned.1.call-update) | async-done | bytes 131088 | tf_op jit(solution)/shard_map/reduce_scatter | solution.py:113
  (223 shorter events, 96.5 us)
Async XLA Ops:
  7.2 428.4 %all-reduce.27.cloned.1.call-start = ((), (), s32[]{:S(2)}) async-start(), calls=%async_computation.2 | async-start | bytes 786432 | tf_op jit(solution)/shard_map/psum | solution.py:26
  9.2 7.8 collective-permute-start.24
  11.1 6.5 collective-permute-start.25
  16.8 820.6 %reduce-scatter.2.cloned.1.call-start = ((), (), s32[]{:S(2)}) async-start(), calls=%async_computation.1 | async-start | bytes 4325376 | tf_op jit(solution)/shard_map/reduce_scatter | solution.py:113
  21.2 5.3 collective-permute-start.26
  24.0 6.3 collective-permute-start.27
  33.0 6.2 collective-permute-start.28
  34.9 6.3 collective-permute-start.29
  44.6 403.2 %collective-permute-start.30 = (f32[4,2,1,4096]{3,0,2,1:T(4,128)}, f32[4,2,1,4096]{3,0,2,1:T(4,128)S(1)}, u32[]{:S(2)}, u32[]{:S(2)}) collective-permute-start(f32[4,2,1,4096]{3,0,2,1:T(4,128)} %get-tuple-element.50), channel_id=1, source_target_pairs={{1,0},{2,1},{3,2},{4,3},{5,4},{6,5},{7,6},{9,8},{10,9},{11,10},{12... | collective-permute-start | bytes 393224 | tf_op jit(solution)/shard_map/ppermute | solution.py:19
  46.5 401.3 %collective-permute-start.31 = (f32[4,2,1,4096]{3,0,2,1:T(4,128)}, f32[4,2,1,4096]{3,0,2,1:T(4,128)S(1)}, u32[]{:S(2)}, u32[]{:S(2)}) collective-permute-start(f32[4,2,1,4096]{3,0,2,1:T(4,128)} %get-tuple-element.49), channel_id=1, source_target_pairs={{0,1},{1,2},{2,3},{3,4},{4,5},{5,6},{6,7},{8,9},{9,10},{10,11},{11... | collective-permute-start | bytes 393224 | tf_op jit(solution)/shard_map/ppermute | solution.py:18
  441.3 16.5 %collective-permute-start = (f32[4,2,1,4096]{3,0,2,1:T(4,128)S(1)}, f32[4,2,1,4096]{3,0,2,1:T(4,128)S(1)}, u32[]{:S(2)}, u32[]{:S(2)}) collective-permute-start(f32[4,2,1,4096]{3,0,2,1:T(4,128)S(1)} %get-tuple-element.110), channel_id=1, source_target_pairs={{1,0},{2,1},{3,2},{4,3},{5,4},{6,5},{7,6},{9,8},{10,9},{11,10},{12... | collective-permute-start | bytes 393224 | tf_op jit(solution)/shard_map/ppermute | solution.py:19
  443.2 14.6 %collective-permute-start.1 = (f32[4,2,1,4096]{3,0,2,1:T(4,128)S(1)}, f32[4,2,1,4096]{3,0,2,1:T(4,128)S(1)}, u32[]{:S(2)}, u32[]{:S(2)}) collective-permute-start(f32[4,2,1,4096]{3,0,2,1:T(4,128)S(1)} %get-tuple-element.109), channel_id=1, source_target_pairs={{0,1},{1,2},{2,3},{3,4},{4,5},{5,6},{6,7},{8,9},{9,10},{10,11},{11... | collective-permute-start | bytes 393224 | tf_op jit(solution)/shard_map/ppermute | solution.py:18
  452.7 13.3 %collective-permute-start.32 = (f32[4,2,1,4096]{3,0,2,1:T(4,128)S(1)}, f32[4,2,1,4096]{3,0,2,1:T(4,128)S(1)}, u32[]{:S(2)}, u32[]{:S(2)}) collective-permute-start(f32[4,2,1,4096]{3,0,2,1:T(4,128)S(1)} %get-tuple-element.46), channel_id=1, source_target_pairs={{1,0},{2,1},{3,2},{4,3},{5,4},{6,5},{7,6},{9,8},{10,9},{11,10},{12... | collective-permute-start | bytes 393224 | tf_op jit(solution)/shard_map/ppermute | solution.py:19
  455.8 10.1 %collective-permute-start.33 = (f32[4,2,1,4096]{3,0,2,1:T(4,128)S(1)}, f32[4,2,1,4096]{3,0,2,1:T(4,128)S(1)}, u32[]{:S(2)}, u32[]{:S(2)}) collective-permute-start(f32[4,2,1,4096]{3,0,2,1:T(4,128)S(1)} %get-tuple-element.45), channel_id=1, source_target_pairs={{0,1},{1,2},{2,3},{3,4},{4,5},{5,6},{6,7},{8,9},{9,10},{10,11},{11... | collective-permute-start | bytes 393224 | tf_op jit(solution)/shard_map/ppermute | solution.py:18
  460.3 13.8 %collective-permute-start.2 = (f32[4,2,1,4096]{3,0,2,1:T(4,128)S(1)}, f32[4,2,1,4096]{3,0,2,1:T(4,128)S(1)}, u32[]{:S(2)}, u32[]{:S(2)}) collective-permute-start(f32[4,2,1,4096]{3,0,2,1:T(4,128)S(1)} %get-tuple-element.106), channel_id=1, source_target_pairs={{1,0},{2,1},{3,2},{4,3},{5,4},{6,5},{7,6},{9,8},{10,9},{11,10},{12... | collective-permute-start | bytes 393224 | tf_op jit(solution)/shard_map/ppermute | solution.py:19
  464.0 10.1 %collective-permute-start.3 = (f32[4,2,1,4096]{3,0,2,1:T(4,128)S(1)}, f32[4,2,1,4096]{3,0,2,1:T(4,128)S(1)}, u32[]{:S(2)}, u32[]{:S(2)}) collective-permute-start(f32[4,2,1,4096]{3,0,2,1:T(4,128)S(1)} %get-tuple-element.105), channel_id=1, source_target_pairs={{0,1},{1,2},{2,3},{3,4},{4,5},{5,6},{6,7},{8,9},{9,10},{10,11},{11... | collective-permute-start | bytes 393224 | tf_op jit(solution)/shard_map/ppermute | solution.py:18
  468.5 13.8 %collective-permute-start.34 = (f32[4,2,1,4096]{3,0,2,1:T(4,128)S(1)}, f32[4,2,1,4096]{3,0,2,1:T(4,128)S(1)}, u32[]{:S(2)}, u32[]{:S(2)}) collective-permute-start(f32[4,2,1,4096]{3,0,2,1:T(4,128)S(1)} %get-tuple-element.42), channel_id=1, source_target_pairs={{1,0},{2,1},{3,2},{4,3},{5,4},{6,5},{7,6},{9,8},{10,9},{11,10},{12... | collective-permute-start | bytes 393224 | tf_op jit(solution)/shard_map/ppermute | solution.py:19
  472.2 10.1 %collective-permute-start.35 = (f32[4,2,1,4096]{3,0,2,1:T(4,128)S(1)}, f32[4,2,1,4096]{3,0,2,1:T(4,128)S(1)}, u32[]{:S(2)}, u32[]{:S(2)}) collective-permute-start(f32[4,2,1,4096]{3,0,2,1:T(4,128)S(1)} %get-tuple-element.41), channel_id=1, source_target_pairs={{0,1},{1,2},{2,3},{3,4},{4,5},{5,6},{6,7},{8,9},{9,10},{10,11},{11... | collective-permute-start | bytes 393224 | tf_op jit(solution)/shard_map/ppermute | solution.py:18
  476.3 13.8 %collective-permute-start.4 = (f32[4,2,1,4096]{3,0,2,1:T(4,128)S(1)}, f32[4,2,1,4096]{3,0,2,1:T(4,128)S(1)}, u32[]{:S(2)}, u32[]{:S(2)}) collective-permute-start(f32[4,2,1,4096]{3,0,2,1:T(4,128)S(1)} %get-tuple-element.102), channel_id=1, source_target_pairs={{1,0},{2,1},{3,2},{4,3},{5,4},{6,5},{7,6},{9,8},{10,9},{11,10},{12... | collective-permute-start | bytes 393224 | tf_op jit(solution)/shard_map/ppermute | solution.py:19
  479.9 10.1 %collective-permute-start.5 = (f32[4,2,1,4096]{3,0,2,1:T(4,128)S(1)}, f32[4,2,1,4096]{3,0,2,1:T(4,128)S(1)}, u32[]{:S(2)}, u32[]{:S(2)}) collective-permute-start(f32[4,2,1,4096]{3,0,2,1:T(4,128)S(1)} %get-tuple-element.101), channel_id=1, source_target_pairs={{0,1},{1,2},{2,3},{3,4},{4,5},{5,6},{6,7},{8,9},{9,10},{10,11},{11... | collective-permute-start | bytes 393224 | tf_op jit(solution)/shard_map/ppermute | solution.py:18
  484.5 13.3 %collective-permute-start.36 = (f32[4,2,1,4096]{3,0,2,1:T(4,128)S(1)}, f32[4,2,1,4096]{3,0,2,1:T(4,128)S(1)}, u32[]{:S(2)}, u32[]{:S(2)}) collective-permute-start(f32[4,2,1,4096]{3,0,2,1:T(4,128)S(1)} %get-tuple-element.38), channel_id=1, source_target_pairs={{1,0},{2,1},{3,2},{4,3},{5,4},{6,5},{7,6},{9,8},{10,9},{11,10},{12... | collective-permute-start | bytes 393224 | tf_op jit(solution)/shard_map/ppermute | solution.py:19
  488.1 9.7 %collective-permute-start.37 = (f32[4,2,1,4096]{3,0,2,1:T(4,128)S(1)}, f32[4,2,1,4096]{3,0,2,1:T(4,128)S(1)}, u32[]{:S(2)}, u32[]{:S(2)}) collective-permute-start(f32[4,2,1,4096]{3,0,2,1:T(4,128)S(1)} %get-tuple-element.37), channel_id=1, source_target_pairs={{0,1},{1,2},{2,3},{3,4},{4,5},{5,6},{6,7},{8,9},{9,10},{10,11},{11... | collective-permute-start | bytes 393224 | tf_op jit(solution)/shard_map/ppermute | solution.py:18
  492.2 13.3 %collective-permute-start.6 = (f32[4,2,1,4096]{3,0,2,1:T(4,128)S(1)}, f32[4,2,1,4096]{3,0,2,1:T(4,128)S(1)}, u32[]{:S(2)}, u32[]{:S(2)}) collective-permute-start(f32[4,2,1,4096]{3,0,2,1:T(4,128)S(1)} %get-tuple-element.98), channel_id=1, source_target_pairs={{1,0},{2,1},{3,2},{4,3},{5,4},{6,5},{7,6},{9,8},{10,9},{11,10},{12... | collective-permute-start | bytes 393224 | tf_op jit(solution)/shard_map/ppermute | solution.py:19
  495.9 9.7 %collective-permute-start.7 = (f32[4,2,1,4096]{3,0,2,1:T(4,128)S(1)}, f32[4,2,1,4096]{3,0,2,1:T(4,128)S(1)}, u32[]{:S(2)}, u32[]{:S(2)}) collective-permute-start(f32[4,2,1,4096]{3,0,2,1:T(4,128)S(1)} %get-tuple-element.97), channel_id=1, source_target_pairs={{0,1},{1,2},{2,3},{3,4},{4,5},{5,6},{6,7},{8,9},{9,10},{10,11},{11... | collective-permute-start | bytes 393224 | tf_op jit(solution)/shard_map/ppermute | solution.py:18
  500.0 14.6 %collective-permute-start.38 = (f32[4,2,1,4096]{3,0,2,1:T(4,128)S(1)}, f32[4,2,1,4096]{3,0,2,1:T(4,128)S(1)}, u32[]{:S(2)}, u32[]{:S(2)}) collective-permute-start(f32[4,2,1,4096]{3,0,2,1:T(4,128)S(1)} %get-tuple-element.34), channel_id=1, source_target_pairs={{1,0},{2,1},{3,2},{4,3},{5,4},{6,5},{7,6},{9,8},{10,9},{11,10},{12... | collective-permute-start | bytes 393224 | tf_op jit(solution)/shard_map/ppermute | solution.py:19
  503.6 11.0 %collective-permute-start.39 = (f32[4,2,1,4096]{3,0,2,1:T(4,128)S(1)}, f32[4,2,1,4096]{3,0,2,1:T(4,128)S(1)}, u32[]{:S(2)}, u32[]{:S(2)}) collective-permute-start(f32[4,2,1,4096]{3,0,2,1:T(4,128)S(1)} %get-tuple-element.33), channel_id=1, source_target_pairs={{0,1},{1,2},{2,3},{3,4},{4,5},{5,6},{6,7},{8,9},{9,10},{10,11},{11... | collective-permute-start | bytes 393224 | tf_op jit(solution)/shard_map/ppermute | solution.py:18
  508.9 14.6 %collective-permute-start.8 = (f32[4,2,1,4096]{3,0,2,1:T(4,128)S(1)}, f32[4,2,1,4096]{3,0,2,1:T(4,128)S(1)}, u32[]{:S(2)}, u32[]{:S(2)}) collective-permute-start(f32[4,2,1,4096]{3,0,2,1:T(4,128)S(1)} %get-tuple-element.94), channel_id=1, source_target_pairs={{1,0},{2,1},{3,2},{4,3},{5,4},{6,5},{7,6},{9,8},{10,9},{11,10},{12... | collective-permute-start | bytes 393224 | tf_op jit(solution)/shard_map/ppermute | solution.py:19
  512.5 11.0 %collective-permute-start.9 = (f32[4,2,1,4096]{3,0,2,1:T(4,128)S(1)}, f32[4,2,1,4096]{3,0,2,1:T(4,128)S(1)}, u32[]{:S(2)}, u32[]{:S(2)}) collective-permute-start(f32[4,2,1,4096]{3,0,2,1:T(4,128)S(1)} %get-tuple-element.93), channel_id=1, source_target_pairs={{0,1},{1,2},{2,3},{3,4},{4,5},{5,6},{6,7},{8,9},{9,10},{10,11},{11... | collective-permute-start | bytes 393224 | tf_op jit(solution)/shard_map/ppermute | solution.py:18
  517.9 14.5 %collective-permute-start.40 = (f32[4,2,1,4096]{3,0,2,1:T(4,128)S(1)}, f32[4,2,1,4096]{3,0,2,1:T(4,128)S(1)}, u32[]{:S(2)}, u32[]{:S(2)}) collective-permute-start(f32[4,2,1,4096]{3,0,2,1:T(4,128)S(1)} %get-tuple-element.30), channel_id=1, source_target_pairs={{1,0},{2,1},{3,2},{4,3},{5,4},{6,5},{7,6},{9,8},{10,9},{11,10},{12... | collective-permute-start | bytes 393224 | tf_op jit(solution)/shard_map/ppermute | solution.py:19
  521.5 10.9 %collective-permute-start.41 = (f32[4,2,1,4096]{3,0,2,1:T(4,128)S(1)}, f32[4,2,1,4096]{3,0,2,1:T(4,128)S(1)}, u32[]{:S(2)}, u32[]{:S(2)}) collective-permute-start(f32[4,2,1,4096]{3,0,2,1:T(4,128)S(1)} %get-tuple-element.29), channel_id=1, source_target_pairs={{0,1},{1,2},{2,3},{3,4},{4,5},{5,6},{6,7},{8,9},{9,10},{10,11},{11... | collective-permute-start | bytes 393224 | tf_op jit(solution)/shard_map/ppermute | solution.py:18
  526.1 14.5 %collective-permute-start.10 = (f32[4,2,1,4096]{3,0,2,1:T(4,128)S(1)}, f32[4,2,1,4096]{3,0,2,1:T(4,128)S(1)}, u32[]{:S(2)}, u32[]{:S(2)}) collective-permute-start(f32[4,2,1,4096]{3,0,2,1:T(4,128)S(1)} %get-tuple-element.90), channel_id=1, source_target_pairs={{1,0},{2,1},{3,2},{4,3},{5,4},{6,5},{7,6},{9,8},{10,9},{11,10},{12... | collective-permute-start | bytes 393224 | tf_op jit(solution)/shard_map/ppermute | solution.py:19
  529.7 10.9 %collective-permute-start.11 = (f32[4,2,1,4096]{3,0,2,1:T(4,128)S(1)}, f32[4,2,1,4096]{3,0,2,1:T(4,128)S(1)}, u32[]{:S(2)}, u32[]{:S(2)}) collective-permute-start(f32[4,2,1,4096]{3,0,2,1:T(4,128)S(1)} %get-tuple-element.89), channel_id=1, source_target_pairs={{0,1},{1,2},{2,3},{3,4},{4,5},{5,6},{6,7},{8,9},{9,10},{10,11},{11... | collective-permute-start | bytes 393224 | tf_op jit(solution)/shard_map/ppermute | solution.py:18
  535.0 13.6 %collective-permute-start.42 = (f32[4,2,1,4096]{3,0,2,1:T(4,128)S(1)}, f32[4,2,1,4096]{3,0,2,1:T(4,128)S(1)}, u32[]{:S(2)}, u32[]{:S(2)}) collective-permute-start(f32[4,2,1,4096]{3,0,2,1:T(4,128)S(1)} %get-tuple-element.26), channel_id=1, source_target_pairs={{1,0},{2,1},{3,2},{4,3},{5,4},{6,5},{7,6},{9,8},{10,9},{11,10},{12... | collective-permute-start | bytes 393224 | tf_op jit(solution)/shard_map/ppermute | solution.py:19
  538.6 9.9 %collective-permute-start.43 = (f32[4,2,1,4096]{3,0,2,1:T(4,128)S(1)}, f32[4,2,1,4096]{3,0,2,1:T(4,128)S(1)}, u32[]{:S(2)}, u32[]{:S(2)}) collective-permute-start(f32[4,2,1,4096]{3,0,2,1:T(4,128)S(1)} %get-tuple-element.25), channel_id=1, source_target_pairs={{0,1},{1,2},{2,3},{3,4},{4,5},{5,6},{6,7},{8,9},{9,10},{10,11},{11... | collective-permute-start | bytes 393224 | tf_op jit(solution)/shard_map/ppermute | solution.py:18
  542.7 13.6 %collective-permute-start.12 = (f32[4,2,1,4096]{3,0,2,1:T(4,128)S(1)}, f32[4,2,1,4096]{3,0,2,1:T(4,128)S(1)}, u32[]{:S(2)}, u32[]{:S(2)}) collective-permute-start(f32[4,2,1,4096]{3,0,2,1:T(4,128)S(1)} %get-tuple-element.86), channel_id=1, source_target_pairs={{1,0},{2,1},{3,2},{4,3},{5,4},{6,5},{7,6},{9,8},{10,9},{11,10},{12... | collective-permute-start | bytes 393224 | tf_op jit(solution)/shard_map/ppermute | solution.py:19
  546.4 9.9 %collective-permute-start.13 = (f32[4,2,1,4096]{3,0,2,1:T(4,128)S(1)}, f32[4,2,1,4096]{3,0,2,1:T(4,128)S(1)}, u32[]{:S(2)}, u32[]{:S(2)}) collective-permute-start(f32[4,2,1,4096]{3,0,2,1:T(4,128)S(1)} %get-tuple-element.85), channel_id=1, source_target_pairs={{0,1},{1,2},{2,3},{3,4},{4,5},{5,6},{6,7},{8,9},{9,10},{10,11},{11... | collective-permute-start | bytes 393224 | tf_op jit(solution)/shard_map/ppermute | solution.py:18
  550.7 13.3 %collective-permute-start.44 = (f32[4,2,1,4096]{3,0,2,1:T(4,128)S(1)}, f32[4,2,1,4096]{3,0,2,1:T(4,128)S(1)}, u32[]{:S(2)}, u32[]{:S(2)}) collective-permute-start(f32[4,2,1,4096]{3,0,2,1:T(4,128)S(1)} %get-tuple-element.22), channel_id=1, source_target_pairs={{1,0},{2,1},{3,2},{4,3},{5,4},{6,5},{7,6},{9,8},{10,9},{11,10},{12... | collective-permute-start | bytes 393224 | tf_op jit(solution)/shard_map/ppermute | solution.py:19
  554.4 9.7 %collective-permute-start.45 = (f32[4,2,1,4096]{3,0,2,1:T(4,128)S(1)}, f32[4,2,1,4096]{3,0,2,1:T(4,128)S(1)}, u32[]{:S(2)}, u32[]{:S(2)}) collective-permute-start(f32[4,2,1,4096]{3,0,2,1:T(4,128)S(1)} %get-tuple-element.21), channel_id=1, source_target_pairs={{0,1},{1,2},{2,3},{3,4},{4,5},{5,6},{6,7},{8,9},{9,10},{10,11},{11... | collective-permute-start | bytes 393224 | tf_op jit(solution)/shard_map/ppermute | solution.py:18
  558.5 13.3 %collective-permute-start.14 = (f32[4,2,1,4096]{3,0,2,1:T(4,128)S(1)}, f32[4,2,1,4096]{3,0,2,1:T(4,128)S(1)}, u32[]{:S(2)}, u32[]{:S(2)}) collective-permute-start(f32[4,2,1,4096]{3,0,2,1:T(4,128)S(1)} %get-tuple-element.82), channel_id=1, source_target_pairs={{1,0},{2,1},{3,2},{4,3},{5,4},{6,5},{7,6},{9,8},{10,9},{11,10},{12... | collective-permute-start | bytes 393224 | tf_op jit(solution)/shard_map/ppermute | solution.py:19
  562.1 9.7 %collective-permute-start.15 = (f32[4,2,1,4096]{3,0,2,1:T(4,128)S(1)}, f32[4,2,1,4096]{3,0,2,1:T(4,128)S(1)}, u32[]{:S(2)}, u32[]{:S(2)}) collective-permute-start(f32[4,2,1,4096]{3,0,2,1:T(4,128)S(1)} %get-tuple-element.81), channel_id=1, source_target_pairs={{0,1},{1,2},{2,3},{3,4},{4,5},{5,6},{6,7},{8,9},{9,10},{10,11},{11... | collective-permute-start | bytes 393224 | tf_op jit(solution)/shard_map/ppermute | solution.py:18
  566.2 15.5 %collective-permute-start.46 = (f32[4,2,1,4096]{3,0,2,1:T(4,128)S(1)}, f32[4,2,1,4096]{3,0,2,1:T(4,128)S(1)}, u32[]{:S(2)}, u32[]{:S(2)}) collective-permute-start(f32[4,2,1,4096]{3,0,2,1:T(4,128)S(1)} %get-tuple-element.18), channel_id=1, source_target_pairs={{1,0},{2,1},{3,2},{4,3},{5,4},{6,5},{7,6},{9,8},{10,9},{11,10},{12... | collective-permute-start | bytes 393224 | tf_op jit(solution)/shard_map/ppermute | solution.py:19
  569.9 11.8 %collective-permute-start.47 = (f32[4,2,1,4096]{3,0,2,1:T(4,128)S(1)}, f32[4,2,1,4096]{3,0,2,1:T(4,128)S(1)}, u32[]{:S(2)}, u32[]{:S(2)}) collective-permute-start(f32[4,2,1,4096]{3,0,2,1:T(4,128)S(1)} %get-tuple-element.17), channel_id=1, source_target_pairs={{0,1},{1,2},{2,3},{3,4},{4,5},{5,6},{6,7},{8,9},{9,10},{10,11},{11... | collective-permute-start | bytes 393224 | tf_op jit(solution)/shard_map/ppermute | solution.py:18
  575.1 14.2 %collective-permute-start.16 = (f32[4,2,1,4096]{3,0,2,1:T(4,128)S(1)}, f32[4,2,1,4096]{3,0,2,1:T(4,128)S(1)}, u32[]{:S(2)}, u32[]{:S(2)}) collective-permute-start(f32[4,2,1,4096]{3,0,2,1:T(4,128)S(1)} %get-tuple-element.78), channel_id=1, source_target_pairs={{1,0},{2,1},{3,2},{4,3},{5,4},{6,5},{7,6},{9,8},{10,9},{11,10},{12... | collective-permute-start | bytes 393224 | tf_op jit(solution)/shard_map/ppermute | solution.py:19
  578.8 10.5 %collective-permute-start.17 = (f32[4,2,1,4096]{3,0,2,1:T(4,128)S(1)}, f32[4,2,1,4096]{3,0,2,1:T(4,128)S(1)}, u32[]{:S(2)}, u32[]{:S(2)}) collective-permute-start(f32[4,2,1,4096]{3,0,2,1:T(4,128)S(1)} %get-tuple-element.77), channel_id=1, source_target_pairs={{0,1},{1,2},{2,3},{3,4},{4,5},{5,6},{6,7},{8,9},{9,10},{10,11},{11... | collective-permute-start | bytes 393224 | tf_op jit(solution)/shard_map/ppermute | solution.py:18
  592.6 8.5 %collective-permute-start.18 = (f32[4,2,1,4096]{3,0,2,1:T(4,128)}, f32[4,2,1,4096]{3,0,2,1:T(4,128)S(1)}, u32[]{:S(2)}, u32[]{:S(2)}) collective-permute-start(f32[4,2,1,4096]{3,0,2,1:T(4,128)} %get-tuple-element.74), channel_id=1, source_target_pairs={{1,0},{2,1},{3,2},{4,3},{5,4},{6,5},{7,6},{9,8},{10,9},{11,10},{12... | collective-permute-start | bytes 393224 | tf_op jit(solution)/shard_map/ppermute | solution.py:19
  596.2 6.3 collective-permute-start.19
  607.0 7.0 collective-permute-start.21
  618.1 9.0 %collective-permute-start.23 = (f32[4,2,1,4096]{3,0,2,1:T(4,128)S(1)}, f32[4,2,1,4096]{3,0,2,1:T(4,128)S(1)}, u32[]{:S(2)}, u32[]{:S(2)}) collective-permute-start(f32[4,2,1,4096]{3,0,2,1:T(4,128)S(1)} %get-tuple-element.65), channel_id=1, source_target_pairs={{0,1},{1,2},{2,3},{3,4},{4,5},{5,6},{6,7},{8,9},{9,10},{10,11},{11... | collective-permute-start | bytes 393224 | tf_op jit(solution)/shard_map/ppermute | solution.py:18
  (16 other events, 62.0 us)
Sparse Core Ops, SparseCore 0:
  16.9 418.6 all-reduce.26
  601.2 236.1 reduce-scatter.1
where the time goes:
time: 854 us; the launch traced here: 845 us
  waiting for transfers between devices  612 us (72%)
  starting transfers between devices  126 us (15%)
  other arithmetic  78.6 us (9%)
  between operations  18.1 us (2%)
  local copies, waits for them, and re-layouts  9.5 us (1%)
    psum x1, waiting for transfers between devices, broadcast(): return lax.psum(block, axis)  387 us
    reduce_scatter x1, waiting for transfers between devices, body(): lax.psum_scatter(buffer, 'illum', scatter_dimension=0, tiled=True)  206 us
    ppermute x24, starting transfers between devices, extended(): after = lax.ppermute(initial, axis, down)  76 us
    ppermute x24, starting transfers between devices, extended(): before = lax.ppermute(last, axis, up)  50.3 us
    ppermute x24, waiting for transfers between devices, extended(): before = lax.ppermute(last, axis, up)  18.5 us
    concatenate x24, other arithmetic, extended(): array = jnp.concatenate([before, array, after], axis=dim)  18.3 us
    sub x24, other arithmetic, laplace_padded(): framed[:, :, 2:, 1:-1] + framed[:, :, :-2, 1:-1]  17.8 us
  transfers between devices with their start and end apart: 50, of which 10 were waited for; matrix products, arithmetic and copies ran while one was open for 10% of the time, Pallas kernels for 0%

commit v1 on v0

v1 whole, which is shorter than its diff:
```python
import functools
import math

import jax
import jax.numpy as jnp
from jax import lax
from jax.experimental import pallas as pl
from jax.experimental.pallas import tpu as pltpu
from jax.sharding import PartitionSpec as P

rate_scale = 0.3
ROWS = 8
COLS = 4096
TILES = COLS // 128
LAYERS = 3
HALO = 8
EXT = ROWS + 2 * HALO

SIN_C = (0.9999999996397458, -0.16666666036106006, 0.00833331543673961,
         -0.00019839409893936808, 2.7469726872825416e-06, -2.3138942785856126e-08)
COS_C = (0.9999999953627682, -0.49999991881071015, 0.04166643614419552,
         -0.001388649171259302, 2.4688583708756773e-05, -2.5084304017242627e-07)


def horner(coefs, z):
    r = z * coefs[-1] + coefs[-2]
    for c in coefs[-3::-1]:
        r = r * z + c
    return r


def sincos(x):
    y = x * 0.5
    z = y * y
    s = y * horner(SIN_C, z)
    c = horner(COS_C, z)
    s2 = s + s
    return s2 * c, 1.0 - s2 * s


def cs(t):
    return slice(t * 128, (t + 1) * 128)


class Masks:
    def __init__(self):
        lane = lax.broadcasted_iota(jnp.int32, (8, 128), 1)
        sub = lax.broadcasted_iota(jnp.int32, (8, 128), 0)
        self.first = lane == 0
        self.last = lane == 127
        self.even = (sub & 1) == 0

    def turn(self, x):
        return jnp.where(self.even, -pltpu.roll(x, 7, 0), pltpu.roll(x, 1, 0))


def lap_tiles(m, src, r):
    c = [src[r, :, cs(t)] for t in range(TILES)]
    rl = [pltpu.roll(v, 1, 1) for v in c]
    rr = [pltpu.roll(v, 127, 1) for v in c]
    zero = jnp.zeros((8, 128), jnp.float32)
    out = []
    for t in range(TILES):
        left = jnp.where(m.first, rl[t - 1] if t else zero, rl[t])
        right = jnp.where(m.last, rr[t + 1] if t < TILES - 1 else zero, rr[t])
        out.append((src[r - 1, :, cs(t)] + src[r + 1, :, cs(t)]) + (left + right) - 4.0 * c[t])
    return out


def clear_edges(row, ref, base):
    @pl.when(row == 0)
    def _():
        ref[base - 1] = jnp.zeros((8, COLS), jnp.float32)

    @pl.when(row == 7)
    def _():
        ref[base + ROWS] = jnp.zeros((8, COLS), jnp.float32)


def step(m, row, src, base, h, powers, factor, write, edge_write=None):
    prev = src
    for k, dst in enumerate(powers):
        lo, hi = base - h + 1 + k, base + ROWS + h - 1 - k

        def body(r, _, prev=prev, dst=dst):
            for t, v in enumerate(lap_tiles(m, prev, r)):
                dst[r, :, cs(t)] = v
            return 0

        lax.fori_loop(lo, hi, body, 0)
        clear_edges(row, dst, base)
        prev = dst
    l1, l2, l3 = powers
    c1, c2, c3, c4 = factor, -factor**2 / 2, -factor**3 / 6, factor**4 / 24

    def last(r, _, put):
        for t, v4 in enumerate(lap_tiles(m, l3, r)):
            even = src[r, :, cs(t)] + (c2 * l2[r, :, cs(t)] + c4 * v4)
            odd = c1 * l1[r, :, cs(t)] + c3 * l3[r, :, cs(t)]
            put(r, t, even + m.turn(odd))
        return 0

    lo, hi = base - h + 4, base + ROWS + h - 4
    if edge_write is None:
        lax.fori_loop(lo, hi, functools.partial(last, put=write), 0)
    else:
        lax.fori_loop(base, base + ROWS, functools.partial(last, put=write), 0)
        lax.fori_loop(lo, base, functools.partial(last, put=edge_write), 0)
        lax.fori_loop(base + ROWS, hi, functools.partial(last, put=edge_write), 0)


def planes(r, t):
    return pl.ds(t * ROWS + r, 8, stride=TILES * ROWS)


def split_kernel(cot, low, high):
    for r in range(4):
        for t in range(TILES):
            low[r, :, cs(t)] = cot[planes(r, t), :]
            high[r, :, cs(t)] = cot[planes(r + 4, t), :]


def adjoint_kernel(row_ref, cot, top, bot, out, u, l1, l2, l3):
    m = Masks()
    row = row_ref[0]
    for r in range(4):
        u[r] = top[r]
        u[12 + r] = bot[r]
    for r in range(ROWS):
        for t in range(TILES):
            u[4 + r, :, cs(t)] = cot[planes(r, t), :]

    def write(r, t, v):
        out[r - 4, :, cs(t)] = v

    step(m, row, u, 4, 4, (l1, l2, l3), -rate_scale, write)


def exit_kernel(row_ref, own, top, bot, out, u, l1, l2, l3):
    m = Masks()
    row = row_ref[0]
    for r in range(4):
        u[r] = top[r]
        u[12 + r] = bot[r]
    for r in range(ROWS):
        u[4 + r] = own[r]

    def write(r, t, v):
        out[planes(r - 4, t), :] = v

    step(m, row, u, 4, 4, (l1, l2, l3), rate_scale, write)


def main_kernel(row_ref, p8, q8, phases, w_own, w_top, w_bot, terms, last_refr,
                cosr, sinr, beam, beam_turn, u, v, w, w2, l1, l2, l3):
    m = Masks()
    row = row_ref[0]

    def trig(t, _):
        for j in range(LAYERS * EXT // 8):
            s, c = sincos(phases[t, j * 8:(j + 1) * 8, :])
            sinr[t, j * 8:(j + 1) * 8, :] = s
            cosr[t, j * 8:(j + 1) * 8, :] = c
        k = (q8[...] * (t * 128 + lax.broadcasted_iota(jnp.int32, (8, 128), 1))) & (COLS - 1)
        s, c = sincos((k - COLS // 2).astype(jnp.float32) * (2.0 * math.pi / COLS))
        at = pl.ds(pl.multiple_of(t * 128, 128), 128)
        beam[:, at] = jnp.where(m.even, -c, -s)
        beam_turn[:, at] = jnp.where(m.even, s, -c)
        return 0

    lax.fori_loop(0, TILES, trig, 0)

    def phase_at(layer, r, t):
        at = pl.ds(layer * EXT + r, 1)
        c = jnp.broadcast_to(cosr[t, at, :], (8, 128))
        s = jnp.broadcast_to(sinr[t, at, :], (8, 128))
        return c, s

    total = 8 * ROWS

    def incident(r, _):
        k = (p8[...] * (row * ROWS + r - HALO)) & (total - 1)
        sa, ca = sincos((k - total // 2).astype(jnp.float32) * (2.0 * math.pi / total))
        for t in range(TILES):
            c, s = phase_at(0, r, t)
            u[r, :, cs(t)] = (beam_turn[:, cs(t)] * -(sa * c + ca * s)
                              - beam[:, cs(t)] * (ca * c - sa * s))
        return 0

    lax.fori_loop(0, EXT, incident, 0)
    clear_edges(row, u, HALO)

    def write_v(r, t, x):
        c, s = phase_at(1, r, t)
        v[r, :, cs(t)] = x * c + m.turn(x) * s

    step(m, row, u, HALO, 8, (l1, l2, l3), rate_scale, write_v)
    clear_edges(row, v, HALO)

    def write_last(r, t, x):
        c, s = phase_at(2, r, t)
        last_refr[r - HALO, :, cs(t)] = x * c + m.turn(x) * s

    step(m, row, v, HALO, 4, (l1, l2, l3), rate_scale, write_last)

    def term(layer, r, t, adjoint, stored):
        terms[t, pl.ds(layer * ROWS + r, 1), :] = jnp.sum(
            adjoint * m.turn(stored), axis=0, keepdims=True)

    def term_two(r, _):
        for t in range(TILES):
            term(2, r, t, w_own[r, :, cs(t)], last_refr[r, :, cs(t)])
        return 0

    lax.fori_loop(0, ROWS, term_two, 0)

    def back(src, first):
        def body(r, _):
            for t in range(TILES):
                c, s = phase_at(2, r + first, t)
                x = src[r, :, cs(t)]
                w[r + first, :, cs(t)] = x * c - m.turn(x) * s
            return 0

        lax.fori_loop(0, ROWS, body, 0)

    back(w_top, 0)
    back(w_own, HALO)
    back(w_bot, HALO + ROWS)

    def mid_edge(r, t, x):
        c, s = phase_at(1, r, t)
        w2[r, :, cs(t)] = x * c - m.turn(x) * s

    def mid(r, t, x):
        mid_edge(r, t, x)
        term(1, r - HALO, t, x, v[r, :, cs(t)])

    step(m, row, w, HALO, 8, (l1, l2, l3), -rate_scale, mid, mid_edge)
    clear_edges(row, w2, HALO)

    def final(r, t, x):
        term(0, r - HALO, t, x, u[r, :, cs(t)])

    step(m, row, w2, HALO, 4, (l1, l2, l3), -rate_scale, final)


def vm():
    return pl.BlockSpec(memory_space=pltpu.VMEM)


def sm():
    return pl.BlockSpec(memory_space=pltpu.SMEM)


def field(rows):
    return jax.ShapeDtypeStruct((rows, 8, COLS), jnp.float32)


def scratch(rows, n):
    return [pltpu.VMEM((rows, 8, COLS), jnp.float32)] * n


def call(kernel, ins, outs, scr, name, mib):
    return pl.pallas_call(
        kernel, out_shape=outs, in_specs=ins, out_specs=jax.tree.map(lambda _: vm(), outs),
        scratch_shapes=scr, name=name,
        compiler_params=pltpu.CompilerParams(vmem_limit_bytes=mib << 20),
        cost_estimate=pl.CostEstimate(flops=20_000_000, bytes_accessed=4 << 20, transcendentals=0),
    )


def body(angles, depth_order, slices, cotangent):
    peers = lax.axis_size("illum")
    n_row = lax.axis_size("row")
    row = lax.axis_index("row").astype(jnp.int32).reshape(1)
    me = lax.axis_index("illum")
    up = [(i, i + 1) for i in range(n_row - 1)]
    down = [(i + 1, i) for i in range(n_row - 1)]

    cot = cotangent.reshape(8, ROWS, TILES, 128).transpose(0, 2, 1, 3).reshape(-1, 128)
    low, high = call(split_kernel, [vm()], (field(4), field(4)), [], "split", 6)(cot)
    cot_top = lax.ppermute(high, "row", up)
    cot_bot = lax.ppermute(low, "row", down)

    mine = slices[0].reshape(ROWS, TILES, 128).transpose(1, 0, 2)
    got = lax.all_to_all(mine, "illum", 0, 0, tiled=True)
    chunk = jnp.concatenate(
        [lax.dynamic_slice_in_dim(got, depth_order[l], 1, 0) for l in range(LAYERS)], 0)

    w1 = call(adjoint_kernel, [sm(), vm(), vm(), vm()], field(8), scratch(16, 4), "adjoint1", 14)(
        row, cot, cot_top, cot_bot)
    w_top = lax.ppermute(w1, "row", up)
    w_bot = lax.ppermute(w1, "row", down)

    c_top = lax.ppermute(chunk, "row", up)
    c_bot = lax.ppermute(chunk, "row", down)
    wide = jnp.concatenate([c_top, chunk, c_bot], axis=1).reshape(LAYERS * EXT, 128)
    phases = lax.all_to_all(
        jnp.broadcast_to(wide[None], (peers, LAYERS * EXT, 128)), "illum", 0, 0, tiled=True)

    p8 = jnp.broadcast_to(jnp.repeat(angles[:, 0], 2)[:, None], (8, 128))
    q8 = jnp.broadcast_to(jnp.repeat(angles[:, 1], 2)[:, None], (8, 128))
    table = pltpu.VMEM((TILES, LAYERS * EXT, 128), jnp.float32)
    line = pltpu.VMEM((8, COLS), jnp.float32)
    terms, refr = call(
        main_kernel, [sm()] + [vm()] * 6,
        (jax.ShapeDtypeStruct((TILES, LAYERS * ROWS, 128), jnp.float32), field(8)),
        [table, table, line, line] + scratch(EXT, 7), "main", 36)(
            row, p8, q8, phases, w1, w_top, w_bot)
    r_top = lax.ppermute(refr[4:], "row", up)
    r_bot = lax.ppermute(refr[:4], "row", down)

    parts = lax.all_to_all(terms, "illum", 0, 0, tiled=True)
    summed = jnp.sum(parts, axis=0).reshape(LAYERS, ROWS, 128)
    owners = jnp.arange(peers, dtype=jnp.int32)
    send = sum(
        jnp.where((owners == depth_order[l])[:, None, None], summed[l][None], 0.0)
        for l in range(LAYERS))
    out = call(exit_kernel, [sm(), vm(), vm(), vm()],
               jax.ShapeDtypeStruct(cot.shape, jnp.float32),
               scratch(16, 4), "exit", 14)(row, refr, r_top, r_bot)
    grad = lax.all_to_all(send, "illum", 0, 0, tiled=True)
    grad = grad.transpose(1, 0, 2).reshape(1, ROWS, COLS)
    out = out.reshape(8, TILES, ROWS, 128).transpose(0, 2, 1, 3)
    return out.reshape(cotangent.shape), grad


def solution(mesh):
    placed = (P("illum", None), P(), P("illum", "row", None), P("illum", None, "row", None))
    return jax.shard_map(
        body,
        mesh=mesh,
        in_specs=placed,
        out_specs=(P("illum", None, "row", None), P("illum", "row", None)),
        check_vma=False,
    )
```

time: 854 us -> 192 us (0.22)
  waiting for transfers between devices: 612 us -> 57.2 us
  other arithmetic: 78.6 us -> 2.78 us
  starting transfers between devices: 126 us -> 53.9 us
  Pallas kernels: 0 us -> 58.2 us
  between operations: 18.1 us -> 6.53 us
    psum x1 -> x0, waiting for transfers between devices: 387 us -> none  [broadcast(): return lax.psum(block, axis)]
    reduce_scatter x1 -> x0, waiting for transfers between devices: 206 us -> none  [body(): lax.psum_scatter(buffer, 'illum', scatter_dimension=0, tiled=True)]
    ppermute x48 -> x8, starting transfers between devices: 126 us -> 18.5 us  [the longest x1 3.64 us: body(): cot_bot = lax.ppermute(low, 'row', down)]
    pallas_call x0 -> x4, Pallas kernels: none -> 58.2 us  [the longest x1 41.9 us: body(): call(main_kernel, [sm()] + [vm()] * 6, (jax.ShapeDtypeStruct((TILES, LAYE...]
    all_to_all x0 -> x4, starting transfers between devices: none -> 35.4 us  [the longest x1 13.1 us: body(): got = lax.all_to_all(mine, 'illum', 0, 0, tiled=True)]
    add x31 -> x1, other arithmetic: 24.6 us -> 0.83 us  [body(): sum((jnp.where((owners == depth_order[l])[:, None, None], summed[l][None]...]
    all_to_all x0 -> x4, waiting for transfers between devices: none -> 19.7 us  [the longest x1 9.6 us: body(): parts = lax.all_to_all(terms, 'illum', 0, 0, tiled=True)]
    concatenate x24 -> x2, other arithmetic: 18.3 us -> 0.01 us  [the longest x1 0.01 us: body(): jnp.concatenate([lax.dynamic_slice_in_dim(got, depth_order[l], 1, 0) for...]
  transfers between devices with their start and end apart: 50 -> 12, of which waited for: 10 -> 7; matrix products, arithmetic and copies ran while one was open for 10% -> 3% of each run, Pallas kernels for 0% -> 9%
where the time goes in v1:
time: 192 us; the launch traced here: 190 us
  Pallas kernels  58.2 us (30%)
  waiting for transfers between devices  57.2 us (30%)
  starting transfers between devices  53.9 us (28%)
  local copies, waits for them, and re-layouts  11.1 us (6%)
  between operations  6.53 us (3%)
  other arithmetic  2.78 us (1%)
    pallas_call x1, Pallas kernels, body(): call(main_kernel, [sm()] + [vm()] * 6, (jax.ShapeDtypeStruct((TILES, LAYE...  41.9 us
    ppermute x1, waiting for transfers between devices, body(): cot_top = lax.ppermute(high, 'row', up)  24.2 us
    all_to_all x1, starting transfers between devices, body(): got = lax.all_to_all(mine, 'illum', 0, 0, tiled=True)  13.1 us
    all_to_all x1, starting transfers between devices, body(): parts = lax.all_to_all(terms, 'illum', 0, 0, tiled=True)  11.6 us
    all_to_all x1, waiting for transfers between devices, body(): parts = lax.all_to_all(terms, 'illum', 0, 0, tiled=True)  9.6 us
    pallas_call x1, Pallas kernels, body(): call(exit_kernel, [sm(), vm(), vm(), vm()], jax.ShapeDtypeStruct(cot.shap...  7.81 us
    ppermute x1, waiting for transfers between devices, body(): w_bot = lax.ppermute(w1, 'row', down)  7.63 us
    unnamed x19, local copies, waits for them, and re-layouts  7.29 us
  transfers between devices with their start and end apart: 12, of which 7 were waited for; matrix products, arithmetic and copies ran while one was open for 3% of the time, Pallas kernels for 9%

profile of v1, /device:TPU:32, one launch (start us, length us, event | category | flops | bytes accessed | tf_op | source)
XLA Modules:
  0.0 189.7 jit_solution(4807532073880979557)
XLA Ops:
  0.6 13.1 %all-to-all-start = ((f32[32,8,128]{2,1,0:T(8,128)}), f32[32,8,128]{2,1,0:T(8,128)S(1)}, u32[]{:S(2)}, u32[]{:S(2)}) async-start(f32[32,8,128]{2,1,0:T(8,128)} %bitcast.30), calls=%async_computation | async-start | bytes 262144 | tf_op jit(solution)/shard_map/all_to_all | solution.py:287
  13.7 1.4 fusion.2
  20.8 5.5 %all-to-all-done = f32[32,8,128]{2,1,0:T(8,128)S(1)} async-done(((f32[32,8,128]{2,1,0:T(8,128)}), f32[32,8,128]{2,1,0:T(8,128)S(1)}, u32[]{:S(2)}, u32[]{:S(2)}) %all-to-all-start) | async-done | bytes 131104 | tf_op jit(solution)/shard_map/all_to_all | solution.py:287
  26.3 1.9 %collective-permute-start.1 = (f32[3,8,128]{2,1,0:T(8,128)S(1)}, f32[3,8,128]{2,1,0:T(8,128)S(1)}, u32[]{:S(2)}, u32[]{:S(2)}) collective-permute-start(f32[3,8,128]{2,1,0:T(8,128)S(1)} %pad_maximum_fusion.1), channel_id=1, source_target_pairs={{1,0},{2,1},{3,2},{4,3},{5,4},{6,5},{7,6},{9,8},{10,9},{11,10},{12... | collective-permute-start | bytes 36872 | tf_op jit(solution)/shard_map/ppermute | solution.py:297
  28.3 2.4 %collective-permute-start = (f32[3,8,128]{2,1,0:T(8,128)S(1)}, f32[3,8,128]{2,1,0:T(8,128)S(1)}, u32[]{:S(2)}, u32[]{:S(2)}) collective-permute-start(f32[3,8,128]{2,1,0:T(8,128)S(1)} %pad_maximum_fusion.1), channel_id=1, source_target_pairs={{0,1},{1,2},{2,3},{3,4},{4,5},{5,6},{6,7},{8,9},{9,10},{10,11},{11... | collective-permute-start | bytes 36872 | tf_op jit(solution)/shard_map/ppermute | solution.py:296
  30.7 0.0 collective-permute-done.1
  30.7 2.6 %collective-permute-done = f32[3,8,128]{2,1,0:T(8,128)S(1)} collective-permute-done((f32[3,8,128]{2,1,0:T(8,128)S(1)}, f32[3,8,128]{2,1,0:T(8,128)S(1)}, u32[]{:S(2)}, u32[]{:S(2)}) %collective-permute-start) | collective-permute-done | bytes 12320 | tf_op jit(solution)/shard_map/ppermute | solution.py:296
  33.3 1.1 broadcast_in_dim.79
  34.4 6.9 %all-to-all-start.1 = ((f32[32,72,128]{2,1,0:T(8,128)}), f32[32,72,128]{2,1,0:T(8,128)S(1)}, u32[]{:S(2)}, u32[]{:S(2)}) async-start(f32[32,72,128]{2,1,0:T(8,128)} %broadcast_in_dim.79), calls=%async_computation.1 | async-start | bytes 2359296 | tf_op jit(solution)/shard_map/all_to_all | solution.py:299
  41.3 1.6 split.1
  42.9 1.9 %collective-permute-start.2 = (f32[4,8,4096]{2,1,0:T(8,128)}, f32[4,8,4096]{2,1,0:T(8,128)S(1)}, u32[]{:S(2)}, u32[]{:S(2)}) collective-permute-start(f32[4,8,4096]{2,1,0:T(8,128)} %get-tuple-element.6), channel_id=1, source_target_pairs={{0,1},{1,2},{2,3},{3,4},{4,5},{5,6},{6,7},{8,9},{9,10},{10,11},{11... | collective-permute-start | bytes 1572872 | tf_op jit(solution)/shard_map/ppermute | solution.py:283
  44.8 3.6 %collective-permute-start.3 = (f32[4,8,4096]{2,1,0:T(8,128)}, f32[4,8,4096]{2,1,0:T(8,128)S(1)}, u32[]{:S(2)}, u32[]{:S(2)}) collective-permute-start(f32[4,8,4096]{2,1,0:T(8,128)} %get-tuple-element.7), channel_id=1, source_target_pairs={{1,0},{2,1},{3,2},{4,3},{5,4},{6,5},{7,6},{9,8},{10,9},{11,10},{12... | collective-permute-start | bytes 1572872 | tf_op jit(solution)/shard_map/ppermute | solution.py:284
  48.4 24.2 %collective-permute-done.2.top = f32[4,8,4096]{2,1,0:T(8,128)S(1)} collective-permute-done((f32[4,8,4096]{2,1,0:T(8,128)}, f32[4,8,4096]{2,1,0:T(8,128)S(1)}, u32[]{:S(2)}, u32[]{:S(2)}) %collective-permute-start.2) | collective-permute-done | bytes 524320 | tf_op jit(solution)/shard_map/ppermute | solution.py:283
  72.7 0.8 copy-done.3
  73.5 0.0 collective-permute-done.3.bot
  73.5 0.8 copy-done.5
  74.3 1.0 copy-done.4
  75.3 1.0 copy-done.6
  76.4 6.9 %adjoint1.1.w_own = f32[8,8,4096]{2,1,0:T(8,128)S(1)} custom-call(s32[1]{0:T(128)} %bitcast.row_ref, f32[2048,128]{1,0:T(8,128)S(1)} %bitcast.26, f32[4,8,4096]{2,1,0:T(8,128)S(1)} %copy-done.4, f32[4,8,4096]{2,1,0:T(8,128)S(1)} %copy-done.6), custom_call_target="tpu_custom_call" | custom-call | flops 20000000 | bytes 4194304 | tf_op jit(solution)/shard_map/adjoint1/pallas_call | solution.py:291
  83.2 1.9 %collective-permute-start.5 = (f32[8,8,4096]{2,1,0:T(8,128)S(1)}, f32[8,8,4096]{2,1,0:T(8,128)S(1)}, u32[]{:S(2)}, u32[]{:S(2)}) collective-permute-start(f32[8,8,4096]{2,1,0:T(8,128)S(1)} %adjoint1.1.w_own), channel_id=1, source_target_pairs={{1,0},{2,1},{3,2},{4,3},{5,4},{6,5},{7,6},{9,8},{10,9},{11,10},{12... | collective-permute-start | bytes 3145736 | tf_op jit(solution)/shard_map/ppermute | solution.py:294
  85.2 2.4 %collective-permute-start.4 = (f32[8,8,4096]{2,1,0:T(8,128)S(1)}, f32[8,8,4096]{2,1,0:T(8,128)}, u32[]{:S(2)}, u32[]{:S(2)}) collective-permute-start(f32[8,8,4096]{2,1,0:T(8,128)S(1)} %adjoint1.1.w_own), channel_id=1, source_target_pairs={{0,1},{1,2},{2,3},{3,4},{4,5},{5,6},{6,7},{8,9},{9,10},{10,11},{11... | collective-permute-start | bytes 3145736 | tf_op jit(solution)/shard_map/ppermute | solution.py:293
  87.6 0.1 broadcast_in_dim.75
  87.7 0.1 broadcast_in_dim.76
  87.8 0.1 broadcast_in_dim.72
  87.8 0.1 broadcast_in_dim.73
  87.9 0.7 iota_compare_fusion.2
  88.6 1.3 iota_compare_fusion
  89.8 7.6 %collective-permute-done.5.w_bot = f32[8,8,4096]{2,1,0:T(8,128)S(1)} collective-permute-done((f32[8,8,4096]{2,1,0:T(8,128)S(1)}, f32[8,8,4096]{2,1,0:T(8,128)S(1)}, u32[]{:S(2)}, u32[]{:S(2)}) %collective-permute-start.5) | collective-permute-done | bytes 1048608 | tf_op jit(solution)/shard_map/ppermute | solution.py:294
  97.5 1.0 copy-done.1
  98.4 3.0 %collective-permute-done.4.w_top = f32[8,8,4096]{2,1,0:T(8,128)} collective-permute-done((f32[8,8,4096]{2,1,0:T(8,128)S(1)}, f32[8,8,4096]{2,1,0:T(8,128)}, u32[]{:S(2)}, u32[]{:S(2)}) %collective-permute-start.4) | collective-permute-done | bytes 1048608 | tf_op jit(solution)/shard_map/ppermute | solution.py:293
  101.4 0.0 all-to-all-done.1.phases
  101.4 0.1 broadcast_in_dim.74.p8
  101.5 0.1 broadcast_in_dim.77.q8
  101.5 1.2 copy-done.2
  102.8 41.9 %main.1 = (f32[32,24,128]{2,1,0:T(8,128)S(1)}, f32[8,8,4096]{2,1,0:T(8,128)S(1)}) custom-call(s32[1]{0:T(128)} %bitcast.row_ref, s32[8,128]{1,0:T(8,128)S(1)} %broadcast_in_dim.74.p8, s32[8,128]{1,0:T(8,128)S(1)} %broadcast_in_dim.77.q8, f32[32,72,128]{2,1,0:T(8,128)S(1)} %all-to-all-done.1.phases, f32[8,8,4096]{2,1,0:T(8,128)S(1)} %adjoint1.1.w_own, ...), custom_call_target="tpu_custom_call" | custom-call | flops 20000000 | bytes 4194304 | tf_op jit(solution)/shard_map/main/pallas_call | solution.py:306
  144.7 0.8 copy-done.7
  145.4 11.6 %all-to-all-start.2 = ((f32[32,24,128]{2,1,0:T(8,128)}), f32[32,24,128]{2,1,0:T(8,128)S(1)}, u32[]{:S(2)}, u32[]{:S(2)}) async-start(f32[32,24,128]{2,1,0:T(8,128)} %copy-done.7), calls=%async_computation.2 | async-start | bytes 786432 | tf_op jit(solution)/shard_map/all_to_all | solution.py:314
  157.0 0.9 fusion
  157.9 1.9 %collective-permute-start.7 = (f32[4,8,4096]{2,1,0:T(8,128)}, f32[4,8,4096]{2,1,0:T(8,128)S(1)}, u32[]{:S(2)}, u32[]{:S(2)}) collective-permute-start(f32[4,8,4096]{2,1,0:T(8,128)} %get-tuple-element.10), channel_id=1, source_target_pairs={{1,0},{2,1},{3,2},{4,3},{5,4},{6,5},{7,6},{9,8},{10,9},{11,10},{12... | collective-permute-start | bytes 1572872 | tf_op jit(solution)/shard_map/ppermute | solution.py:312
  159.8 2.4 %collective-permute-start.6 = (f32[4,8,4096]{2,1,0:T(8,128)S(1)}, f32[4,8,4096]{2,1,0:T(8,128)S(1)}, u32[]{:S(2)}, u32[]{:S(2)}) collective-permute-start(f32[4,8,4096]{2,1,0:T(8,128)S(1)} %get-tuple-element.11), channel_id=1, source_target_pairs={{0,1},{1,2},{2,3},{3,4},{4,5},{5,6},{6,7},{8,9},{9,10},{10,11},{11... | collective-permute-start | bytes 1572872 | tf_op jit(solution)/shard_map/ppermute | solution.py:311
  162.2 9.6 %all-to-all-done.2 = f32[32,24,128]{2,1,0:T(8,128)S(1)} async-done(((f32[32,24,128]{2,1,0:T(8,128)}), f32[32,24,128]{2,1,0:T(8,128)S(1)}, u32[]{:S(2)}, u32[]{:S(2)}) %all-to-all-start.2) | async-done | bytes 393248 | tf_op jit(solution)/shard_map/all_to_all | solution.py:314
  171.9 0.8 select_add_fusion
  172.7 3.9 %all-to-all-start.3 = ((f32[32,8,128]{2,1,0:T(8,128)}), f32[32,8,128]{2,1,0:T(8,128)S(1)}, u32[]{:S(2)}, u32[]{:S(2)}) async-start(f32[32,8,128]{2,1,0:T(8,128)} %select_add_fusion), calls=%async_computation.3 | async-start | bytes 262144 | tf_op jit(solution)/shard_map/all_to_all | solution.py:323
  176.6 0.0 collective-permute-done.7.bot
  176.6 0.0 collective-permute-done.6.top
  176.6 7.8 %exit.1 = f32[2048,128]{1,0:T(8,128)} custom-call(s32[1]{0:T(128)} %bitcast.row_ref, f32[8,8,4096]{2,1,0:T(8,128)S(1)} %get-tuple-element.8.own, f32[4,8,4096]{2,1,0:T(8,128)S(1)} %collective-permute-done.6.top, f32[4,8,4096]{2,1,0:T(8,128)S(1)} %collective-permute-done.7.bot), custom_call_target="tpu_custom_call" | custom-call | flops 20000000 | bytes 4194304 | tf_op jit(solution)/shard_map/exit/pallas_call | solution.py:320
  184.5 4.6 %all-to-all-done.3 = f32[32,8,128]{2,1,0:T(8,128)S(1)} async-done(((f32[32,8,128]{2,1,0:T(8,128)}), f32[32,8,128]{2,1,0:T(8,128)S(1)}, u32[]{:S(2)}, u32[]{:S(2)}) %all-to-all-start.3) | async-done | bytes 131104 | tf_op jit(solution)/shard_map/all_to_all | solution.py:323
  189.1 0.7 copy.7
  (17 shorter events, 0.1 us)
Async XLA Ops:
  0.6 25.7 %all-to-all-start = ((f32[32,8,128]{2,1,0:T(8,128)}), f32[32,8,128]{2,1,0:T(8,128)S(1)}, u32[]{:S(2)}, u32[]{:S(2)}) async-start(f32[32,8,128]{2,1,0:T(8,128)} %bitcast.30), calls=%async_computation | async-start | bytes 262144 | tf_op jit(solution)/shard_map/all_to_all | solution.py:287
  26.3 4.3 %collective-permute-start.1 = (f32[3,8,128]{2,1,0:T(8,128)S(1)}, f32[3,8,128]{2,1,0:T(8,128)S(1)}, u32[]{:S(2)}, u32[]{:S(2)}) collective-permute-start(f32[3,8,128]{2,1,0:T(8,128)S(1)} %pad_maximum_fusion.1), channel_id=1, source_target_pairs={{1,0},{2,1},{3,2},{4,3},{5,4},{6,5},{7,6},{9,8},{10,9},{11,10},{12... | collective-permute-start | bytes 36872 | tf_op jit(solution)/shard_map/ppermute | solution.py:297
  28.3 5.0 %collective-permute-start = (f32[3,8,128]{2,1,0:T(8,128)S(1)}, f32[3,8,128]{2,1,0:T(8,128)S(1)}, u32[]{:S(2)}, u32[]{:S(2)}) collective-permute-start(f32[3,8,128]{2,1,0:T(8,128)S(1)} %pad_maximum_fusion.1), channel_id=1, source_target_pairs={{0,1},{1,2},{2,3},{3,4},{4,5},{5,6},{6,7},{8,9},{9,10},{10,11},{11... | collective-permute-start | bytes 36872 | tf_op jit(solution)/shard_map/ppermute | solution.py:296
  34.4 6.9 %copy-start = (f32[4,2,8,4096]{3,2,1,0:T(8,128)S(1)}, f32[4,2,8,4096]{3,2,1,0:T(8,128)}, u32[]{:S(2)}) copy-start(f32[4,2,8,4096]{3,2,1,0:T(8,128)} %param.7) | copy-start | bytes 3145732
  34.4 67.0 %all-to-all-start.1 = ((f32[32,72,128]{2,1,0:T(8,128)}), f32[32,72,128]{2,1,0:T(8,128)S(1)}, u32[]{:S(2)}, u32[]{:S(2)}) async-start(f32[32,72,128]{2,1,0:T(8,128)} %broadcast_in_dim.79), calls=%async_computation.1 | async-start | bytes 2359296 | tf_op jit(solution)/shard_map/all_to_all | solution.py:299
  42.9 29.8 %collective-permute-start.2 = (f32[4,8,4096]{2,1,0:T(8,128)}, f32[4,8,4096]{2,1,0:T(8,128)S(1)}, u32[]{:S(2)}, u32[]{:S(2)}) collective-permute-start(f32[4,8,4096]{2,1,0:T(8,128)} %get-tuple-element.6), channel_id=1, source_target_pairs={{0,1},{1,2},{2,3},{3,4},{4,5},{5,6},{6,7},{8,9},{9,10},{10,11},{11... | collective-permute-start | bytes 1572872 | tf_op jit(solution)/shard_map/ppermute | solution.py:283
  44.8 28.7 %collective-permute-start.3 = (f32[4,8,4096]{2,1,0:T(8,128)}, f32[4,8,4096]{2,1,0:T(8,128)S(1)}, u32[]{:S(2)}, u32[]{:S(2)}) collective-permute-start(f32[4,8,4096]{2,1,0:T(8,128)} %get-tuple-element.7), channel_id=1, source_target_pairs={{1,0},{2,1},{3,2},{4,3},{5,4},{6,5},{7,6},{9,8},{10,9},{11,10},{12... | collective-permute-start | bytes 1572872 | tf_op jit(solution)/shard_map/ppermute | solution.py:284
  72.7 0.8 copy-start.3
  73.5 0.8 copy-start.5
  74.3 1.0 copy-start.4
  75.3 1.0 copy-start.6
  76.4 11.2 %copy-start.8 = (s32[4,2]{0,1:T(2,128)S(1)}, s32[4,2]{0,1:T(2,128)}, u32[]{:S(2)}) copy-start(s32[4,2]{0,1:T(2,128)} %param.4) | copy-start | bytes 100
  83.2 14.2 %collective-permute-start.5 = (f32[8,8,4096]{2,1,0:T(8,128)S(1)}, f32[8,8,4096]{2,1,0:T(8,128)S(1)}, u32[]{:S(2)}, u32[]{:S(2)}) collective-permute-start(f32[8,8,4096]{2,1,0:T(8,128)S(1)} %adjoint1.1.w_own), channel_id=1, source_target_pairs={{1,0},{2,1},{3,2},{4,3},{5,4},{6,5},{7,6},{9,8},{10,9},{11,10},{12... | collective-permute-start | bytes 3145736 | tf_op jit(solution)/shard_map/ppermute | solution.py:294
  85.2 16.2 %collective-permute-start.4 = (f32[8,8,4096]{2,1,0:T(8,128)S(1)}, f32[8,8,4096]{2,1,0:T(8,128)}, u32[]{:S(2)}, u32[]{:S(2)}) collective-permute-start(f32[8,8,4096]{2,1,0:T(8,128)S(1)} %adjoint1.1.w_own), channel_id=1, source_target_pairs={{0,1},{1,2},{2,3},{3,4},{4,5},{5,6},{6,7},{8,9},{9,10},{10,11},{11... | collective-permute-start | bytes 3145736 | tf_op jit(solution)/shard_map/ppermute | solution.py:293
  97.5 1.0 copy-start.1
  101.5 1.2 copy-start.2
  144.7 0.8 copy-start.7
  145.4 26.4 %all-to-all-start.2 = ((f32[32,24,128]{2,1,0:T(8,128)}), f32[32,24,128]{2,1,0:T(8,128)S(1)}, u32[]{:S(2)}, u32[]{:S(2)}) async-start(f32[32,24,128]{2,1,0:T(8,128)} %copy-done.7), calls=%async_computation.2 | async-start | bytes 786432 | tf_op jit(solution)/shard_map/all_to_all | solution.py:314
  157.9 18.7 %collective-permute-start.7 = (f32[4,8,4096]{2,1,0:T(8,128)}, f32[4,8,4096]{2,1,0:T(8,128)S(1)}, u32[]{:S(2)}, u32[]{:S(2)}) collective-permute-start(f32[4,8,4096]{2,1,0:T(8,128)} %get-tuple-element.10), channel_id=1, source_target_pairs={{1,0},{2,1},{3,2},{4,3},{5,4},{6,5},{7,6},{9,8},{10,9},{11,10},{12... | collective-permute-start | bytes 1572872 | tf_op jit(solution)/shard_map/ppermute | solution.py:312
  159.8 16.8 %collective-permute-start.6 = (f32[4,8,4096]{2,1,0:T(8,128)S(1)}, f32[4,8,4096]{2,1,0:T(8,128)S(1)}, u32[]{:S(2)}, u32[]{:S(2)}) collective-permute-start(f32[4,8,4096]{2,1,0:T(8,128)S(1)} %get-tuple-element.11), channel_id=1, source_target_pairs={{0,1},{1,2},{2,3},{3,4},{4,5},{5,6},{6,7},{8,9},{9,10},{10,11},{11... | collective-permute-start | bytes 1572872 | tf_op jit(solution)/shard_map/ppermute | solution.py:311
  172.7 16.4 %all-to-all-start.3 = ((f32[32,8,128]{2,1,0:T(8,128)}), f32[32,8,128]{2,1,0:T(8,128)S(1)}, u32[]{:S(2)}, u32[]{:S(2)}) async-start(f32[32,8,128]{2,1,0:T(8,128)} %select_add_fusion), calls=%async_computation.3 | async-start | bytes 262144 | tf_op jit(solution)/shard_map/all_to_all | solution.py:323

commit v2 on v0

v2 whole, which is shorter than its diff:
```python
import functools
import math

import jax
import jax.numpy as jnp
from jax import lax
from jax.experimental import pallas as pl
from jax.experimental.pallas import tpu as pltpu
from jax.sharding import PartitionSpec as P

rate_scale = 0.3
ROWS = 8
COLS = 4096
TILES = COLS // 128
LAYERS = 3
HALO = 8
EXT = ROWS + 2 * HALO
N_ROW = 8
NX = ROWS * N_ROW
PAD = 144
PLANE = 16

SIN_C = (0.9999999996397458, -0.16666666036106006, 0.00833331543673961,
         -0.00019839409893936808, 2.7469726872825416e-06, -2.3138942785856126e-08)
COS_C = (0.9999999953627682, -0.49999991881071015, 0.04166643614419552,
         -0.001388649171259302, 2.4688583708756773e-05, -2.5084304017242627e-07)


def horner(coefs, z):
    r = z * coefs[-1] + coefs[-2]
    for c in coefs[-3::-1]:
        r = r * z + c
    return r


def sincos(x):
    y = x * 0.5
    z = y * y
    s = y * horner(SIN_C, z)
    c = horner(COS_C, z)
    s2 = s + s
    return s2 * c, 1.0 - s2 * s


def chunk(j):
    return slice(8 * j, 8 * j + 8)


def padded(j, shift=0):
    return slice(8 + 8 * j + shift, 16 + 8 * j + shift)


def fill_pads(ref, rows):
    flat = ref.reshape(rows * 2 * PAD, 128)
    tile = lax.broadcasted_iota(jnp.int32, (rows * 2, 128), 1) & (TILES - 1)
    high = flat[pl.ds(135, rows * 2, stride=PAD), :]
    low = flat[pl.ds(8, rows * 2, stride=PAD), :]
    flat[pl.ds(7, rows * 2, stride=PAD), :] = jnp.where(tile == 0, 0.0, pltpu.roll(high, 1, 1))
    flat[pl.ds(136, rows * 2, stride=PAD), :] = jnp.where(
        tile == TILES - 1, 0.0, pltpu.roll(low, 127, 1))


def clear_outside(row, ref, base, rows):
    for at in (base - 1 - ROWS * row, base + NX - ROWS * row):
        @pl.when((at >= 0) & (at < rows))
        def _(at=at):
            ref[at] = jnp.zeros((2, PAD, 128), jnp.float32)


def lap_pair(src, r, k, j):
    v = [src[r + q, k, padded(j), :] for q in (-1, 0, 1, 2)]
    out = []
    for q in (0, 1):
        side = src[r + q, k, padded(j, -1), :] + src[r + q, k, padded(j, 1), :]
        out.append((v[q] + v[q + 2]) + side - 4.0 * v[q + 1])
    return out


def step(row, src, rows, base, h, powers, factor, write):
    prev = src
    for n, dst in enumerate(powers):
        lo, count = base - h + 1 + n, ROWS + 2 * (h - 1 - n)

        def body(i, _, prev=prev, dst=dst, lo=lo):
            r = lo + 2 * i
            for k in range(2):
                for j in range(16):
                    a, b = lap_pair(prev, r, k, j)
                    dst[r, k, padded(j), :] = a
                    dst[r + 1, k, padded(j), :] = b
            return 0

        lax.fori_loop(0, count // 2, body, 0)
        fill_pads(dst, rows)
        clear_outside(row, dst, base, rows)
        prev = dst
    l1, l2, l3 = powers
    c1, c2, c3, c4 = factor, -factor**2 / 2, -factor**3 / 6, factor**4 / 24
    lo = base - h + 4

    def last(i, _):
        r = lo + 2 * i
        for j in range(16):
            l4 = [lap_pair(l3, r, k, j) for k in range(2)]
            for q in (0, 1):
                even, odd = [], []
                for k in range(2):
                    at = (r + q, k, padded(j), slice(None))
                    even.append(src[at] + (c2 * l2[at] + c4 * l4[k][q]))
                    odd.append(c1 * l1[at] + c3 * l3[at])
                write(r + q, j, even[0] - odd[1], even[1] + odd[0])
        return 0

    lax.fori_loop(0, (ROWS + 2 * (h - 4)) // 2, last, 0)


def natural(g, k, r):
    return pl.ds((g * 2 + k) * TILES * ROWS + r, TILES, stride=ROWS)


def split_kernel(cot, out, low, high):
    def body(r, _):
        for k in range(2):
            out[r, k] = jnp.concatenate([cot[natural(g, k, r), :] for g in range(4)], axis=0).T
        return 0

    lax.fori_loop(0, ROWS, body, 0)
    for r in range(4):
        low[r] = out[r]
        high[r] = out[r + 4]


def put(dst, at, src, n):
    def body(r, _):
        for k in range(2):
            dst[at + r, k, 8:136, :] = src[r, k]
        return 0

    lax.fori_loop(0, n, body, 0)


def adjoint_kernel(row_ref, own, top, bot, top2, bot2, out, u, l1, l2, l3):
    row = row_ref[0]
    put(u, 0, top2, 4)
    put(u, 4, top, 8)
    put(u, 12, own, 8)
    put(u, 20, bot, 8)
    put(u, 28, bot2, 4)
    fill_pads(u, 32)

    def write(r, j, re, im):
        out[r - 4, 0, chunk(j), :] = re
        out[r - 4, 1, chunk(j), :] = im

    step(row, u, 32, 12, 12, (l1, l2, l3), -rate_scale, write)


def exit_kernel(row_ref, low, high, top, bot, out, u, l1, l2, l3, res):
    row = row_ref[0]
    put(u, 0, top, 4)
    put(u, 4, low, 4)
    put(u, 8, high, 4)
    put(u, 12, bot, 4)
    fill_pads(u, 16)

    def write(r, j, re, im):
        res[r - 4, 0, chunk(j), :] = re
        res[r - 4, 1, chunk(j), :] = im

    step(row, u, 16, 4, 4, (l1, l2, l3), rate_scale, write)

    def body(r, _):
        for k in range(2):
            x = res[r, k].T
            for g in range(4):
                out[natural(g, k, r), :] = x[g * TILES:(g + 1) * TILES]
        return 0

    lax.fori_loop(0, ROWS, body, 0)


def trig_tables(phases, cos_n, sin_n):
    def body(i, _):
        at = pl.ds(pl.multiple_of(i * 24, 8), 24)
        s, c = sincos(phases[at, :])
        sin_n[at, :] = s
        cos_n[at, :] = c
        return 0

    lax.fori_loop(0, TILES, body, 0)


def spread(ref, n):
    x = ref[pl.ds(n, TILES, stride=LAYERS * ROWS), :]
    return jnp.concatenate([x] * 4, axis=0).T


def phase_kernel(phases, cos_out, sin_out, cos_n, sin_n):
    trig_tables(phases, cos_n, sin_n)

    def body(n, _):
        cos_out[n] = spread(cos_n, n)
        sin_out[n] = spread(sin_n, n)
        return 0

    lax.fori_loop(0, LAYERS * ROWS, body, 0)


def main_kernel(row_ref, pv, qv, ph_top, ph_bot, cos_own, sin_own, w1,
                terms, last_low, last_high,
                cos_n, sin_n, cosr, sinr, beam, u, v, w, w2, raw, l1, l2, l3):
    row = row_ref[0]
    for ph, first in ((ph_top, 0), (ph_bot, HALO + ROWS)):
        trig_tables(ph, cos_n, sin_n)
        for layer in range(LAYERS):
            lo, hi = (0, 8) if layer != 1 else ((4, 8) if first == 0 else (0, 4))

            def body(r, _, layer=layer, first=first):
                cosr[layer * EXT + first + r] = spread(cos_n, layer * ROWS + r)
                sinr[layer * EXT + first + r] = spread(sin_n, layer * ROWS + r)
                return 0

            lax.fori_loop(lo, hi, body, 0)
    for layer in range(LAYERS):
        def copy(r, _, layer=layer):
            cosr[layer * EXT + HALO + r] = cos_own[layer * ROWS + r]
            sinr[layer * EXT + HALO + r] = sin_own[layer * ROWS + r]
            return 0

        lax.fori_loop(0, ROWS, copy, 0)

    lane = lax.broadcasted_iota(jnp.int32, (8, 128), 1)
    sub = lax.broadcasted_iota(jnp.int32, (8, 128), 0)
    for j in range(16):
        col = (lane & (TILES - 1)) * 128 + sub + 8 * j
        k = (qv[...] * col) & (COLS - 1)
        s, c = sincos((k - COLS // 2).astype(jnp.float32) * (2.0 * math.pi / COLS))
        beam[0, chunk(j), :] = -c
        beam[1, chunk(j), :] = -s

    def phase_at(layer, r, j):
        return cosr[layer * EXT + r, chunk(j), :], sinr[layer * EXT + r, chunk(j), :]

    def incident(r, _):
        k = (pv[...] * (row * ROWS + r - HALO)) & (NX - 1)
        sa, ca = sincos((k - NX // 2).astype(jnp.float32) * (2.0 * math.pi / NX))
        for j in range(16):
            c, s = phase_at(0, r, j)
            a = sa * s - ca * c
            b = -(sa * c + ca * s)
            er, ei = beam[0, chunk(j), :], beam[1, chunk(j), :]
            u[r, 0, padded(j), :] = er * a - ei * b
            u[r, 1, padded(j), :] = ei * a + er * b
        return 0

    lax.fori_loop(0, EXT, incident, 0)
    fill_pads(u, EXT)
    clear_outside(row, u, HALO, EXT)

    def write_v(r, j, re, im):
        c, s = phase_at(1, r, j)
        v[r, 0, padded(j), :] = re * c - im * s
        v[r, 1, padded(j), :] = re * s + im * c

    step(row, u, EXT, HALO, 8, (l1, l2, l3), rate_scale, write_v)
    fill_pads(v, EXT)
    clear_outside(row, v, HALO, EXT)

    def write_last(r, j, re, im):
        c, s = phase_at(2, r, j)
        w2[r, 0, padded(j), :] = re * c - im * s
        w2[r, 1, padded(j), :] = re * s + im * c

    step(row, v, EXT, HALO, 4, (l1, l2, l3), rate_scale, write_last)
    for r in range(4):
        for k in range(2):
            last_low[r, k] = w2[HALO + r, k, 8:136, :]
            last_high[r, k] = w2[HALO + 4 + r, k, 8:136, :]

    def term(layer, adjoint, stored):
        def body(r, _):
            x = adjoint(r, 1) * stored(r, 0) - adjoint(r, 0) * stored(r, 1)
            x = x.T
            x = (x[:TILES] + x[TILES:2 * TILES]) + (x[2 * TILES:3 * TILES] + x[3 * TILES:])
            terms[pl.ds(layer * ROWS + r, TILES, stride=LAYERS * ROWS), :] = x
            return 0

        lax.fori_loop(0, ROWS, body, 0)

    def own(ref):
        return lambda r, k: ref[HALO + r, k, 8:136, :]

    term(2, lambda r, k: w1[HALO + r, k], own(w2))

    def back(r, _):
        for j in range(16):
            c, s = phase_at(2, r, j)
            re, im = w1[r, 0, chunk(j), :], w1[r, 1, chunk(j), :]
            w[r, 0, padded(j), :] = re * c + im * s
            w[r, 1, padded(j), :] = im * c - re * s
        return 0

    lax.fori_loop(0, EXT, back, 0)
    fill_pads(w, EXT)
    clear_outside(row, w, HALO, EXT)

    def mid(r, j, re, im):
        c, s = phase_at(1, r, j)
        raw[r - 4, 0, chunk(j), :] = re
        raw[r - 4, 1, chunk(j), :] = im
        w2[r, 0, padded(j), :] = re * c + im * s
        w2[r, 1, padded(j), :] = im * c - re * s

    step(row, w, EXT, HALO, 8, (l1, l2, l3), -rate_scale, mid)
    fill_pads(w2, EXT)
    clear_outside(row, w2, HALO, EXT)
    term(1, lambda r, k: raw[r + 4, k], own(v))

    def final(r, j, re, im):
        raw[r - 4, 0, chunk(j), :] = re
        raw[r - 4, 1, chunk(j), :] = im

    step(row, w2, EXT, HALO, 4, (l1, l2, l3), -rate_scale, final)
    term(0, lambda r, k: raw[r + 4, k], own(u))


def vm():
    return pl.BlockSpec(memory_space=pltpu.VMEM)


def sm():
    return pl.BlockSpec(memory_space=pltpu.SMEM)


def shape(*dims):
    return jax.ShapeDtypeStruct(dims, jnp.float32)


def field(rows):
    return shape(rows, 2, 128, 128)


def scr(*dims):
    return pltpu.VMEM(dims, jnp.float32)


def wide(rows):
    return scr(rows, 2, PAD, 128)


def call(kernel, ins, outs, scratch, name, mib):
    return pl.pallas_call(
        kernel, out_shape=outs, in_specs=ins, out_specs=jax.tree.map(lambda _: vm(), outs),
        scratch_shapes=scratch, name=name,
        compiler_params=pltpu.CompilerParams(vmem_limit_bytes=mib << 20),
        cost_estimate=pl.CostEstimate(flops=20_000_000, bytes_accessed=4 << 20, transcendentals=0),
    )


def body(angles, depth_order, slices, cotangent):
    row = lax.axis_index("row").astype(jnp.int32).reshape(1)
    z = lax.axis_index("illum") // PLANE
    here = lax.axis_index("illum") % PLANE
    n_row = lax.axis_size("row")
    groups = [list(range(g * PLANE, (g + 1) * PLANE)) for g in range(2)]
    swap = [(i, (i + PLANE) % (2 * PLANE)) for i in range(2 * PLANE)]

    def to_next(x, by):
        return lax.ppermute(x, "row", [(i, i + by) for i in range(n_row - by)])

    def to_prev(x, by):
        return lax.ppermute(x, "row", [(i + by, i) for i in range(n_row - by)])

    def exchange(x):
        return lax.all_to_all(x, "illum", 0, 0, axis_index_groups=groups, tiled=True)

    mine = slices[0]
    other = lax.ppermute(mine, "illum", swap)

    cot = cotangent.reshape(8, ROWS, TILES, 128).transpose(0, 2, 1, 3).reshape(-1, 128)
    own, low, high = call(split_kernel, [vm()], (field(8), field(4), field(4)), [], "split", 8)(cot)
    top, bot = to_next(own, 1), to_prev(own, 1)
    top2, bot2 = to_next(high, 2), to_prev(low, 2)

    both = jnp.stack([jnp.where(z == 0, mine, other), jnp.where(z == 0, other, mine)], 0)
    both = both.reshape(2 * ROWS, TILES, 128).transpose(1, 0, 2)
    got = exchange(both.reshape(TILES * 2 * ROWS, 128)).reshape(PLANE, 2, 2, ROWS, 128)
    picked = [
        lax.dynamic_slice(got, (depth_order[l] % PLANE, 0, depth_order[l] // PLANE, 0, 0),
                          (1, 2, 1, ROWS, 128))[0]
        for l in range(LAYERS)
    ]
    piece = jnp.concatenate(picked, 1).reshape(1, 2 * LAYERS * ROWS, 128)
    phases = exchange(
        jnp.broadcast_to(piece, (PLANE, 2 * LAYERS * ROWS, 128)).reshape(-1, 128))
    ph_top, ph_bot = to_next(phases, 1), to_prev(phases, 1)

    w1 = call(adjoint_kernel, [sm()] + [vm()] * 5, field(EXT), [wide(32)] * 4, "adjoint1", 26)(
        row, own, top, bot, top2, bot2)
    table = scr(TILES * LAYERS * ROWS, 128)
    cos_own, sin_own = call(
        phase_kernel, [vm()], (shape(LAYERS * ROWS, 128, 128),) * 2, [table] * 2, "phases", 8)(
            phases)

    pv = jnp.broadcast_to(jnp.repeat(angles[:, 0], TILES)[None], (8, 128))
    qv = jnp.broadcast_to(jnp.repeat(angles[:, 1], TILES)[None], (8, 128))
    spreads = scr(LAYERS * EXT, 128, 128)
    terms, last_low, last_high = call(
        main_kernel, [sm()] + [vm()] * 7,
        (shape(TILES * LAYERS * ROWS, 128), field(4), field(4)),
        [table, table, spreads, spreads, scr(2, 128, 128)] + [wide(EXT)] * 4
        + [scr(16, 2, 128, 128)] + [wide(EXT)] * 3, "main", 52)(
            row, pv, qv, ph_top, ph_bot, cos_own, sin_own, w1)
    r_top, r_bot = to_next(last_high, 1), to_prev(last_low, 1)

    parts = exchange(terms).reshape(PLANE, 2, LAYERS, ROWS, 128)
    half = jnp.sum(parts, axis=0)
    full = half + lax.ppermute(half, "illum", swap)
    owners = jnp.arange(PLANE, dtype=jnp.int32) + z * PLANE
    send = sum(
        jnp.where((owners == depth_order[l])[:, None, None, None], full[None, :, l], 0.0)
        for l in range(LAYERS))
    out = call(exit_kernel, [sm()] + [vm()] * 4, shape(2048, 128),
               [wide(16)] * 4 + [scr(8, 2, 128, 128)], "exit", 16)(
                   row, last_low, last_high, r_top, r_bot)
    grad = exchange(send.reshape(TILES * ROWS, 128)).reshape(TILES, ROWS, 128)
    grad = grad.transpose(1, 0, 2).reshape(1, ROWS, COLS)
    out = out.reshape(8, TILES, ROWS, 128).transpose(0, 2, 1, 3)
    return out.reshape(cotangent.shape), grad


def solution(mesh):
    placed = (P("illum", None), P(), P("illum", "row", None), P("illum", None, "row", None))
    return jax.shard_map(
        body,
        mesh=mesh,
        in_specs=placed,
        out_specs=(P("illum", None, "row", None), P("illum", "row", None)),
        check_vma=False,
    )
```

time: 854 us -> 143 us (0.17)
  waiting for transfers between devices: 612 us -> 22.3 us
  starting transfers between devices: 126 us -> 49 us
  other arithmetic: 78.6 us -> 3.03 us
  Pallas kernels: 0 us -> 38.5 us
  blocking collectives: 0 us -> 11.4 us
  between operations: 18.1 us -> 8.68 us
    psum x1 -> x0, waiting for transfers between devices: 387 us -> none  [broadcast(): return lax.psum(block, axis)]
    reduce_scatter x1 -> x0, waiting for transfers between devices: 206 us -> none  [body(): lax.psum_scatter(buffer, 'illum', scatter_dimension=0, tiled=True)]
    ppermute x48 -> x10, starting transfers between devices: 126 us -> 30.5 us  [the longest x4 10.4 us: to_next(): return lax.ppermute(x, 'row', [(i, i + by) for i in range(n_row - by)])]
    pallas_call x0 -> x5, Pallas kernels: none -> 38.5 us  [the longest x1 23.9 us: body(): call(main_kernel, [sm()] + [vm()] * 7, (shape(TILES * LAYERS * ROWS, 128)...]
    add x31 -> x2, other arithmetic: 24.6 us -> 0.13 us  [the longest x1 0.12 us: body(): sum((jnp.where((owners == depth_order[l])[:, None, None, None], full[None...]
    all_to_all x0 -> x3, starting transfers between devices: none -> 18.5 us  [exchange(): lax.all_to_all(x, 'illum', 0, 0, axis_index_groups=groups, tiled=True)]
    concatenate x24 -> x1, other arithmetic: 18.3 us -> 0.01 us  [body(): piece = jnp.concatenate(picked, 1).reshape(1, 2 * LAYERS * ROWS, 128)]
    sub x24 -> x0, other arithmetic: 17.8 us -> none  [laplace_padded(): framed[:, :, 2:, 1:-1] + framed[:, :, :-2, 1:-1]]
  transfers between devices with their start and end apart: 50 -> 13, of which waited for: 10 -> 3; matrix products, arithmetic and copies ran while one was open for 10% -> 3% of each run, Pallas kernels for 0% -> 8%
where the time goes in v2:
time: 143 us; the launch traced here: 140 us
  starting transfers between devices  49 us (34%)
  Pallas kernels  38.5 us (27%)
  waiting for transfers between devices  22.3 us (16%)
  blocking collectives  11.4 us (8%)
  between operations  8.68 us (6%)
  local copies, waits for them, and re-layouts  7.37 us (5%)
  other arithmetic  3.03 us (2%)
    pallas_call x1, Pallas kernels, body(): call(main_kernel, [sm()] + [vm()] * 7, (shape(TILES * LAYERS * ROWS, 128)...  23.9 us
    all_to_all x3, starting transfers between devices, exchange(): lax.all_to_all(x, 'illum', 0, 0, axis_index_groups=groups, tiled=True)  18.5 us
    all_to_all x3, waiting for transfers between devices, exchange(): lax.all_to_all(x, 'illum', 0, 0, axis_index_groups=groups, tiled=True)  15.7 us
    all_to_all x1, blocking collectives, exchange(): lax.all_to_all(x, 'illum', 0, 0, axis_index_groups=groups, tiled=True)  11.4 us
    ppermute x4, starting transfers between devices, to_next(): return lax.ppermute(x, 'row', [(i, i + by) for i in range(n_row - by)])  10.4 us
    ppermute x4, starting transfers between devices, to_prev(): return lax.ppermute(x, 'row', [(i + by, i) for i in range(n_row - by)])  8.39 us
    ppermute x1, waiting for transfers between devices, body(): other = lax.ppermute(mine, 'illum', swap)  6.56 us
    ppermute x1, starting transfers between devices, body(): other = lax.ppermute(mine, 'illum', swap)  6.38 us
  transfers between devices with their start and end apart: 13, of which 3 were waited for; matrix products, arithmetic and copies ran while one was open for 3% of the time, Pallas kernels for 8%

profile of v2, /device:TPU:32, one launch (start us, length us, event | category | flops | bytes accessed | tf_op | source)
XLA Modules:
  0.0 140.2 jit_solution(14975464483189274160)
XLA Ops:
  0.6 6.4 %collective-permute-start = (f32[8,4096]{1,0:T(8,128)}, f32[8,4096]{1,0:T(8,128)S(1)}, u32[]{:S(2)}, u32[]{:S(2)}) collective-permute-start(f32[8,4096]{1,0:T(8,128)} %bitcast.62), channel_id=1, source_target_pairs={{0,128},{8,136},{16,144},{24,152},{32,160},{40,168},{48,176},{56,1... | collective-permute-start | bytes 393224 | tf_op jit(solution)/shard_map/ppermute | solution.py:378
  7.0 6.6 %collective-permute-done = f32[8,4096]{1,0:T(8,128)S(1)} collective-permute-done((f32[8,4096]{1,0:T(8,128)}, f32[8,4096]{1,0:T(8,128)S(1)}, u32[]{:S(2)}, u32[]{:S(2)}) %collective-permute-start) | collective-permute-done | bytes 131104 | tf_op jit(solution)/shard_map/ppermute | solution.py:378
  13.6 0.9 select_bitcast_fusion.1
  14.5 0.0 copy-start.5
  14.5 0.1 copy.7
  14.6 0.9 copy.6
  15.5 7.2 %all-to-all-start = ((f32[16,32,128]{2,1,0:T(8,128)}), f32[16,32,128]{2,1,0:T(8,128)S(1)}, u32[]{:S(2)}, u32[]{:S(2)}) async-start(f32[16,32,128]{2,1,0:T(8,128)} %bitcast.7), calls=%async_computation | async-start | bytes 524288 | tf_op jit(solution)/shard_map/all_to_all | solution.py:375
  22.7 1.9 %split.1 = (f32[8,2,128,128]{3,2,1,0:T(8,128)S(1)}, f32[4,2,128,128]{3,2,1,0:T(8,128)}, f32[4,2,128,128]{3,2,1,0:T(8,128)}) custom-call(f32[2048,128]{1,0:T(8,128)S(1)} %bitcast.57), custom_call_target="tpu_custom_call" | custom-call | flops 20000000 | bytes 4194304 | tf_op jit(solution)/shard_map/split/pallas_call | solution.py:381
  24.5 1.9 %collective-permute-start.4 = (f32[8,2,128,128]{3,2,1,0:T(8,128)S(1)}, f32[8,2,128,128]{3,2,1,0:T(8,128)S(1)}, u32[]{:S(2)}, u32[]{:S(2)}) collective-permute-start(f32[8,2,128,128]{3,2,1,0:T(8,128)S(1)} %get-tuple-element.12.own), channel_id=1, source_target_pairs={{1,0},{2,1},{3,2},{4,3},{5,4},{6,5},{7,6},{9,8},{10,9},{11,10},{12... | collective-permute-start | bytes 3145736 | tf_op jit(solution)/shard_map/ppermute | solution.py:372
  26.5 2.4 %collective-permute-start.3 = (f32[8,2,128,128]{3,2,1,0:T(8,128)S(1)}, f32[8,2,128,128]{3,2,1,0:T(8,128)}, u32[]{:S(2)}, u32[]{:S(2)}) collective-permute-start(f32[8,2,128,128]{3,2,1,0:T(8,128)S(1)} %get-tuple-element.12.own), channel_id=1, source_target_pairs={{0,1},{1,2},{2,3},{3,4},{4,5},{5,6},{6,7},{8,9},{9,10},{10,11},{11... | collective-permute-start | bytes 3145736 | tf_op jit(solution)/shard_map/ppermute | solution.py:369
  28.9 3.3 %collective-permute-start.5 = (f32[4,2,128,128]{3,2,1,0:T(8,128)}, f32[4,2,128,128]{3,2,1,0:T(8,128)S(1)}, u32[]{:S(2)}, u32[]{:S(2)}) collective-permute-start(f32[4,2,128,128]{3,2,1,0:T(8,128)} %get-tuple-element.13), channel_id=1, source_target_pairs={{0,2},{1,3},{2,4},{3,5},{4,6},{5,7},{8,10},{9,11},{10,12},{11,13},... | collective-permute-start | bytes 1572872 | tf_op jit(solution)/shard_map/ppermute | solution.py:369
  32.2 0.7 fusion.3
  40.6 0.0 all-to-all-done
  40.6 0.8 broadcast_in_dim.85
  41.4 7.2 %all-to-all-start.1 = ((f32[16,48,128]{2,1,0:T(8,128)}), f32[16,48,128]{2,1,0:T(8,128)S(1)}, u32[]{:S(2)}, u32[]{:S(2)}) async-start(f32[16,48,128]{2,1,0:T(8,128)} %broadcast_in_dim.85), calls=%async_computation.1 | async-start | bytes 786432 | tf_op jit(solution)/shard_map/all_to_all | solution.py:375
  48.6 2.6 %collective-permute-start.6 = (f32[4,2,128,128]{3,2,1,0:T(8,128)}, f32[4,2,128,128]{3,2,1,0:T(8,128)}, u32[]{:S(2)}, u32[]{:S(2)}) collective-permute-start(f32[4,2,128,128]{3,2,1,0:T(8,128)} %get-tuple-element.14), channel_id=1, source_target_pairs={{2,0},{3,1},{4,2},{5,3},{6,4},{7,5},{10,8},{11,9},{12,10},{13,11},... | collective-permute-start | bytes 1572872 | tf_op jit(solution)/shard_map/ppermute | solution.py:372
  51.2 7.1 %all-to-all-done.1 = f32[16,48,128]{2,1,0:T(8,128)S(1)} async-done(((f32[16,48,128]{2,1,0:T(8,128)}), f32[16,48,128]{2,1,0:T(8,128)S(1)}, u32[]{:S(2)}, u32[]{:S(2)}) %all-to-all-start.1) | async-done | bytes 393248 | tf_op jit(solution)/shard_map/all_to_all | solution.py:375
  58.3 2.0 %collective-permute-start.2 = (f32[768,128]{1,0:T(8,128)S(1)}, f32[768,128]{1,0:T(8,128)S(1)}, u32[]{:S(2)}, u32[]{:S(2)}) collective-permute-start(f32[768,128]{1,0:T(8,128)S(1)} %bitcast.54), channel_id=1, source_target_pairs={{1,0},{2,1},{3,2},{4,3},{5,4},{6,5},{7,6},{9,8},{10,9},{11,10},{12... | collective-permute-start | bytes 1179656 | tf_op jit(solution)/shard_map/ppermute | solution.py:372
  60.3 0.0 collective-permute-done.5.top2
  60.3 2.3 %collective-permute-start.1 = (f32[768,128]{1,0:T(8,128)S(1)}, f32[768,128]{1,0:T(8,128)}, u32[]{:S(2)}, u32[]{:S(2)}) collective-permute-start(f32[768,128]{1,0:T(8,128)S(1)} %bitcast.55), channel_id=1, source_target_pairs={{0,1},{1,2},{2,3},{3,4},{4,5},{5,6},{6,7},{8,9},{9,10},{10,11},{11... | collective-permute-start | bytes 1179656 | tf_op jit(solution)/shard_map/ppermute | solution.py:369
  62.7 0.1 broadcast_in_dim.81
  62.8 0.1 broadcast_in_dim.82
  62.9 0.1 broadcast_in_dim.78
  62.9 0.1 broadcast_in_dim.79
  63.0 3.1 %phases.1 = (f32[24,128,128]{2,1,0:T(8,128)S(1)}, f32[24,128,128]{2,1,0:T(8,128)S(1)}) custom-call(f32[768,128]{1,0:T(8,128)S(1)} %bitcast.56), custom_call_target="tpu_custom_call" | custom-call | flops 20000000 | bytes 4194304 | tf_op jit(solution)/shard_map/phases/pallas_call | solution.py:401
  66.1 1.2 copy-done.1
  67.3 1.2 copy-done.2
  68.5 0.0 collective-permute-done.6.bot2
  68.5 0.0 collective-permute-done.4.bot
  68.5 0.0 collective-permute-done.3.top
  68.5 5.8 %adjoint1.1.w1 = f32[24,2,128,128]{3,2,1,0:T(8,128)S(1)} custom-call(s32[1]{0:T(128)} %bitcast.row_ref, f32[8,2,128,128]{3,2,1,0:T(8,128)S(1)} %get-tuple-element.12.own, f32[8,2,128,128]{3,2,1,0:T(8,128)} %collective-permute-done.3.top, f32[8,2,128,128]{3,2,1,0:T(8,128)S(1)} %collective-permute-done.4.bot, ...), custom_call_target="tpu_custom_call" | custom-call | flops 20000000 | bytes 4194304 | tf_op jit(solution)/shard_map/adjoint1/pallas_call | solution.py:398
  74.3 1.6 %copy-done = f32[24,2,128,128]{3,2,1,0:T(8,128)} copy-done((f32[24,2,128,128]{3,2,1,0:T(8,128)}, f32[24,2,128,128]{3,2,1,0:T(8,128)S(1)}, u32[]{:S(2)}) %copy-start) | copy-done | bytes 3145752
  76.0 0.0 collective-permute-done.2.ph_bot
  76.0 23.9 %main.1 = (f32[768,128]{1,0:T(8,128)}, f32[4,2,128,128]{3,2,1,0:T(8,128)S(1)}, f32[4,2,128,128]{3,2,1,0:T(8,128)}) custom-call(s32[1]{0:T(128)} %bitcast.row_ref, s32[8,128]{1,0:T(8,128)S(1)} %broadcast_in_dim.80.pv, s32[8,128]{1,0:T(8,128)S(1)} %broadcast_in_dim.83.qv, f32[768,128]{1,0:T(8,128)} %collective-permute-done.1.ph_top, ...), custom_call_target="tpu_custom_call" | custom-call | flops 20000000 | bytes 4194304 | tf_op jit(solution)/shard_map/main/pallas_call | solution.py:408
  99.9 4.1 %all-to-all-start.2 = ((f32[16,48,128]{2,1,0:T(8,128)}), f32[16,48,128]{2,1,0:T(8,128)S(1)}, u32[]{:S(2)}, u32[]{:S(2)}) async-start(f32[16,48,128]{2,1,0:T(8,128)} %bitcast.23), calls=%async_computation.2 | async-start | bytes 786432 | tf_op jit(solution)/shard_map/all_to_all | solution.py:375
  104.1 1.2 fusion
  105.3 8.5 %all-to-all-done.2 = f32[16,48,128]{2,1,0:T(8,128)S(1)} async-done(((f32[16,48,128]{2,1,0:T(8,128)}), f32[16,48,128]{2,1,0:T(8,128)S(1)}, u32[]{:S(2)}, u32[]{:S(2)}) %all-to-all-start.2) | async-done | bytes 393248 | tf_op jit(solution)/shard_map/all_to_all | solution.py:375
  113.9 5.3 %collective-permute-start.9 = (f32[2,3,8,128]{3,2,1,0:T(8,128)S(1)}, f32[2,3,8,128]{3,2,1,0:T(8,128)S(1)}, u32[]{:S(2)}, u32[]{:S(2)}) collective-permute-start(f32[2,3,8,128]{3,2,1,0:T(8,128)S(1)} %bitcast.63), channel_id=1, source_target_pairs={{0,128},{8,136},{16,144},{24,152},{32,160},{40,168},{48,176},{56,1... | collective-permute-start | bytes 73736 | tf_op jit(solution)/shard_map/ppermute | solution.py:418
  119.1 0.7 fusion.2
  119.8 1.9 %collective-permute-start.8 = (f32[4,2,128,128]{3,2,1,0:T(8,128)S(1)}, f32[4,2,128,128]{3,2,1,0:T(8,128)S(1)}, u32[]{:S(2)}, u32[]{:S(2)}) collective-permute-start(f32[4,2,128,128]{3,2,1,0:T(8,128)S(1)} %get-tuple-element.15.low), channel_id=1, source_target_pairs={{1,0},{2,1},{3,2},{4,3},{5,4},{6,5},{7,6},{9,8},{10,9},{11,10},{12... | collective-permute-start | bytes 1572872 | tf_op jit(solution)/shard_map/ppermute | solution.py:372
  121.8 2.4 %collective-permute-start.7 = (f32[4,2,128,128]{3,2,1,0:T(8,128)}, f32[4,2,128,128]{3,2,1,0:T(8,128)S(1)}, u32[]{:S(2)}, u32[]{:S(2)}) collective-permute-start(f32[4,2,128,128]{3,2,1,0:T(8,128)} %get-tuple-element.16.high), channel_id=1, source_target_pairs={{0,1},{1,2},{2,3},{3,4},{4,5},{5,6},{6,7},{8,9},{9,10},{10,11},{11... | collective-permute-start | bytes 1572872 | tf_op jit(solution)/shard_map/ppermute | solution.py:369
  124.2 0.0 collective-permute-done.9
  124.2 0.1 select_add_fusion
  124.3 11.4 %all_to_all.32 = f32[16,16,128]{2,1,0:T(8,128)S(1)} all-to-all(f32[16,16,128]{2,1,0:T(8,128)S(1)} %select_add_fusion), channel_id=1, replica_groups={{0,8,16,24,32,40,48,56,64,72,80,88,96,104,112,120},{128,136,144,152,160..., dimensions={0} | all-to-all | bytes 262144 | tf_op jit(solution)/shard_map/all_to_all | solution.py:375
  135.7 0.0 collective-permute-done.8.bot
  135.7 0.0 collective-permute-done.7.top
  135.7 3.8 %exit.1 = f32[2048,128]{1,0:T(8,128)} custom-call(s32[1]{0:T(128)} %bitcast.row_ref, f32[4,2,128,128]{3,2,1,0:T(8,128)S(1)} %get-tuple-element.15.low, f32[4,2,128,128]{3,2,1,0:T(8,128)S(1)} %copy-done.4, f32[4,2,128,128]{3,2,1,0:T(8,128)S(1)} %collective-permute-done.7.top, f32[4,2,128,128]{3,2,1,0:T(8,128)S(1)} %collective-permute-done.8.bot), custom_call_target="tpu_custom_call" | custom-call | flops 20000000 | bytes 4194304 | tf_op jit(solution)/shard_map/exit/pallas_call | solution.py:423
  139.5 0.7 copy.9
  (20 shorter events, 0.1 us)
Async XLA Ops:
  0.6 22.0 %copy-start.3 = (f32[4,2,8,4096]{3,2,1,0:T(8,128)S(1)}, f32[4,2,8,4096]{3,2,1,0:T(8,128)}, u32[]{:S(2)}) copy-start(f32[4,2,8,4096]{3,2,1,0:T(8,128)} %param.7) | copy-start | bytes 3145732
  0.6 12.9 %collective-permute-start = (f32[8,4096]{1,0:T(8,128)}, f32[8,4096]{1,0:T(8,128)S(1)}, u32[]{:S(2)}, u32[]{:S(2)}) collective-permute-start(f32[8,4096]{1,0:T(8,128)} %bitcast.62), channel_id=1, source_target_pairs={{0,128},{8,136},{16,144},{24,152},{32,160},{40,168},{48,176},{56,1... | collective-permute-start | bytes 393224 | tf_op jit(solution)/shard_map/ppermute | solution.py:378
  14.5 17.7 %copy-start.5 = (s32[3]{0:T(128)S(1)}, s32[3]{0:T(128)}, u32[]{:S(2)}) copy-start(s32[3]{0:T(128)} %param.5) | copy-start | bytes 40
  15.5 47.2 %copy-start.6 = (s32[4,2]{0,1:T(2,128)S(1)}, s32[4,2]{0,1:T(2,128)}, u32[]{:S(2)}) copy-start(s32[4,2]{0,1:T(2,128)} %param.4) | copy-start | bytes 100
  15.5 25.1 %all-to-all-start = ((f32[16,32,128]{2,1,0:T(8,128)}), f32[16,32,128]{2,1,0:T(8,128)S(1)}, u32[]{:S(2)}, u32[]{:S(2)}) async-start(f32[16,32,128]{2,1,0:T(8,128)} %bitcast.7), calls=%async_computation | async-start | bytes 524288 | tf_op jit(solution)/shard_map/all_to_all | solution.py:375
  24.5 44.0 %collective-permute-start.4 = (f32[8,2,128,128]{3,2,1,0:T(8,128)S(1)}, f32[8,2,128,128]{3,2,1,0:T(8,128)S(1)}, u32[]{:S(2)}, u32[]{:S(2)}) collective-permute-start(f32[8,2,128,128]{3,2,1,0:T(8,128)S(1)} %get-tuple-element.12.own), channel_id=1, source_target_pairs={{1,0},{2,1},{3,2},{4,3},{5,4},{6,5},{7,6},{9,8},{10,9},{11,10},{12... | collective-permute-start | bytes 3145736 | tf_op jit(solution)/shard_map/ppermute | solution.py:372
  26.5 42.0 %collective-permute-start.3 = (f32[8,2,128,128]{3,2,1,0:T(8,128)S(1)}, f32[8,2,128,128]{3,2,1,0:T(8,128)}, u32[]{:S(2)}, u32[]{:S(2)}) collective-permute-start(f32[8,2,128,128]{3,2,1,0:T(8,128)S(1)} %get-tuple-element.12.own), channel_id=1, source_target_pairs={{0,1},{1,2},{2,3},{3,4},{4,5},{5,6},{6,7},{8,9},{9,10},{10,11},{11... | collective-permute-start | bytes 3145736 | tf_op jit(solution)/shard_map/ppermute | solution.py:369
  28.9 31.4 %collective-permute-start.5 = (f32[4,2,128,128]{3,2,1,0:T(8,128)}, f32[4,2,128,128]{3,2,1,0:T(8,128)S(1)}, u32[]{:S(2)}, u32[]{:S(2)}) collective-permute-start(f32[4,2,128,128]{3,2,1,0:T(8,128)} %get-tuple-element.13), channel_id=1, source_target_pairs={{0,2},{1,3},{2,4},{3,5},{4,6},{5,7},{8,10},{9,11},{10,12},{11,13},... | collective-permute-start | bytes 1572872 | tf_op jit(solution)/shard_map/ppermute | solution.py:369
  41.4 16.9 %all-to-all-start.1 = ((f32[16,48,128]{2,1,0:T(8,128)}), f32[16,48,128]{2,1,0:T(8,128)S(1)}, u32[]{:S(2)}, u32[]{:S(2)}) async-start(f32[16,48,128]{2,1,0:T(8,128)} %broadcast_in_dim.85), calls=%async_computation.1 | async-start | bytes 786432 | tf_op jit(solution)/shard_map/all_to_all | solution.py:375
  48.6 19.9 %collective-permute-start.6 = (f32[4,2,128,128]{3,2,1,0:T(8,128)}, f32[4,2,128,128]{3,2,1,0:T(8,128)}, u32[]{:S(2)}, u32[]{:S(2)}) collective-permute-start(f32[4,2,128,128]{3,2,1,0:T(8,128)} %get-tuple-element.14), channel_id=1, source_target_pairs={{2,0},{3,1},{4,2},{5,3},{6,4},{7,5},{10,8},{11,9},{12,10},{13,11},... | collective-permute-start | bytes 1572872 | tf_op jit(solution)/shard_map/ppermute | solution.py:372
  58.3 17.6 %collective-permute-start.2 = (f32[768,128]{1,0:T(8,128)S(1)}, f32[768,128]{1,0:T(8,128)S(1)}, u32[]{:S(2)}, u32[]{:S(2)}) collective-permute-start(f32[768,128]{1,0:T(8,128)S(1)} %bitcast.54), channel_id=1, source_target_pairs={{1,0},{2,1},{3,2},{4,3},{5,4},{6,5},{7,6},{9,8},{10,9},{11,10},{12... | collective-permute-start | bytes 1179656 | tf_op jit(solution)/shard_map/ppermute | solution.py:372
  60.3 15.6 %collective-permute-start.1 = (f32[768,128]{1,0:T(8,128)S(1)}, f32[768,128]{1,0:T(8,128)}, u32[]{:S(2)}, u32[]{:S(2)}) collective-permute-start(f32[768,128]{1,0:T(8,128)S(1)} %bitcast.55), channel_id=1, source_target_pairs={{0,1},{1,2},{2,3},{3,4},{4,5},{5,6},{6,7},{8,9},{9,10},{10,11},{11... | collective-permute-start | bytes 1179656 | tf_op jit(solution)/shard_map/ppermute | solution.py:369
  66.1 1.2 copy-start.1
  67.3 1.2 copy-start.2
  74.3 1.6 %copy-start = (f32[24,2,128,128]{3,2,1,0:T(8,128)}, f32[24,2,128,128]{3,2,1,0:T(8,128)S(1)}, u32[]{:S(2)}) copy-start(f32[24,2,128,128]{3,2,1,0:T(8,128)S(1)} %adjoint1.1.w1) | copy-start | bytes 9437188
  99.9 35.8 %copy-start.4 = (f32[4,2,128,128]{3,2,1,0:T(8,128)S(1)}, f32[4,2,128,128]{3,2,1,0:T(8,128)}, u32[]{:S(2)}) copy-start(f32[4,2,128,128]{3,2,1,0:T(8,128)} %get-tuple-element.16.high) | copy-start | bytes 1572868
  99.9 13.9 %all-to-all-start.2 = ((f32[16,48,128]{2,1,0:T(8,128)}), f32[16,48,128]{2,1,0:T(8,128)S(1)}, u32[]{:S(2)}, u32[]{:S(2)}) async-start(f32[16,48,128]{2,1,0:T(8,128)} %bitcast.23), calls=%async_computation.2 | async-start | bytes 786432 | tf_op jit(solution)/shard_map/all_to_all | solution.py:375
  113.9 10.3 %collective-permute-start.9 = (f32[2,3,8,128]{3,2,1,0:T(8,128)S(1)}, f32[2,3,8,128]{3,2,1,0:T(8,128)S(1)}, u32[]{:S(2)}, u32[]{:S(2)}) collective-permute-start(f32[2,3,8,128]{3,2,1,0:T(8,128)S(1)} %bitcast.63), channel_id=1, source_target_pairs={{0,128},{8,136},{16,144},{24,152},{32,160},{40,168},{48,176},{56,1... | collective-permute-start | bytes 73736 | tf_op jit(solution)/shard_map/ppermute | solution.py:418
  119.8 15.9 %collective-permute-start.8 = (f32[4,2,128,128]{3,2,1,0:T(8,128)S(1)}, f32[4,2,128,128]{3,2,1,0:T(8,128)S(1)}, u32[]{:S(2)}, u32[]{:S(2)}) collective-permute-start(f32[4,2,128,128]{3,2,1,0:T(8,128)S(1)} %get-tuple-element.15.low), channel_id=1, source_target_pairs={{1,0},{2,1},{3,2},{4,3},{5,4},{6,5},{7,6},{9,8},{10,9},{11,10},{12... | collective-permute-start | bytes 1572872 | tf_op jit(solution)/shard_map/ppermute | solution.py:372
  121.8 14.0 %collective-permute-start.7 = (f32[4,2,128,128]{3,2,1,0:T(8,128)}, f32[4,2,128,128]{3,2,1,0:T(8,128)S(1)}, u32[]{:S(2)}, u32[]{:S(2)}) collective-permute-start(f32[4,2,128,128]{3,2,1,0:T(8,128)} %get-tuple-element.16.high), channel_id=1, source_target_pairs={{0,1},{1,2},{2,3},{3,4},{4,5},{5,6},{6,7},{8,9},{9,10},{10,11},{11... | collective-permute-start | bytes 1572872 | tf_op jit(solution)/shard_map/ppermute | solution.py:369

commit v3 on v2

--- a/solution.py
+++ b/solution.py
@@ -1,4 +1,3 @@
-import functools
 import math
 
 import jax
@@ -7,6 +6,7 @@
 from jax.experimental import pallas as pl
 from jax.experimental.pallas import tpu as pltpu
 from jax.sharding import PartitionSpec as P
+
 
 rate_scale = 0.3
 ROWS = 8
@@ -198,12 +198,13 @@
 def phase_kernel(phases, cos_out, sin_out, cos_n, sin_n):
     trig_tables(phases, cos_n, sin_n)
 
-    def body(n, _):
-        cos_out[n] = spread(cos_n, n)
-        sin_out[n] = spread(sin_n, n)
-        return 0
-
-    lax.fori_loop(0, LAYERS * ROWS, body, 0)
+    def body(i, _):
+        for n in (2 * i, 2 * i + 1):
+            cos_out[n] = spread(cos_n, n)
+            sin_out[n] = spread(sin_n, n)
+        return 0
+
+    lax.fori_loop(0, LAYERS * ROWS // 2, body, 0)
 
 
 def main_kernel(row_ref, pv, qv, ph_top, ph_bot, cos_own, sin_own, w1,
@@ -215,12 +216,13 @@
         for layer in range(LAYERS):
             lo, hi = (0, 8) if layer != 1 else ((4, 8) if first == 0 else (0, 4))
 
-            def body(r, _, layer=layer, first=first):
-                cosr[layer * EXT + first + r] = spread(cos_n, layer * ROWS + r)
-                sinr[layer * EXT + first + r] = spread(sin_n, layer * ROWS + r)
+            def body(i, _, layer=layer, first=first, lo=lo):
+                for r in (lo + 2 * i, lo + 2 * i + 1):
+                    cosr[layer * EXT + first + r] = spread(cos_n, layer * ROWS + r)
+                    sinr[layer * EXT + first + r] = spread(sin_n, layer * ROWS + r)
                 return 0
 
-            lax.fori_loop(lo, hi, body, 0)
+            lax.fori_loop(0, (hi - lo) // 2, body, 0)
     for layer in range(LAYERS):
         def copy(r, _, layer=layer):
             cosr[layer * EXT + HALO + r] = cos_own[layer * ROWS + r]
@@ -278,14 +280,15 @@
             last_high[r, k] = w2[HALO + 4 + r, k, 8:136, :]
 
     def term(layer, adjoint, stored):
-        def body(r, _):
-            x = adjoint(r, 1) * stored(r, 0) - adjoint(r, 0) * stored(r, 1)
-            x = x.T
-            x = (x[:TILES] + x[TILES:2 * TILES]) + (x[2 * TILES:3 * TILES] + x[3 * TILES:])
-            terms[pl.ds(layer * ROWS + r, TILES, stride=LAYERS * ROWS), :] = x
+        def body(i, _):
+            for r in (2 * i, 2 * i + 1):
+                x = adjoint(r, 1) * stored(r, 0) - adjoint(r, 0) * stored(r, 1)
+                x = x.T
+                x = (x[:TILES] + x[TILES:2 * TILES]) + (x[2 * TILES:3 * TILES] + x[3 * TILES:])
+                terms[pl.ds(layer * ROWS + r, TILES, stride=LAYERS * ROWS), :] = x
             return 0
 
-        lax.fori_loop(0, ROWS, body, 0)
+        lax.fori_loop(0, ROWS // 2, body, 0)
 
     def own(ref):
         return lambda r, k: ref[HALO + r, k, 8:136, :]
@@ -324,6 +327,36 @@
     term(0, lambda r, k: raw[r + 4, k], own(u))
 
 
+def deal_kernel(mine, out):
+    for t in range(TILES):
+        x = mine[:, 128 * t:128 * (t + 1)]
+        out[t // 2, t % 2] = x
+        out[PLANE + t // 2, t % 2] = x
+
+
+def pick_kernel(order, got, out):
+    for layer in range(LAYERS):
+        for t in range(2):
+            x = got[order[layer], t]
+            for d in range(PLANE):
+                out[d, t, layer] = x
+
+
+def gather_kernel(order, parts, out):
+    out[...] = jnp.zeros_like(out)
+    for layer in range(LAYERS):
+        for t in range(2):
+            x = [parts[d, t, layer] for d in range(PLANE)]
+            while len(x) > 1:
+                x = [a + b for a, b in zip(x[::2], x[1::2])]
+            out[order[layer], t] = x[0]
+
+
+def finish_kernel(got, out):
+    for t in range(TILES):
+        out[:, 128 * t:128 * (t + 1)] = got[t // 2, t % 2] + got[PLANE + t // 2, t % 2]
+
+
 def vm():
     return pl.BlockSpec(memory_space=pltpu.VMEM)
 
@@ -348,22 +381,19 @@
     return scr(rows, 2, PAD, 128)
 
 
-def call(kernel, ins, outs, scratch, name, mib):
+def call(kernel, ins, outs, scratch, mib):
     return pl.pallas_call(
         kernel, out_shape=outs, in_specs=ins, out_specs=jax.tree.map(lambda _: vm(), outs),
-        scratch_shapes=scratch, name=name,
+        scratch_shapes=scratch,
         compiler_params=pltpu.CompilerParams(vmem_limit_bytes=mib << 20),
         cost_estimate=pl.CostEstimate(flops=20_000_000, bytes_accessed=4 << 20, transcendentals=0),
     )
 
 
-def body(angles, depth_order, slices, cotangent):
+def forward_and_back(angles, depth_order, slices, cotangent):
     row = lax.axis_index("row").astype(jnp.int32).reshape(1)
-    z = lax.axis_index("illum") // PLANE
-    here = lax.axis_index("illum") % PLANE
     n_row = lax.axis_size("row")
     groups = [list(range(g * PLANE, (g + 1) * PLANE)) for g in range(2)]
-    swap = [(i, (i + PLANE) % (2 * PLANE)) for i in range(2 * PLANE)]
 
     def to_next(x, by):
         return lax.ppermute(x, "row", [(i, i + by) for i in range(n_row - by)])
@@ -371,36 +401,29 @@
     def to_prev(x, by):
         return lax.ppermute(x, "row", [(i + by, i) for i in range(n_row - by)])
 
-    def exchange(x):
-        return lax.all_to_all(x, "illum", 0, 0, axis_index_groups=groups, tiled=True)
-
-    mine = slices[0]
-    other = lax.ppermute(mine, "illum", swap)
-
+    def exchange(x, groups=None):
+        flat = x.reshape(-1, 128)
+        flat = lax.all_to_all(flat, "illum", 0, 0, axis_index_groups=groups, tiled=True)
+        return flat.reshape(x.shape)
+
+    dealt = call(deal_kernel, [vm()], shape(2 * PLANE, 2, ROWS, 128), [], 4)(slices[0])
+    got = exchange(dealt)
     cot = cotangent.reshape(8, ROWS, TILES, 128).transpose(0, 2, 1, 3).reshape(-1, 128)
-    own, low, high = call(split_kernel, [vm()], (field(8), field(4), field(4)), [], "split", 8)(cot)
+    own, low, high = call(
+        split_kernel, [vm()], (field(8), field(4), field(4)), [], 6)(cot)
     top, bot = to_next(own, 1), to_prev(own, 1)
     top2, bot2 = to_next(high, 2), to_prev(low, 2)
-
-    both = jnp.stack([jnp.where(z == 0, mine, other), jnp.where(z == 0, other, mine)], 0)
-    both = both.reshape(2 * ROWS, TILES, 128).transpose(1, 0, 2)
-    got = exchange(both.reshape(TILES * 2 * ROWS, 128)).reshape(PLANE, 2, 2, ROWS, 128)
-    picked = [
-        lax.dynamic_slice(got, (depth_order[l] % PLANE, 0, depth_order[l] // PLANE, 0, 0),
-                          (1, 2, 1, ROWS, 128))[0]
-        for l in range(LAYERS)
-    ]
-    piece = jnp.concatenate(picked, 1).reshape(1, 2 * LAYERS * ROWS, 128)
-    phases = exchange(
-        jnp.broadcast_to(piece, (PLANE, 2 * LAYERS * ROWS, 128)).reshape(-1, 128))
+    piece = call(pick_kernel, [sm(), vm()], shape(PLANE, 2, LAYERS, ROWS, 128), [],
+                 4)(depth_order, got)
+    phases = exchange(piece, groups).reshape(-1, 128)
     ph_top, ph_bot = to_next(phases, 1), to_prev(phases, 1)
 
-    w1 = call(adjoint_kernel, [sm()] + [vm()] * 5, field(EXT), [wide(32)] * 4, "adjoint1", 26)(
-        row, own, top, bot, top2, bot2)
     table = scr(TILES * LAYERS * ROWS, 128)
     cos_own, sin_own = call(
-        phase_kernel, [vm()], (shape(LAYERS * ROWS, 128, 128),) * 2, [table] * 2, "phases", 8)(
-            phases)
+        phase_kernel, [vm()], (shape(LAYERS * ROWS, 128, 128),) * 2, [table] * 2,
+        5)(phases)
+    w1 = call(adjoint_kernel, [sm()] + [vm()] * 5, field(EXT), [wide(32)] * 4,
+              20)(row, own, top, bot, top2, bot2)
 
     pv = jnp.broadcast_to(jnp.repeat(angles[:, 0], TILES)[None], (8, 128))
     qv = jnp.broadcast_to(jnp.repeat(angles[:, 1], TILES)[None], (8, 128))
@@ -409,30 +432,25 @@
         main_kernel, [sm()] + [vm()] * 7,
         (shape(TILES * LAYERS * ROWS, 128), field(4), field(4)),
         [table, table, spreads, spreads, scr(2, 128, 128)] + [wide(EXT)] * 4
-        + [scr(16, 2, 128, 128)] + [wide(EXT)] * 3, "main", 52)(
+        + [scr(16, 2, 128, 128)] + [wide(EXT)] * 3, 40)(
             row, pv, qv, ph_top, ph_bot, cos_own, sin_own, w1)
     r_top, r_bot = to_next(last_high, 1), to_prev(last_low, 1)
-
-    parts = exchange(terms).reshape(PLANE, 2, LAYERS, ROWS, 128)
-    half = jnp.sum(parts, axis=0)
-    full = half + lax.ppermute(half, "illum", swap)
-    owners = jnp.arange(PLANE, dtype=jnp.int32) + z * PLANE
-    send = sum(
-        jnp.where((owners == depth_order[l])[:, None, None, None], full[None, :, l], 0.0)
-        for l in range(LAYERS))
+    parts = exchange(terms, groups).reshape(PLANE, 2, LAYERS, ROWS, 128)
+    send = call(gather_kernel, [sm(), vm()], shape(2 * PLANE, 2, ROWS, 128), [],
+                4)(depth_order, parts)
+    back = exchange(send)
     out = call(exit_kernel, [sm()] + [vm()] * 4, shape(2048, 128),
-               [wide(16)] * 4 + [scr(8, 2, 128, 128)], "exit", 16)(
+               [wide(16)] * 4 + [scr(8, 2, 128, 128)], 12)(
                    row, last_low, last_high, r_top, r_bot)
-    grad = exchange(send.reshape(TILES * ROWS, 128)).reshape(TILES, ROWS, 128)
-    grad = grad.transpose(1, 0, 2).reshape(1, ROWS, COLS)
+    grad = call(finish_kernel, [vm()], shape(ROWS, COLS), [], 4)(back)
     out = out.reshape(8, TILES, ROWS, 128).transpose(0, 2, 1, 3)
-    return out.reshape(cotangent.shape), grad
+    return out.reshape(cotangent.shape), grad[None]
 
 
 def solution(mesh):
     placed = (P("illum", None), P(), P("illum", "row", None), P("illum", None, "row", None))
     return jax.shard_map(
-        body,
+        forward_and_back,
         mesh=mesh,
         in_specs=placed,
         out_specs=(P("illum", None, "row", None), P("illum", "row", None)),

time: 143 us -> 122 us (0.85); the launches traced: 140 us -> 121 us
  blocking collectives: 11.4 us -> 0 us
  between operations: 8.68 us -> 0.87 us
  waiting for transfers between devices: 22.3 us -> 28.1 us
  local copies, waits for them, and re-layouts: 7.37 us -> 3.26 us
  other arithmetic: 3.03 us -> 0 us
  starting transfers between devices: 49 us -> 51.7 us
  Pallas kernels: 38.5 us -> 36.8 us
    all_to_all x3 -> x4, starting transfers between devices: 18.5 us -> 32.1 us  [exchange(): lax.all_to_all(flat, 'illum', 0, 0, axis_index_groups=groups, tiled=True)]
    all_to_all x3 -> x4, waiting for transfers between devices: 15.7 us -> 28.1 us  [exchange(): lax.all_to_all(flat, 'illum', 0, 0, axis_index_groups=groups, tiled=True)]
    ppermute x2 -> x0, starting transfers between devices: 11.6 us -> none  [the longest x1 6.38 us: body(): other = lax.ppermute(mine, 'illum', swap)]
    all_to_all x1 -> x0, blocking collectives: 11.4 us -> none  [exchange(): lax.all_to_all(x, 'illum', 0, 0, axis_index_groups=groups, tiled=True)]
    ppermute x2 -> x0, waiting for transfers between devices: 6.57 us -> none  [the longest x1 6.56 us: body(): other = lax.ppermute(mine, 'illum', swap)]
    eq x2 -> x0, other arithmetic: 1.92 us -> none  [body(): owners == depth_order[l]]
    unnamed x16 -> x10, local copies, waits for them, and re-layouts: 4.72 us -> 2.94 us
    pallas_call x5 -> x9, Pallas kernels: 38.5 us -> 36.8 us  [the longest x1 19.4 us: forward_and_back(): call(main_kernel, [sm()] + [vm()] * 7, (shape(TILES * LAYERS * ROWS, 128)...]
  transfers between devices with their start and end apart: 13 -> 12, of which waited for: 3 -> 4; matrix products, arithmetic and copies ran while one was open for 3% -> 0% of each run, Pallas kernels for 8% -> 13%
where the time goes in v3:
time: 122 us; the launch traced here: 121 us
  starting transfers between devices  51.7 us (42%)
  Pallas kernels  36.8 us (30%)
  waiting for transfers between devices  28.1 us (23%)
  local copies, waits for them, and re-layouts  3.26 us (3%)
    all_to_all x4, starting transfers between devices, exchange(): lax.all_to_all(flat, 'illum', 0, 0, axis_index_groups=groups, tiled=True)  32.1 us
    all_to_all x4, waiting for transfers between devices, exchange(): lax.all_to_all(flat, 'illum', 0, 0, axis_index_groups=groups, tiled=True)  28.1 us
    pallas_call x1, Pallas kernels, forward_and_back(): call(main_kernel, [sm()] + [vm()] * 7, (shape(TILES * LAYERS * ROWS, 128)...  19.4 us
    ppermute x4, starting transfers between devices, to_next(): return lax.ppermute(x, 'row', [(i, i + by) for i in range(n_row - by)])  11.2 us
    ppermute x4, starting transfers between devices, to_prev(): return lax.ppermute(x, 'row', [(i + by, i) for i in range(n_row - by)])  8.43 us
    pallas_call x1, Pallas kernels, forward_and_back(): call(adjoint_kernel, [sm()] + [vm()] * 5, field(EXT), [wide(32)] * 4, 20)  5.67 us
    pallas_call x1, Pallas kernels, forward_and_back(): call(exit_kernel, [sm()] + [vm()] * 4, shape(2048, 128), [wide(16)] * 4 +...  3.77 us
    unnamed x10, local copies, waits for them, and re-layouts  2.94 us
  transfers between devices with their start and end apart: 12, of which 4 were waited for; matrix products, arithmetic and copies ran while one was open for 0% of the time, Pallas kernels for 13%

profile of v3, /device:TPU:32, one launch (start us, length us, event | category | flops | bytes accessed | tf_op | source)
XLA Modules:
  0.0 120.7 jit_solution(403416481723343708)
XLA Ops:
  0.6 0.0 copy-start.2
  0.6 0.0 copy-start.1
  0.6 0.9 copy-done.1
  1.6 0.7 shard_map.59
  2.3 0.0 copy-start.4
  2.3 13.2 %all-to-all-start = ((f32[32,16,128]{2,1,0:T(8,128)}), f32[32,16,128]{2,1,0:T(8,128)S(1)}, u32[]{:S(2)}, u32[]{:S(2)}) async-start(f32[32,16,128]{2,1,0:T(8,128)} %bitcast.4), calls=%async_computation | async-start | bytes 524288 | tf_op jit(solution)/shard_map/all_to_all | solution.py:406
  15.5 0.0 copy-start
  15.5 1.2 %copy-done = f32[4,2,8,4096]{3,2,1,0:T(8,128)S(1)} copy-done((f32[4,2,8,4096]{3,2,1,0:T(8,128)S(1)}, f32[4,2,8,4096]{3,2,1,0:T(8,128)}, u32[]{:S(2)}) %copy-start) | copy-done | bytes 1048600
  16.7 1.7 %shard_map.62 = (f32[8,2,128,128]{3,2,1,0:T(8,128)S(1)}, f32[4,2,128,128]{3,2,1,0:T(8,128)S(1)}, f32[4,2,128,128]{3,2,1,0:T(8,128)}) custom-call(f32[2048,128]{1,0:T(8,128)S(1)} %bitcast.29), custom_call_target="tpu_custom_call" | custom-call | flops 20000000 | bytes 4194304 | tf_op jit(solution)/shard_map/pallas_call | solution.py:412
  18.4 0.0 copy-start.3
  18.4 0.8 copy-done.3
  19.2 2.1 %collective-permute-start.3 = (f32[8,2,128,128]{3,2,1,0:T(8,128)S(1)}, f32[8,2,128,128]{3,2,1,0:T(8,128)S(1)}, u32[]{:S(2)}, u32[]{:S(2)}) collective-permute-start(f32[8,2,128,128]{3,2,1,0:T(8,128)S(1)} %get-tuple-element.12.own), channel_id=1, source_target_pairs={{1,0},{2,1},{3,2},{4,3},{5,4},{6,5},{7,6},{9,8},{10,9},{11,10},{12... | collective-permute-start | bytes 3145736 | tf_op jit(solution)/shard_map/ppermute | solution.py:402
  21.2 2.3 %collective-permute-start.2 = (f32[8,2,128,128]{3,2,1,0:T(8,128)S(1)}, f32[8,2,128,128]{3,2,1,0:T(8,128)S(1)}, u32[]{:S(2)}, u32[]{:S(2)}) collective-permute-start(f32[8,2,128,128]{3,2,1,0:T(8,128)S(1)} %get-tuple-element.12.own), channel_id=1, source_target_pairs={{0,1},{1,2},{2,3},{3,4},{4,5},{5,6},{6,7},{8,9},{9,10},{10,11},{11... | collective-permute-start | bytes 3145736 | tf_op jit(solution)/shard_map/ppermute | solution.py:399
  23.5 2.9 %collective-permute-start.4 = (f32[4,2,128,128]{3,2,1,0:T(8,128)}, f32[4,2,128,128]{3,2,1,0:T(8,128)}, u32[]{:S(2)}, u32[]{:S(2)}) collective-permute-start(f32[4,2,128,128]{3,2,1,0:T(8,128)} %get-tuple-element.13), channel_id=1, source_target_pairs={{0,2},{1,3},{2,4},{3,5},{4,6},{5,7},{8,10},{9,11},{10,12},{11,13},... | collective-permute-start | bytes 1572872 | tf_op jit(solution)/shard_map/ppermute | solution.py:399
  26.4 5.0 %all-to-all-done = f32[32,16,128]{2,1,0:T(8,128)S(1)} async-done(((f32[32,16,128]{2,1,0:T(8,128)}), f32[32,16,128]{2,1,0:T(8,128)S(1)}, u32[]{:S(2)}, u32[]{:S(2)}) %all-to-all-start) | async-done | bytes 262176 | tf_op jit(solution)/shard_map/all_to_all | solution.py:406
  31.4 0.0 copy-done.2
  31.4 1.4 %shard_map.60 = f32[16,2,3,8,128]{4,3,2,1,0:T(8,128)} custom-call(s32[3]{0:T(128)S(1)} %copy-done.2, f32[32,2,8,128]{3,2,1,0:T(8,128)S(1)} %bitcast.30), custom_call_target="tpu_custom_call" | custom-call | flops 20000000 | bytes 4194304 | tf_op jit(solution)/shard_map/pallas_call | solution.py:416
  32.8 3.6 %all-to-all-start.1 = ((f32[16,48,128]{2,1,0:T(8,128)}), f32[16,48,128]{2,1,0:T(8,128)S(1)}, u32[]{:S(2)}, u32[]{:S(2)}) async-start(f32[16,48,128]{2,1,0:T(8,128)} %bitcast.6), calls=%async_computation.1 | async-start | bytes 786432 | tf_op jit(solution)/shard_map/all_to_all | solution.py:406
  36.3 2.3 %collective-permute-start.5 = (f32[4,2,128,128]{3,2,1,0:T(8,128)}, f32[4,2,128,128]{3,2,1,0:T(8,128)}, u32[]{:S(2)}, u32[]{:S(2)}) collective-permute-start(f32[4,2,128,128]{3,2,1,0:T(8,128)} %copy-done.3), channel_id=1, source_target_pairs={{2,0},{3,1},{4,2},{5,3},{6,4},{7,5},{10,8},{11,9},{12,10},{13,11},... | collective-permute-start | bytes 1572872 | tf_op jit(solution)/shard_map/ppermute | solution.py:402
  38.6 6.8 %all-to-all-done.1 = f32[16,48,128]{2,1,0:T(8,128)S(1)} async-done(((f32[16,48,128]{2,1,0:T(8,128)}), f32[16,48,128]{2,1,0:T(8,128)S(1)}, u32[]{:S(2)}, u32[]{:S(2)}) %all-to-all-start.1) | async-done | bytes 393248 | tf_op jit(solution)/shard_map/all_to_all | solution.py:406
  45.4 2.1 %collective-permute-start.1 = (f32[768,128]{1,0:T(8,128)S(1)}, f32[768,128]{1,0:T(8,128)}, u32[]{:S(2)}, u32[]{:S(2)}) collective-permute-start(f32[768,128]{1,0:T(8,128)S(1)} %bitcast.25), channel_id=1, source_target_pairs={{1,0},{2,1},{3,2},{4,3},{5,4},{6,5},{7,6},{9,8},{10,9},{11,10},{12... | collective-permute-start | bytes 1179656 | tf_op jit(solution)/shard_map/ppermute | solution.py:402
  47.6 0.0 collective-permute-done.4.top2
  47.6 3.6 %collective-permute-start = (f32[768,128]{1,0:T(8,128)S(1)}, f32[768,128]{1,0:T(8,128)}, u32[]{:S(2)}, u32[]{:S(2)}) collective-permute-start(f32[768,128]{1,0:T(8,128)S(1)} %bitcast.26), channel_id=1, source_target_pairs={{0,1},{1,2},{2,3},{3,4},{4,5},{5,6},{6,7},{8,9},{9,10},{10,11},{11... | collective-permute-start | bytes 1179656 | tf_op jit(solution)/shard_map/ppermute | solution.py:399
  51.2 0.0 copy-done.4
  51.2 0.1 broadcast_in_dim.26
  51.2 0.1 broadcast_in_dim.27
  51.3 0.1 broadcast_in_dim.23
  51.4 0.1 broadcast_in_dim.24
  51.5 2.2 %shard_map.61 = (f32[24,128,128]{2,1,0:T(8,128)S(1)}, f32[24,128,128]{2,1,0:T(8,128)S(1)}) custom-call(f32[768,128]{1,0:T(8,128)S(1)} %bitcast.27), custom_call_target="tpu_custom_call" | custom-call | flops 20000000 | bytes 4194304 | tf_op jit(solution)/shard_map/pallas_call | solution.py:422
  53.7 0.0 collective-permute-done.5.bot2
  53.7 0.0 collective-permute-done.3.bot
  53.8 0.0 collective-permute-done.2.top
  53.8 5.7 %shard_map.63.w1 = f32[24,2,128,128]{3,2,1,0:T(8,128)S(1)} custom-call(s32[1]{0:T(128)} %bitcast.row_ref, f32[8,2,128,128]{3,2,1,0:T(8,128)S(1)} %get-tuple-element.12.own, f32[8,2,128,128]{3,2,1,0:T(8,128)S(1)} %collective-permute-done.2.top, f32[8,2,128,128]{3,2,1,0:T(8,128)S(1)} %collective-permute-done.3.bot, ...), custom_call_target="tpu_custom_call" | custom-call | flops 20000000 | bytes 4194304 | tf_op jit(solution)/shard_map/pallas_call | solution.py:425
  59.4 0.0 collective-permute-done.1.ph_bot
  59.5 0.0 collective-permute-done.ph_top
  59.5 19.4 %shard_map.64 = (f32[768,128]{1,0:T(8,128)}, f32[4,2,128,128]{3,2,1,0:T(8,128)S(1)}, f32[4,2,128,128]{3,2,1,0:T(8,128)S(1)}) custom-call(s32[1]{0:T(128)} %bitcast.row_ref, s32[8,128]{1,0:T(8,128)S(1)} %broadcast_in_dim.25.pv, s32[8,128]{1,0:T(8,128)S(1)} %broadcast_in_dim.28.qv, f32[768,128]{1,0:T(8,128)} %collective-permute-done.ph_top, ...), custom_call_target="tpu_custom_call" | custom-call | flops 20000000 | bytes 4194304 | tf_op jit(solution)/shard_map/pallas_call | solution.py:431
  78.9 6.8 %all-to-all-start.2 = ((f32[16,48,128]{2,1,0:T(8,128)}), f32[16,48,128]{2,1,0:T(8,128)S(1)}, u32[]{:S(2)}, u32[]{:S(2)}) async-start(f32[16,48,128]{2,1,0:T(8,128)} %bitcast.14), calls=%async_computation.2 | async-start | bytes 786432 | tf_op jit(solution)/shard_map/all_to_all | solution.py:406
  85.7 1.9 %collective-permute-start.7 = (f32[4,2,128,128]{3,2,1,0:T(8,128)S(1)}, f32[4,2,128,128]{3,2,1,0:T(8,128)S(1)}, u32[]{:S(2)}, u32[]{:S(2)}) collective-permute-start(f32[4,2,128,128]{3,2,1,0:T(8,128)S(1)} %get-tuple-element.15.low), channel_id=1, source_target_pairs={{1,0},{2,1},{3,2},{4,3},{5,4},{6,5},{7,6},{9,8},{10,9},{11,10},{12... | collective-permute-start | bytes 1572872 | tf_op jit(solution)/shard_map/ppermute | solution.py:402
  87.6 2.4 %collective-permute-start.6 = (f32[4,2,128,128]{3,2,1,0:T(8,128)S(1)}, f32[4,2,128,128]{3,2,1,0:T(8,128)S(1)}, u32[]{:S(2)}, u32[]{:S(2)}) collective-permute-start(f32[4,2,128,128]{3,2,1,0:T(8,128)S(1)} %get-tuple-element.16.high), channel_id=1, source_target_pairs={{0,1},{1,2},{2,3},{3,4},{4,5},{5,6},{6,7},{8,9},{9,10},{10,11},{11... | collective-permute-start | bytes 1572872 | tf_op jit(solution)/shard_map/ppermute | solution.py:399
  90.0 5.7 %all-to-all-done.2 = f32[16,48,128]{2,1,0:T(8,128)S(1)} async-done(((f32[16,48,128]{2,1,0:T(8,128)}), f32[16,48,128]{2,1,0:T(8,128)S(1)}, u32[]{:S(2)}, u32[]{:S(2)}) %all-to-all-start.2) | async-done | bytes 393248 | tf_op jit(solution)/shard_map/all_to_all | solution.py:406
  95.7 1.3 %shard_map.66 = f32[32,2,8,128]{3,2,1,0:T(8,128)} custom-call(s32[3]{0:T(128)S(1)} %copy-done.2, f32[16,2,3,8,128]{4,3,2,1,0:T(8,128)S(1)} %bitcast.28), custom_call_target="tpu_custom_call" | custom-call | flops 20000000 | bytes 4194304 | tf_op jit(solution)/shard_map/pallas_call | solution.py:439
  97.0 8.6 %all-to-all-start.3 = ((f32[32,16,128]{2,1,0:T(8,128)}), f32[32,16,128]{2,1,0:T(8,128)S(1)}, u32[]{:S(2)}, u32[]{:S(2)}) async-start(f32[32,16,128]{2,1,0:T(8,128)} %bitcast.16), calls=%async_computation.3 | async-start | bytes 524288 | tf_op jit(solution)/shard_map/all_to_all | solution.py:406
  105.6 0.0 collective-permute-done.7.bot
  105.6 0.0 collective-permute-done.6.top
  105.6 3.8 %shard_map.65 = f32[2048,128]{1,0:T(8,128)} custom-call(s32[1]{0:T(128)} %bitcast.row_ref, f32[4,2,128,128]{3,2,1,0:T(8,128)S(1)} %get-tuple-element.15.low, f32[4,2,128,128]{3,2,1,0:T(8,128)S(1)} %get-tuple-element.16.high, f32[4,2,128,128]{3,2,1,0:T(8,128)S(1)} %collective-permute-done.6.top, f32[4,2,128,128]{3,2,1,0:T(8,128)S(1)} %collective-permute-done.7.bot), custom_call_target="tpu_custom_call" | custom-call | flops 20000000 | bytes 4194304 | tf_op jit(solution)/shard_map/pallas_call | solution.py:442
  109.3 10.7 %all-to-all-done.3 = f32[32,16,128]{2,1,0:T(8,128)S(1)} async-done(((f32[32,16,128]{2,1,0:T(8,128)}), f32[32,16,128]{2,1,0:T(8,128)S(1)}, u32[]{:S(2)}, u32[]{:S(2)}) %all-to-all-start.3) | async-done | bytes 262176 | tf_op jit(solution)/shard_map/all_to_all | solution.py:406
  120.1 0.7 shard_map.67
  (3 shorter events, 0.0 us)
Async XLA Ops:
  0.6 30.8 %copy-start.2 = (s32[3]{0:T(128)S(1)}, s32[3]{0:T(128)}, u32[]{:S(2)}) copy-start(s32[3]{0:T(128)} %order.3) | copy-start | bytes 40
  0.6 0.9 copy-start.1
  2.3 48.9 %copy-start.4 = (s32[4,2]{0,1:T(2,128)S(1)}, s32[4,2]{0,1:T(2,128)}, u32[]{:S(2)}) copy-start(s32[4,2]{0,1:T(2,128)} %param.4) | copy-start | bytes 100
  2.3 29.1 %all-to-all-start = ((f32[32,16,128]{2,1,0:T(8,128)}), f32[32,16,128]{2,1,0:T(8,128)S(1)}, u32[]{:S(2)}, u32[]{:S(2)}) async-start(f32[32,16,128]{2,1,0:T(8,128)} %bitcast.4), calls=%async_computation | async-start | bytes 524288 | tf_op jit(solution)/shard_map/all_to_all | solution.py:406
  15.5 1.2 %copy-start = (f32[4,2,8,4096]{3,2,1,0:T(8,128)S(1)}, f32[4,2,8,4096]{3,2,1,0:T(8,128)}, u32[]{:S(2)}) copy-start(f32[4,2,8,4096]{3,2,1,0:T(8,128)} %param.7) | copy-start | bytes 3145732
  18.4 0.8 copy-start.3
  19.2 34.6 %collective-permute-start.3 = (f32[8,2,128,128]{3,2,1,0:T(8,128)S(1)}, f32[8,2,128,128]{3,2,1,0:T(8,128)S(1)}, u32[]{:S(2)}, u32[]{:S(2)}) collective-permute-start(f32[8,2,128,128]{3,2,1,0:T(8,128)S(1)} %get-tuple-element.12.own), channel_id=1, source_target_pairs={{1,0},{2,1},{3,2},{4,3},{5,4},{6,5},{7,6},{9,8},{10,9},{11,10},{12... | collective-permute-start | bytes 3145736 | tf_op jit(solution)/shard_map/ppermute | solution.py:402
  21.2 32.5 %collective-permute-start.2 = (f32[8,2,128,128]{3,2,1,0:T(8,128)S(1)}, f32[8,2,128,128]{3,2,1,0:T(8,128)S(1)}, u32[]{:S(2)}, u32[]{:S(2)}) collective-permute-start(f32[8,2,128,128]{3,2,1,0:T(8,128)S(1)} %get-tuple-element.12.own), channel_id=1, source_target_pairs={{0,1},{1,2},{2,3},{3,4},{4,5},{5,6},{6,7},{8,9},{9,10},{10,11},{11... | collective-permute-start | bytes 3145736 | tf_op jit(solution)/shard_map/ppermute | solution.py:399
  23.5 24.0 %collective-permute-start.4 = (f32[4,2,128,128]{3,2,1,0:T(8,128)}, f32[4,2,128,128]{3,2,1,0:T(8,128)}, u32[]{:S(2)}, u32[]{:S(2)}) collective-permute-start(f32[4,2,128,128]{3,2,1,0:T(8,128)} %get-tuple-element.13), channel_id=1, source_target_pairs={{0,2},{1,3},{2,4},{3,5},{4,6},{5,7},{8,10},{9,11},{10,12},{11,13},... | collective-permute-start | bytes 1572872 | tf_op jit(solution)/shard_map/ppermute | solution.py:399
  32.8 12.6 %all-to-all-start.1 = ((f32[16,48,128]{2,1,0:T(8,128)}), f32[16,48,128]{2,1,0:T(8,128)S(1)}, u32[]{:S(2)}, u32[]{:S(2)}) async-start(f32[16,48,128]{2,1,0:T(8,128)} %bitcast.6), calls=%async_computation.1 | async-start | bytes 786432 | tf_op jit(solution)/shard_map/all_to_all | solution.py:406
  36.3 17.4 %collective-permute-start.5 = (f32[4,2,128,128]{3,2,1,0:T(8,128)}, f32[4,2,128,128]{3,2,1,0:T(8,128)}, u32[]{:S(2)}, u32[]{:S(2)}) collective-permute-start(f32[4,2,128,128]{3,2,1,0:T(8,128)} %copy-done.3), channel_id=1, source_target_pairs={{2,0},{3,1},{4,2},{5,3},{6,4},{7,5},{10,8},{11,9},{12,10},{13,11},... | collective-permute-start | bytes 1572872 | tf_op jit(solution)/shard_map/ppermute | solution.py:402
  45.4 14.0 %collective-permute-start.1 = (f32[768,128]{1,0:T(8,128)S(1)}, f32[768,128]{1,0:T(8,128)}, u32[]{:S(2)}, u32[]{:S(2)}) collective-permute-start(f32[768,128]{1,0:T(8,128)S(1)} %bitcast.25), channel_id=1, source_target_pairs={{1,0},{2,1},{3,2},{4,3},{5,4},{6,5},{7,6},{9,8},{10,9},{11,10},{12... | collective-permute-start | bytes 1179656 | tf_op jit(solution)/shard_map/ppermute | solution.py:402
  47.6 11.9 %collective-permute-start = (f32[768,128]{1,0:T(8,128)S(1)}, f32[768,128]{1,0:T(8,128)}, u32[]{:S(2)}, u32[]{:S(2)}) collective-permute-start(f32[768,128]{1,0:T(8,128)S(1)} %bitcast.26), channel_id=1, source_target_pairs={{0,1},{1,2},{2,3},{3,4},{4,5},{5,6},{6,7},{8,9},{9,10},{10,11},{11... | collective-permute-start | bytes 1179656 | tf_op jit(solution)/shard_map/ppermute | solution.py:399
  78.9 16.8 %all-to-all-start.2 = ((f32[16,48,128]{2,1,0:T(8,128)}), f32[16,48,128]{2,1,0:T(8,128)S(1)}, u32[]{:S(2)}, u32[]{:S(2)}) async-start(f32[16,48,128]{2,1,0:T(8,128)} %bitcast.14), calls=%async_computation.2 | async-start | bytes 786432 | tf_op jit(solution)/shard_map/all_to_all | solution.py:406
  85.7 19.9 %collective-permute-start.7 = (f32[4,2,128,128]{3,2,1,0:T(8,128)S(1)}, f32[4,2,128,128]{3,2,1,0:T(8,128)S(1)}, u32[]{:S(2)}, u32[]{:S(2)}) collective-permute-start(f32[4,2,128,128]{3,2,1,0:T(8,128)S(1)} %get-tuple-element.15.low), channel_id=1, source_target_pairs={{1,0},{2,1},{3,2},{4,3},{5,4},{6,5},{7,6},{9,8},{10,9},{11,10},{12... | collective-permute-start | bytes 1572872 | tf_op jit(solution)/shard_map/ppermute | solution.py:402
  87.6 17.9 %collective-permute-start.6 = (f32[4,2,128,128]{3,2,1,0:T(8,128)S(1)}, f32[4,2,128,128]{3,2,1,0:T(8,128)S(1)}, u32[]{:S(2)}, u32[]{:S(2)}) collective-permute-start(f32[4,2,128,128]{3,2,1,0:T(8,128)S(1)} %get-tuple-element.16.high), channel_id=1, source_target_pairs={{0,1},{1,2},{2,3},{3,4},{4,5},{5,6},{6,7},{8,9},{9,10},{10,11},{11... | collective-permute-start | bytes 1572872 | tf_op jit(solution)/shard_map/ppermute | solution.py:399
  97.0 23.1 %all-to-all-start.3 = ((f32[32,16,128]{2,1,0:T(8,128)}), f32[32,16,128]{2,1,0:T(8,128)S(1)}, u32[]{:S(2)}, u32[]{:S(2)}) async-start(f32[32,16,128]{2,1,0:T(8,128)} %bitcast.16), calls=%async_computation.3 | async-start | bytes 524288 | tf_op jit(solution)/shard_map/all_to_all | solution.py:406

commit v4 on v3

--- a/solution.py
+++ b/solution.py
@@ -118,16 +118,26 @@
     return pl.ds((g * 2 + k) * TILES * ROWS + r, TILES, stride=ROWS)
 
 
-def split_kernel(cot, out, low, high):
+def turn_rows(cot, out):
     def body(r, _):
         for k in range(2):
             out[r, k] = jnp.concatenate([cot[natural(g, k, r), :] for g in range(4)], axis=0).T
         return 0
 
     lax.fori_loop(0, ROWS, body, 0)
+
+
+def split_kernel(ids, cot, out, send_e, send_o):
+    turn_rows(cot, out)
+    upper = (ids[0] >> 1) & 1
     for r in range(4):
-        low[r] = out[r]
-        high[r] = out[r + 4]
+        send_e[r] = out[r + 4 * (1 - upper)]
+        send_o[r] = out[r + 4 * upper]
+
+
+def halo_kernel(cot_e, cot_o, out_e, out_o):
+    turn_rows(cot_e, out_e)
+    turn_rows(cot_o, out_o)
 
 
 def put(dst, at, src, n):
@@ -139,13 +149,14 @@
     lax.fori_loop(0, n, body, 0)
 
 
-def adjoint_kernel(row_ref, own, top, bot, top2, bot2, out, u, l1, l2, l3):
-    row = row_ref[0]
-    put(u, 0, top2, 4)
-    put(u, 4, top, 8)
+def adjoint_kernel(ids, own, halo_e, halo_o, far_e, far_o, out, u, l1, l2, l3):
+    row = ids[0]
+    odd, upper = row & 1, (row >> 1) & 1
     put(u, 12, own, 8)
-    put(u, 20, bot, 8)
-    put(u, 28, bot2, 4)
+    put(u, 20 - 16 * odd, halo_e, 8)
+    put(u, 4 + 16 * odd, halo_o, 8)
+    put(u, 28 - 28 * upper, far_e, 4)
+    put(u, 28 * upper, far_o, 4)
     fill_pads(u, 32)
 
     def write(r, j, re, im):
@@ -155,12 +166,13 @@
     step(row, u, 32, 12, 12, (l1, l2, l3), -rate_scale, write)
 
 
-def exit_kernel(row_ref, low, high, top, bot, out, u, l1, l2, l3, res):
-    row = row_ref[0]
-    put(u, 0, top, 4)
-    put(u, 4, low, 4)
-    put(u, 8, high, 4)
-    put(u, 12, bot, 4)
+def exit_kernel(ids, sent_e, sent_o, got_e, got_o, out, u, l1, l2, l3, res):
+    row = ids[0]
+    odd = row & 1
+    put(u, 8 - 4 * odd, sent_e, 4)
+    put(u, 4 + 4 * odd, sent_o, 4)
+    put(u, 12 - 12 * odd, got_e, 4)
+    put(u, 12 * odd, got_o, 4)
     fill_pads(u, 16)
 
     def write(r, j, re, im):
@@ -207,22 +219,25 @@
     lax.fori_loop(0, LAYERS * ROWS // 2, body, 0)
 
 
-def main_kernel(row_ref, pv, qv, ph_top, ph_bot, cos_own, sin_own, w1,
-                terms, last_low, last_high,
+def main_kernel(ids, pv, qv, ph_e, ph_o, cos_own, sin_own, w1,
+                terms, last_e, last_o,
                 cos_n, sin_n, cosr, sinr, beam, u, v, w, w2, raw, l1, l2, l3):
-    row = row_ref[0]
-    for ph, first in ((ph_top, 0), (ph_bot, HALO + ROWS)):
+    row = ids[0]
+    odd = row & 1
+    for ph, above in ((ph_e, odd), (ph_o, 1 - odd)):
         trig_tables(ph, cos_n, sin_n)
+        first = (HALO + ROWS) * (1 - above)
         for layer in range(LAYERS):
-            lo, hi = (0, 8) if layer != 1 else ((4, 8) if first == 0 else (0, 4))
+            lo, count = (4 * above, 4) if layer == 1 else (0, 8)
 
             def body(i, _, layer=layer, first=first, lo=lo):
-                for r in (lo + 2 * i, lo + 2 * i + 1):
+                for q in range(2):
+                    r = lo + 2 * i + q
                     cosr[layer * EXT + first + r] = spread(cos_n, layer * ROWS + r)
                     sinr[layer * EXT + first + r] = spread(sin_n, layer * ROWS + r)
                 return 0
 
-            lax.fori_loop(0, (hi - lo) // 2, body, 0)
+            lax.fori_loop(0, count // 2, body, 0)
     for layer in range(LAYERS):
         def copy(r, _, layer=layer):
             cosr[layer * EXT + HALO + r] = cos_own[layer * ROWS + r]
@@ -276,8 +291,8 @@
     step(row, v, EXT, HALO, 4, (l1, l2, l3), rate_scale, write_last)
     for r in range(4):
         for k in range(2):
-            last_low[r, k] = w2[HALO + r, k, 8:136, :]
-            last_high[r, k] = w2[HALO + 4 + r, k, 8:136, :]
+            last_e[r, k] = w2[HALO + r + 4 * (1 - odd), k, 8:136, :]
+            last_o[r, k] = w2[HALO + r + 4 * odd, k, 8:136, :]
 
     def term(layer, adjoint, stored):
         def body(i, _):
@@ -329,32 +344,44 @@
 
 def deal_kernel(mine, out):
     for t in range(TILES):
-        x = mine[:, 128 * t:128 * (t + 1)]
-        out[t // 2, t % 2] = x
-        out[PLANE + t // 2, t % 2] = x
-
-
-def pick_kernel(order, got, out):
+        out[t // 2, t % 2] = mine[:, 128 * t:128 * (t + 1)]
+
+
+def pick_kernel(ids, order, got, out):
     for layer in range(LAYERS):
+        held = (order[layer] >> 4) == ids[1]
         for t in range(2):
-            x = got[order[layer], t]
-            for d in range(PLANE):
-                out[d, t, layer] = x
-
-
-def gather_kernel(order, parts, out):
-    out[...] = jnp.zeros_like(out)
+            x = got[order[layer] & (PLANE - 1), t]
+            out[t, layer] = jnp.where(held, x, jnp.zeros_like(x))
+
+
+def copies_kernel(mine, other, out):
+    x = mine[...] + other[...]
+    for d in range(PLANE):
+        out[d] = x
+
+
+def sum_kernel(parts, out):
     for layer in range(LAYERS):
         for t in range(2):
             x = [parts[d, t, layer] for d in range(PLANE)]
             while len(x) > 1:
                 x = [a + b for a, b in zip(x[::2], x[1::2])]
-            out[order[layer], t] = x[0]
+            out[t, layer] = x[0]
+
+
+def address_kernel(ids, order, mine, other, out):
+    out[...] = jnp.zeros_like(out)
+    for layer in range(LAYERS):
+        @pl.when((order[layer] >> 4) == ids[1])
+        def _(layer=layer):
+            for t in range(2):
+                out[order[layer] & (PLANE - 1), t] = mine[t, layer] + other[t, layer]
 
 
 def finish_kernel(got, out):
     for t in range(TILES):
-        out[:, 128 * t:128 * (t + 1)] = got[t // 2, t % 2] + got[PLANE + t // 2, t % 2]
+        out[:, 128 * t:128 * (t + 1)] = got[t // 2, t % 2]
 
 
 def vm():
@@ -391,58 +418,72 @@
 
 
 def forward_and_back(angles, depth_order, slices, cotangent):
-    row = lax.axis_index("row").astype(jnp.int32).reshape(1)
     n_row = lax.axis_size("row")
+    group = lax.axis_index("illum") // PLANE
+    ids = jnp.stack([lax.axis_index("row"), group]).astype(jnp.int32)
     groups = [list(range(g * PLANE, (g + 1) * PLANE)) for g in range(2)]
-
-    def to_next(x, by):
-        return lax.ppermute(x, "row", [(i, i + by) for i in range(n_row - by)])
-
-    def to_prev(x, by):
-        return lax.ppermute(x, "row", [(i + by, i) for i in range(n_row - by)])
-
-    def exchange(x, groups=None):
+    swap = [(i, (i + PLANE) % (2 * PLANE)) for i in range(2 * PLANE)]
+
+    def meet(x_e, x_o, by):
+        even = [(i, i ^ by) for i in range(n_row)]
+        odd = [(i, i + by) for i in range(by, n_row - by) if i & by]
+        odd = odd + [(j, i) for i, j in odd]
+        got_o = lax.ppermute(x_o, "row", odd)
+        got_e = lax.ppermute(x_e, "row", even)
+        return got_e, got_o
+
+    def exchange(x):
         flat = x.reshape(-1, 128)
         flat = lax.all_to_all(flat, "illum", 0, 0, axis_index_groups=groups, tiled=True)
         return flat.reshape(x.shape)
 
-    dealt = call(deal_kernel, [vm()], shape(2 * PLANE, 2, ROWS, 128), [], 4)(slices[0])
+    def rows_first(x):
+        return x.reshape(8, ROWS, TILES, 128).transpose(0, 2, 1, 3).reshape(-1, 128)
+
+    cot_e, cot_o = meet(cotangent, cotangent, 1)
+    dealt = call(deal_kernel, [vm()], shape(PLANE, 2, ROWS, 128), [], 4)(slices[0])
     got = exchange(dealt)
-    cot = cotangent.reshape(8, ROWS, TILES, 128).transpose(0, 2, 1, 3).reshape(-1, 128)
-    own, low, high = call(
-        split_kernel, [vm()], (field(8), field(4), field(4)), [], 6)(cot)
-    top, bot = to_next(own, 1), to_prev(own, 1)
-    top2, bot2 = to_next(high, 2), to_prev(low, 2)
-    piece = call(pick_kernel, [sm(), vm()], shape(PLANE, 2, LAYERS, ROWS, 128), [],
-                 4)(depth_order, got)
-    phases = exchange(piece, groups).reshape(-1, 128)
-    ph_top, ph_bot = to_next(phases, 1), to_prev(phases, 1)
+    own, send_e, send_o = call(
+        split_kernel, [sm(), vm()], (field(8), field(4), field(4)), [], 6)(
+            ids, rows_first(cotangent))
+    piece = call(pick_kernel, [sm(), sm(), vm()], shape(2, LAYERS, ROWS, 128), [],
+                 2)(ids, depth_order, got)
+    piece_z = lax.ppermute(piece, "illum", swap)
+    far_e, far_o = meet(send_e, send_o, 2)
+    halo_e, halo_o = call(halo_kernel, [vm()] * 2, (field(8),) * 2, [], 6)(
+        rows_first(cot_e), rows_first(cot_o))
+    whole = call(copies_kernel, [vm()] * 2, shape(PLANE, 2, LAYERS, ROWS, 128), [],
+                 2)(piece, piece_z)
+    phases = exchange(whole).reshape(-1, 128)
+    ph_e, ph_o = meet(phases, phases, 1)
 
     table = scr(TILES * LAYERS * ROWS, 128)
     cos_own, sin_own = call(
         phase_kernel, [vm()], (shape(LAYERS * ROWS, 128, 128),) * 2, [table] * 2,
         5)(phases)
     w1 = call(adjoint_kernel, [sm()] + [vm()] * 5, field(EXT), [wide(32)] * 4,
-              20)(row, own, top, bot, top2, bot2)
+              20)(ids, own, halo_e, halo_o, far_e, far_o)
 
     pv = jnp.broadcast_to(jnp.repeat(angles[:, 0], TILES)[None], (8, 128))
     qv = jnp.broadcast_to(jnp.repeat(angles[:, 1], TILES)[None], (8, 128))
     spreads = scr(LAYERS * EXT, 128, 128)
-    terms, last_low, last_high = call(
+    terms, last_e, last_o = call(
         main_kernel, [sm()] + [vm()] * 7,
         (shape(TILES * LAYERS * ROWS, 128), field(4), field(4)),
         [table, table, spreads, spreads, scr(2, 128, 128)] + [wide(EXT)] * 4
         + [scr(16, 2, 128, 128)] + [wide(EXT)] * 3, 40)(
-            row, pv, qv, ph_top, ph_bot, cos_own, sin_own, w1)
-    r_top, r_bot = to_next(last_high, 1), to_prev(last_low, 1)
-    parts = exchange(terms, groups).reshape(PLANE, 2, LAYERS, ROWS, 128)
-    send = call(gather_kernel, [sm(), vm()], shape(2 * PLANE, 2, ROWS, 128), [],
-                4)(depth_order, parts)
+            ids, pv, qv, ph_e, ph_o, cos_own, sin_own, w1)
+    parts = exchange(terms).reshape(PLANE, 2, LAYERS, ROWS, 128)
+    half = call(sum_kernel, [vm()], shape(2, LAYERS, ROWS, 128), [], 2)(parts)
+    half_z = lax.ppermute(half, "illum", swap)
+    r_e, r_o = meet(last_e, last_o, 1)
+    send = call(address_kernel, [sm(), sm()] + [vm()] * 2, shape(PLANE, 2, ROWS, 128), [],
+                2)(ids, depth_order, half, half_z)
     back = exchange(send)
     out = call(exit_kernel, [sm()] + [vm()] * 4, shape(2048, 128),
                [wide(16)] * 4 + [scr(8, 2, 128, 128)], 12)(
-                   row, last_low, last_high, r_top, r_bot)
-    grad = call(finish_kernel, [vm()], shape(ROWS, COLS), [], 4)(back)
+                   ids, last_e, last_o, r_e, r_o)
+    grad = call(finish_kernel, [vm()], shape(ROWS, COLS), [], 2)(back)
     out = out.reshape(8, TILES, ROWS, 128).transpose(0, 2, 1, 3)
     return out.reshape(cotangent.shape), grad[None]
 

time: 122 us -> 125 us (1.025)
  blocking collectives: 0 us -> 29.1 us
  starting transfers between devices: 51.7 us -> 35.1 us
  waiting for transfers between devices: 28.1 us -> 17 us
  Pallas kernels: 36.8 us -> 38.4 us
    all_to_all x0 -> x2, blocking collectives: none -> 29.1 us  [exchange(): lax.all_to_all(flat, 'illum', 0, 0, axis_index_groups=groups, tiled=True)]
    all_to_all x4 -> x2, starting transfers between devices: 32.1 us -> 10.6 us  [exchange(): lax.all_to_all(flat, 'illum', 0, 0, axis_index_groups=groups, tiled=True)]
    all_to_all x4 -> x2, waiting for transfers between devices: 28.1 us -> 9.48 us  [exchange(): lax.all_to_all(flat, 'illum', 0, 0, axis_index_groups=groups, tiled=True)]
    ppermute x8 -> x10, waiting for transfers between devices: 0.02 us -> 7.54 us  [the longest x1 3.03 us: forward_and_back(): half_z = lax.ppermute(half, 'illum', swap)]
    ppermute x8 -> x10, starting transfers between devices: 19.6 us -> 24.5 us  [the longest x4 9.38 us: meet(): got_o = lax.ppermute(x_o, 'row', odd)]
    pallas_call x5 -> x8, Pallas kernels: 5.71 us -> 7.34 us  [the longest x1 2.44 us: forward_and_back(): call(split_kernel, [sm(), vm()], (field(8), field(4), field(4)), [], 6)]
    unnamed x10 -> x14, local copies, waits for them, and re-layouts: 2.94 us -> 2.55 us
  transfers between devices with their start and end apart: 12 -> 12, of which waited for: 4 -> 5; matrix products, arithmetic and copies ran while one was open for 0% -> 0% of each run, Pallas kernels for 13% -> 12%
where the time goes in v4:
time: 125 us; the launch traced here: 123 us
  Pallas kernels  38.4 us (31%)
  starting transfers between devices  35.1 us (28%)
  blocking collectives  29.1 us (23%)
  waiting for transfers between devices  17 us (14%)
  local copies, waits for them, and re-layouts  2.87 us (2%)
    all_to_all x2, blocking collectives, exchange(): lax.all_to_all(flat, 'illum', 0, 0, axis_index_groups=groups, tiled=True)  29.1 us
    pallas_call x1, Pallas kernels, forward_and_back(): call(main_kernel, [sm()] + [vm()] * 7, (shape(TILES * LAYERS * ROWS, 128)...  18.8 us
    all_to_all x2, starting transfers between devices, exchange(): lax.all_to_all(flat, 'illum', 0, 0, axis_index_groups=groups, tiled=True)  10.6 us
    all_to_all x2, waiting for transfers between devices, exchange(): lax.all_to_all(flat, 'illum', 0, 0, axis_index_groups=groups, tiled=True)  9.48 us
    ppermute x4, starting transfers between devices, meet(): got_o = lax.ppermute(x_o, 'row', odd)  9.38 us
    pallas_call x1, Pallas kernels, forward_and_back(): call(adjoint_kernel, [sm()] + [vm()] * 5, field(EXT), [wide(32)] * 4, 20)  5.7 us
    ppermute x1, starting transfers between devices, forward_and_back(): piece_z = lax.ppermute(piece, 'illum', swap)  5.48 us
    ppermute x4, starting transfers between devices, meet(): got_e = lax.ppermute(x_e, 'row', even)  4.8 us
  transfers between devices with their start and end apart: 12, of which 5 were waited for; matrix products, arithmetic and copies ran while one was open for 0% of the time, Pallas kernels for 12%

profile of v4, /device:TPU:32, one launch (start us, length us, event | category | flops | bytes accessed | tf_op | source)
XLA Modules:
  0.0 123.4 jit_solution(365894768159415994)
XLA Ops:
  0.6 0.0 copy-start
  0.6 2.1 %collective-permute-start.4 = (f32[4,2,8,4096]{3,2,1,0:T(8,128)}, f32[4,2,8,4096]{3,2,1,0:T(8,128)S(1)}, u32[]{:S(2)}, u32[]{:S(2)}) collective-permute-start(f32[4,2,8,4096]{3,2,1,0:T(8,128)} %param.7), channel_id=1, source_target_pairs={{1,2},{3,4},{5,6},{2,1},{4,3},{6,5},{9,10},{11,12},{13,14},{10,9},... | collective-permute-start | bytes 3145736 | tf_op jit(solution)/shard_map/ppermute | solution.py:431
  2.7 2.1 %collective-permute-start.3 = (f32[4,2,8,4096]{3,2,1,0:T(8,128)}, f32[4,2,8,4096]{3,2,1,0:T(8,128)S(1)}, u32[]{:S(2)}, u32[]{:S(2)}) collective-permute-start(f32[4,2,8,4096]{3,2,1,0:T(8,128)} %param.7), channel_id=1, source_target_pairs={{0,1},{1,0},{2,3},{3,2},{4,5},{5,4},{6,7},{7,6},{8,9},{9,8},{10,11... | collective-permute-start | bytes 3145736 | tf_op jit(solution)/shard_map/ppermute | solution.py:432
  4.8 0.9 copy-done.3
  5.7 0.7 shard_map.59
  6.4 7.0 %all-to-all-start = ((f32[16,16,128]{2,1,0:T(8,128)}), f32[16,16,128]{2,1,0:T(8,128)S(1)}, u32[]{:S(2)}, u32[]{:S(2)}) async-start(f32[16,16,128]{2,1,0:T(8,128)} %bitcast.5), calls=%async_computation | async-start | bytes 262144 | tf_op jit(solution)/shard_map/all_to_all | solution.py:437
  13.4 0.1 pad_add_fusion.ids
  13.5 7.8 %all-to-all-done = f32[16,16,128]{2,1,0:T(8,128)S(1)} async-done(((f32[16,16,128]{2,1,0:T(8,128)}), f32[16,16,128]{2,1,0:T(8,128)S(1)}, u32[]{:S(2)}, u32[]{:S(2)}) %all-to-all-start) | async-done | bytes 131104 | tf_op jit(solution)/shard_map/all_to_all | solution.py:437
  21.3 0.7 copy-done.4
  21.9 0.6 shard_map.60.mine
  22.5 5.5 %collective-permute-start = (f32[2,3,8,128]{3,2,1,0:T(8,128)S(1)}, f32[2,3,8,128]{3,2,1,0:T(8,128)S(1)}, u32[]{:S(2)}, u32[]{:S(2)}) collective-permute-start(f32[2,3,8,128]{3,2,1,0:T(8,128)S(1)} %shard_map.60.mine), channel_id=1, source_target_pairs={{0,128},{8,136},{16,144},{24,152},{32,160},{40,168},{48,176},{56,1... | collective-permute-start | bytes 73736 | tf_op jit(solution)/shard_map/ppermute | solution.py:451
  28.0 2.3 %collective-permute-done.other = f32[2,3,8,128]{3,2,1,0:T(8,128)S(1)} collective-permute-done((f32[2,3,8,128]{3,2,1,0:T(8,128)S(1)}, f32[2,3,8,128]{3,2,1,0:T(8,128)S(1)}, u32[]{:S(2)}, u32[]{:S(2)}) %collective-permute-start) | collective-permute-done | bytes 24608 | tf_op jit(solution)/shard_map/ppermute | solution.py:451
  30.3 0.8 shard_map.61
  31.1 3.6 %all-to-all-start.1 = ((f32[16,48,128]{2,1,0:T(8,128)}), f32[16,48,128]{2,1,0:T(8,128)S(1)}, u32[]{:S(2)}, u32[]{:S(2)}) async-start(f32[16,48,128]{2,1,0:T(8,128)} %bitcast.7), calls=%async_computation.1 | async-start | bytes 786432 | tf_op jit(solution)/shard_map/all_to_all | solution.py:437
  34.7 0.0 copy-done
  34.7 2.4 %shard_map.63 = (f32[8,2,128,128]{3,2,1,0:T(8,128)S(1)}, f32[4,2,128,128]{3,2,1,0:T(8,128)}, f32[4,2,128,128]{3,2,1,0:T(8,128)}) custom-call(s32[2]{0:T(128)S(1)} %pad_add_fusion.ids, f32[2048,128]{1,0:T(8,128)S(1)} %bitcast.40), custom_call_target="tpu_custom_call" | custom-call | flops 20000000 | bytes 4194304 | tf_op jit(solution)/shard_map/pallas_call | solution.py:446
  37.1 1.0 copy-done.1
  38.1 0.5 collective-permute-start.5
  38.6 3.5 %collective-permute-start.6 = (f32[4,2,128,128]{3,2,1,0:T(8,128)}, f32[4,2,128,128]{3,2,1,0:T(8,128)}, u32[]{:S(2)}, u32[]{:S(2)}) collective-permute-start(f32[4,2,128,128]{3,2,1,0:T(8,128)} %get-tuple-element.18), channel_id=1, source_target_pairs={{2,4},{3,5},{4,2},{5,3},{10,12},{11,13},{12,10},{13,11},{18,20},{1... | collective-permute-start | bytes 1572872 | tf_op jit(solution)/shard_map/ppermute | solution.py:431
  42.1 1.7 %all-to-all-done.1 = f32[16,48,128]{2,1,0:T(8,128)S(1)} async-done(((f32[16,48,128]{2,1,0:T(8,128)}), f32[16,48,128]{2,1,0:T(8,128)S(1)}, u32[]{:S(2)}, u32[]{:S(2)}) %all-to-all-start.1) | async-done | bytes 393248 | tf_op jit(solution)/shard_map/all_to_all | solution.py:437
  43.8 1.9 %collective-permute-start.2 = (f32[768,128]{1,0:T(8,128)S(1)}, f32[768,128]{1,0:T(8,128)}, u32[]{:S(2)}, u32[]{:S(2)}) collective-permute-start(f32[768,128]{1,0:T(8,128)S(1)} %bitcast.36), channel_id=1, source_target_pairs={{1,2},{3,4},{5,6},{2,1},{4,3},{6,5},{9,10},{11,12},{13,14},{10,9},... | collective-permute-start | bytes 1179656 | tf_op jit(solution)/shard_map/ppermute | solution.py:431
  45.7 0.0 collective-permute-done.4
  45.7 2.1 %collective-permute-start.1 = (f32[768,128]{1,0:T(8,128)S(1)}, f32[768,128]{1,0:T(8,128)}, u32[]{:S(2)}, u32[]{:S(2)}) collective-permute-start(f32[768,128]{1,0:T(8,128)S(1)} %bitcast.37), channel_id=1, source_target_pairs={{0,1},{1,0},{2,3},{3,2},{4,5},{5,4},{6,7},{7,6},{8,9},{9,8},{10,11... | collective-permute-start | bytes 1179656 | tf_op jit(solution)/shard_map/ppermute | solution.py:432
  47.9 0.1 broadcast_in_dim.26
  48.0 0.1 broadcast_in_dim.27
  48.0 0.1 broadcast_in_dim.23
  48.1 0.1 broadcast_in_dim.24
  48.2 2.2 %shard_map.62 = (f32[24,128,128]{2,1,0:T(8,128)S(1)}, f32[24,128,128]{2,1,0:T(8,128)S(1)}) custom-call(f32[768,128]{1,0:T(8,128)S(1)} %bitcast.38), custom_call_target="tpu_custom_call" | custom-call | flops 20000000 | bytes 4194304 | tf_op jit(solution)/shard_map/pallas_call | solution.py:461
  50.4 0.0 collective-permute-done.3
  50.5 1.6 %shard_map.64 = (f32[8,2,128,128]{3,2,1,0:T(8,128)S(1)}, f32[8,2,128,128]{3,2,1,0:T(8,128)S(1)}) custom-call(f32[2048,128]{1,0:T(8,128)S(1)} %bitcast.42, f32[2048,128]{1,0:T(8,128)S(1)} %bitcast.41), custom_call_target="tpu_custom_call" | custom-call | flops 20000000 | bytes 4194304 | tf_op jit(solution)/shard_map/pallas_call | solution.py:453
  52.1 0.0 collective-permute-done.5.far_e
  52.1 2.2 %collective-permute-done.6.far_o = f32[4,2,128,128]{3,2,1,0:T(8,128)} collective-permute-done((f32[4,2,128,128]{3,2,1,0:T(8,128)}, f32[4,2,128,128]{3,2,1,0:T(8,128)}, u32[]{:S(2)}, u32[]{:S(2)}) %collective-permute-start.6) | collective-permute-done | bytes 524320 | tf_op jit(solution)/shard_map/ppermute | solution.py:431
  54.3 5.7 %shard_map.65.w1 = f32[24,2,128,128]{3,2,1,0:T(8,128)S(1)} custom-call(s32[2]{0:T(128)S(1)} %pad_add_fusion.ids, f32[8,2,128,128]{3,2,1,0:T(8,128)S(1)} %copy-done.2, f32[8,2,128,128]{3,2,1,0:T(8,128)S(1)} %get-tuple-element.15.halo_e, f32[8,2,128,128]{3,2,1,0:T(8,128)S(1)} %get-tuple-element.16.halo_o, f32[4,2,128,128]{3,2,1,0:T(8,128)} %collective-permute-done.5.far_e, ...), custom_call_target="tpu_custom_call" | custom-call | flops 20000000 | bytes 4194304 | tf_op jit(solution)/shard_map/pallas_call | solution.py:464
  60.0 0.0 collective-permute-done.2.ph_o
  60.0 0.0 collective-permute-done.1.ph_e
  60.0 0.0 copy-start.5
  60.0 18.8 %shard_map.66 = (f32[768,128]{1,0:T(8,128)S(1)}, f32[4,2,128,128]{3,2,1,0:T(8,128)S(1)}, f32[4,2,128,128]{3,2,1,0:T(8,128)S(1)}) custom-call(s32[2]{0:T(128)S(1)} %pad_add_fusion.ids, s32[8,128]{1,0:T(8,128)S(1)} %broadcast_in_dim.25.pv, s32[8,128]{1,0:T(8,128)S(1)} %broadcast_in_dim.28.qv, f32[768,128]{1,0:T(8,128)} %collective-permute-done.1.ph_e, ...), custom_call_target="tpu_custom_call" | custom-call | flops 20000000 | bytes 4194304 | tf_op jit(solution)/shard_map/pallas_call | solution.py:470
  78.8 0.1 collective-permute-start.7
  78.9 1.9 %collective-permute-start.8 = (f32[4,2,128,128]{3,2,1,0:T(8,128)S(1)}, f32[4,2,128,128]{3,2,1,0:T(8,128)S(1)}, u32[]{:S(2)}, u32[]{:S(2)}) collective-permute-start(f32[4,2,128,128]{3,2,1,0:T(8,128)S(1)} %get-tuple-element.20.sent_o), channel_id=1, source_target_pairs={{1,2},{3,4},{5,6},{2,1},{4,3},{6,5},{9,10},{11,12},{13,14},{10,9},... | collective-permute-start | bytes 1572872 | tf_op jit(solution)/shard_map/ppermute | solution.py:431
  80.9 16.8 %all_to_all.38 = f32[16,48,128]{2,1,0:T(8,128)S(1)} all-to-all(f32[16,48,128]{2,1,0:T(8,128)S(1)} %bitcast.46), channel_id=1, replica_groups={{0,8,16,24,32,40,48,56,64,72,80,88,96,104,112,120},{128,136,144,152,160..., dimensions={0} | all-to-all | bytes 786432 | tf_op jit(solution)/shard_map/all_to_all | solution.py:437
  97.7 4.8 %collective-permute-start.9 = (f32[2,3,8,128]{3,2,1,0:T(8,128)S(1)}, f32[2,3,8,128]{3,2,1,0:T(8,128)S(1)}, u32[]{:S(2)}, u32[]{:S(2)}) collective-permute-start(f32[2,3,8,128]{3,2,1,0:T(8,128)S(1)} %shard_map.68.mine), channel_id=1, source_target_pairs={{0,128},{8,136},{16,144},{24,152},{32,160},{40,168},{48,176},{56,1... | collective-permute-start | bytes 73736 | tf_op jit(solution)/shard_map/ppermute | solution.py:478
  102.5 3.0 %collective-permute-done.9.other = f32[2,3,8,128]{3,2,1,0:T(8,128)S(1)} collective-permute-done((f32[2,3,8,128]{3,2,1,0:T(8,128)S(1)}, f32[2,3,8,128]{3,2,1,0:T(8,128)S(1)}, u32[]{:S(2)}, u32[]{:S(2)}) %collective-permute-start.9) | collective-permute-done | bytes 24608 | tf_op jit(solution)/shard_map/ppermute | solution.py:478
  105.6 0.6 shard_map.69
  106.1 12.3 %all_to_all.39 = f32[16,16,128]{2,1,0:T(8,128)S(1)} all-to-all(f32[16,16,128]{2,1,0:T(8,128)S(1)} %bitcast.44), channel_id=1, replica_groups={{0,8,16,24,32,40,48,56,64,72,80,88,96,104,112,120},{128,136,144,152,160..., dimensions={0} | all-to-all | bytes 262144 | tf_op jit(solution)/shard_map/all_to_all | solution.py:437
  118.4 0.7 shard_map.70
  119.1 0.0 collective-permute-done.7.got_e
  119.1 0.0 collective-permute-done.8.got_o
  119.1 4.3 %shard_map.67 = f32[2048,128]{1,0:T(8,128)} custom-call(s32[2]{0:T(128)S(1)} %pad_add_fusion.ids, f32[4,2,128,128]{3,2,1,0:T(8,128)S(1)} %get-tuple-element.19.sent_e, f32[4,2,128,128]{3,2,1,0:T(8,128)S(1)} %get-tuple-element.20.sent_o, f32[4,2,128,128]{3,2,1,0:T(8,128)S(1)} %collective-permute-done.7.got_e, f32[4,2,128,128]{3,2,1,0:T(8,128)S(1)} %collective-permute-done.8.got_o), custom_call_target="tpu_custom_call" | custom-call | flops 20000000 | bytes 4194304 | tf_op jit(solution)/shard_map/pallas_call | solution.py:483
  (12 shorter events, 0.0 us)
Async XLA Ops:
  0.6 34.1 %copy-start = (f32[4,2,8,4096]{3,2,1,0:T(8,128)S(1)}, f32[4,2,8,4096]{3,2,1,0:T(8,128)}, u32[]{:S(2)}) copy-start(f32[4,2,8,4096]{3,2,1,0:T(8,128)} %param.7) | copy-start | bytes 3145732
  0.6 45.1 %collective-permute-start.4 = (f32[4,2,8,4096]{3,2,1,0:T(8,128)}, f32[4,2,8,4096]{3,2,1,0:T(8,128)S(1)}, u32[]{:S(2)}, u32[]{:S(2)}) collective-permute-start(f32[4,2,8,4096]{3,2,1,0:T(8,128)} %param.7), channel_id=1, source_target_pairs={{1,2},{3,4},{5,6},{2,1},{4,3},{6,5},{9,10},{11,12},{13,14},{10,9},... | collective-permute-start | bytes 3145736 | tf_op jit(solution)/shard_map/ppermute | solution.py:431
  2.7 47.7 %collective-permute-start.3 = (f32[4,2,8,4096]{3,2,1,0:T(8,128)}, f32[4,2,8,4096]{3,2,1,0:T(8,128)S(1)}, u32[]{:S(2)}, u32[]{:S(2)}) collective-permute-start(f32[4,2,8,4096]{3,2,1,0:T(8,128)} %param.7), channel_id=1, source_target_pairs={{0,1},{1,0},{2,3},{3,2},{4,5},{5,4},{6,7},{7,6},{8,9},{9,8},{10,11... | collective-permute-start | bytes 3145736 | tf_op jit(solution)/shard_map/ppermute | solution.py:432
  4.8 0.9 copy-start.3
  6.4 14.9 %all-to-all-start = ((f32[16,16,128]{2,1,0:T(8,128)}), f32[16,16,128]{2,1,0:T(8,128)S(1)}, u32[]{:S(2)}, u32[]{:S(2)}) async-start(f32[16,16,128]{2,1,0:T(8,128)} %bitcast.5), calls=%async_computation | async-start | bytes 262144 | tf_op jit(solution)/shard_map/all_to_all | solution.py:437
  21.3 0.7 copy-start.4
  21.9 26.0 %copy-start.6 = (s32[4,2]{0,1:T(2,128)S(1)}, s32[4,2]{0,1:T(2,128)}, u32[]{:S(2)}) copy-start(s32[4,2]{0,1:T(2,128)} %param.4) | copy-start | bytes 100
  22.5 7.8 %collective-permute-start = (f32[2,3,8,128]{3,2,1,0:T(8,128)S(1)}, f32[2,3,8,128]{3,2,1,0:T(8,128)S(1)}, u32[]{:S(2)}, u32[]{:S(2)}) collective-permute-start(f32[2,3,8,128]{3,2,1,0:T(8,128)S(1)} %shard_map.60.mine), channel_id=1, source_target_pairs={{0,128},{8,136},{16,144},{24,152},{32,160},{40,168},{48,176},{56,1... | collective-permute-start | bytes 73736 | tf_op jit(solution)/shard_map/ppermute | solution.py:451
  31.1 12.7 %all-to-all-start.1 = ((f32[16,48,128]{2,1,0:T(8,128)}), f32[16,48,128]{2,1,0:T(8,128)S(1)}, u32[]{:S(2)}, u32[]{:S(2)}) async-start(f32[16,48,128]{2,1,0:T(8,128)} %bitcast.7), calls=%async_computation.1 | async-start | bytes 786432 | tf_op jit(solution)/shard_map/all_to_all | solution.py:437
  37.1 1.0 copy-start.1
  38.1 16.2 %copy-start.2 = (f32[8,2,128,128]{3,2,1,0:T(8,128)S(1)}, f32[8,2,128,128]{3,2,1,0:T(8,128)}, u32[]{:S(2)}) copy-start(f32[8,2,128,128]{3,2,1,0:T(8,128)} %copy-done.1) | copy-start | bytes 3145732
  38.1 14.0 %collective-permute-start.5 = (f32[4,2,128,128]{3,2,1,0:T(8,128)}, f32[4,2,128,128]{3,2,1,0:T(8,128)}, u32[]{:S(2)}, u32[]{:S(2)}) collective-permute-start(f32[4,2,128,128]{3,2,1,0:T(8,128)} %get-tuple-element.17), channel_id=1, source_target_pairs={{0,2},{1,3},{2,0},{3,1},{4,6},{5,7},{6,4},{7,5},{8,10},{9,11},{10,... | collective-permute-start | bytes 1572872 | tf_op jit(solution)/shard_map/ppermute | solution.py:432
  38.6 15.7 %collective-permute-start.6 = (f32[4,2,128,128]{3,2,1,0:T(8,128)}, f32[4,2,128,128]{3,2,1,0:T(8,128)}, u32[]{:S(2)}, u32[]{:S(2)}) collective-permute-start(f32[4,2,128,128]{3,2,1,0:T(8,128)} %get-tuple-element.18), channel_id=1, source_target_pairs={{2,4},{3,5},{4,2},{5,3},{10,12},{11,13},{12,10},{13,11},{18,20},{1... | collective-permute-start | bytes 1572872 | tf_op jit(solution)/shard_map/ppermute | solution.py:431
  43.8 16.2 %collective-permute-start.2 = (f32[768,128]{1,0:T(8,128)S(1)}, f32[768,128]{1,0:T(8,128)}, u32[]{:S(2)}, u32[]{:S(2)}) collective-permute-start(f32[768,128]{1,0:T(8,128)S(1)} %bitcast.36), channel_id=1, source_target_pairs={{1,2},{3,4},{5,6},{2,1},{4,3},{6,5},{9,10},{11,12},{13,14},{10,9},... | collective-permute-start | bytes 1179656 | tf_op jit(solution)/shard_map/ppermute | solution.py:431
  45.7 14.2 %collective-permute-start.1 = (f32[768,128]{1,0:T(8,128)S(1)}, f32[768,128]{1,0:T(8,128)}, u32[]{:S(2)}, u32[]{:S(2)}) collective-permute-start(f32[768,128]{1,0:T(8,128)S(1)} %bitcast.37), channel_id=1, source_target_pairs={{0,1},{1,0},{2,3},{3,2},{4,5},{5,4},{6,7},{7,6},{8,9},{9,8},{10,11... | collective-permute-start | bytes 1179656 | tf_op jit(solution)/shard_map/ppermute | solution.py:432
  60.0 45.5 %copy-start.5 = (s32[3]{0:T(128)S(1)}, s32[3]{0:T(128)}, u32[]{:S(2)}) copy-start(s32[3]{0:T(128)} %order.3) | copy-start | bytes 40
  78.8 40.3 %collective-permute-start.7 = (f32[4,2,128,128]{3,2,1,0:T(8,128)S(1)}, f32[4,2,128,128]{3,2,1,0:T(8,128)S(1)}, u32[]{:S(2)}, u32[]{:S(2)}) collective-permute-start(f32[4,2,128,128]{3,2,1,0:T(8,128)S(1)} %get-tuple-element.19.sent_e), channel_id=1, source_target_pairs={{0,1},{1,0},{2,3},{3,2},{4,5},{5,4},{6,7},{7,6},{8,9},{9,8},{10,11... | collective-permute-start | bytes 1572872 | tf_op jit(solution)/shard_map/ppermute | solution.py:432
  78.9 40.2 %collective-permute-start.8 = (f32[4,2,128,128]{3,2,1,0:T(8,128)S(1)}, f32[4,2,128,128]{3,2,1,0:T(8,128)S(1)}, u32[]{:S(2)}, u32[]{:S(2)}) collective-permute-start(f32[4,2,128,128]{3,2,1,0:T(8,128)S(1)} %get-tuple-element.20.sent_o), channel_id=1, source_target_pairs={{1,2},{3,4},{5,6},{2,1},{4,3},{6,5},{9,10},{11,12},{13,14},{10,9},... | collective-permute-start | bytes 1572872 | tf_op jit(solution)/shard_map/ppermute | solution.py:431
  97.7 7.8 %collective-permute-start.9 = (f32[2,3,8,128]{3,2,1,0:T(8,128)S(1)}, f32[2,3,8,128]{3,2,1,0:T(8,128)S(1)}, u32[]{:S(2)}, u32[]{:S(2)}) collective-permute-start(f32[2,3,8,128]{3,2,1,0:T(8,128)S(1)} %shard_map.68.mine), channel_id=1, source_target_pairs={{0,128},{8,136},{16,144},{24,152},{32,160},{40,168},{48,176},{56,1... | collective-permute-start | bytes 73736 | tf_op jit(solution)/shard_map/ppermute | solution.py:478

commit v5 on v4

--- a/solution.py
+++ b/solution.py
@@ -219,7 +219,7 @@
     lax.fori_loop(0, LAYERS * ROWS // 2, body, 0)
 
 
-def main_kernel(ids, pv, qv, ph_e, ph_o, cos_own, sin_own, w1,
+def main_kernel(ids, angles, ph_e, ph_o, cos_own, sin_own, w1,
                 terms, last_e, last_o,
                 cos_n, sin_n, cosr, sinr, beam, u, v, w, w2, raw, l1, l2, l3):
     row = ids[0]
@@ -248,9 +248,16 @@
 
     lane = lax.broadcasted_iota(jnp.int32, (8, 128), 1)
     sub = lax.broadcasted_iota(jnp.int32, (8, 128), 0)
+    beam_of = lane >> 5
+    pv, qv = [
+        jnp.where(beam_of < 2,
+                  jnp.where(beam_of == 0, angles[0, n], angles[1, n]),
+                  jnp.where(beam_of == 2, angles[2, n], angles[3, n]))
+        for n in range(2)
+    ]
     for j in range(16):
         col = (lane & (TILES - 1)) * 128 + sub + 8 * j
-        k = (qv[...] * col) & (COLS - 1)
+        k = (qv * col) & (COLS - 1)
         s, c = sincos((k - COLS // 2).astype(jnp.float32) * (2.0 * math.pi / COLS))
         beam[0, chunk(j), :] = -c
         beam[1, chunk(j), :] = -s
@@ -259,7 +266,7 @@
         return cosr[layer * EXT + r, chunk(j), :], sinr[layer * EXT + r, chunk(j), :]
 
     def incident(r, _):
-        k = (pv[...] * (row * ROWS + r - HALO)) & (NX - 1)
+        k = (pv * (row * ROWS + r - HALO)) & (NX - 1)
         sa, ca = sincos((k - NX // 2).astype(jnp.float32) * (2.0 * math.pi / NX))
         for j in range(16):
             c, s = phase_at(0, r, j)
@@ -342,23 +349,18 @@
     term(0, lambda r, k: raw[r + 4, k], own(u))
 
 
-def deal_kernel(mine, out):
+def deal_kernel(mine, other, out):
     for t in range(TILES):
-        out[t // 2, t % 2] = mine[:, 128 * t:128 * (t + 1)]
+        out[t // 2, 0, t % 2] = mine[t]
+        out[t // 2, 1, t % 2] = other[t]
 
 
 def pick_kernel(ids, order, got, out):
     for layer in range(LAYERS):
-        held = (order[layer] >> 4) == ids[1]
         for t in range(2):
-            x = got[order[layer] & (PLANE - 1), t]
-            out[t, layer] = jnp.where(held, x, jnp.zeros_like(x))
-
-
-def copies_kernel(mine, other, out):
-    x = mine[...] + other[...]
-    for d in range(PLANE):
-        out[d] = x
+            x = got[order[layer] & (PLANE - 1), (order[layer] >> 4) ^ ids[1], t]
+            for d in range(PLANE):
+                out[d, t, layer] = x
 
 
 def sum_kernel(parts, out):
@@ -440,39 +442,36 @@
     def rows_first(x):
         return x.reshape(8, ROWS, TILES, 128).transpose(0, 2, 1, 3).reshape(-1, 128)
 
+    mine = slices[0].reshape(ROWS, TILES, 128).transpose(1, 0, 2)
+    other = lax.ppermute(mine, "illum", swap)
     cot_e, cot_o = meet(cotangent, cotangent, 1)
-    dealt = call(deal_kernel, [vm()], shape(PLANE, 2, ROWS, 128), [], 4)(slices[0])
-    got = exchange(dealt)
     own, send_e, send_o = call(
         split_kernel, [sm(), vm()], (field(8), field(4), field(4)), [], 6)(
             ids, rows_first(cotangent))
-    piece = call(pick_kernel, [sm(), sm(), vm()], shape(2, LAYERS, ROWS, 128), [],
-                 2)(ids, depth_order, got)
-    piece_z = lax.ppermute(piece, "illum", swap)
     far_e, far_o = meet(send_e, send_o, 2)
+    dealt = call(deal_kernel, [vm()] * 2, shape(PLANE, 2, 2, ROWS, 128), [], 2)(
+        mine, other)
+    got = exchange(dealt)
     halo_e, halo_o = call(halo_kernel, [vm()] * 2, (field(8),) * 2, [], 6)(
         rows_first(cot_e), rows_first(cot_o))
-    whole = call(copies_kernel, [vm()] * 2, shape(PLANE, 2, LAYERS, ROWS, 128), [],
-                 2)(piece, piece_z)
+    whole = call(pick_kernel, [sm(), sm(), vm()], shape(PLANE, 2, LAYERS, ROWS, 128), [],
+                 2)(ids, depth_order, got)
     phases = exchange(whole).reshape(-1, 128)
     ph_e, ph_o = meet(phases, phases, 1)
 
     table = scr(TILES * LAYERS * ROWS, 128)
+    w1 = call(adjoint_kernel, [sm()] + [vm()] * 5, field(EXT), [wide(32)] * 4,
+              20)(ids, own, halo_e, halo_o, far_e, far_o)
     cos_own, sin_own = call(
         phase_kernel, [vm()], (shape(LAYERS * ROWS, 128, 128),) * 2, [table] * 2,
         5)(phases)
-    w1 = call(adjoint_kernel, [sm()] + [vm()] * 5, field(EXT), [wide(32)] * 4,
-              20)(ids, own, halo_e, halo_o, far_e, far_o)
-
-    pv = jnp.broadcast_to(jnp.repeat(angles[:, 0], TILES)[None], (8, 128))
-    qv = jnp.broadcast_to(jnp.repeat(angles[:, 1], TILES)[None], (8, 128))
     spreads = scr(LAYERS * EXT, 128, 128)
     terms, last_e, last_o = call(
-        main_kernel, [sm()] + [vm()] * 7,
+        main_kernel, [sm()] * 2 + [vm()] * 5,
         (shape(TILES * LAYERS * ROWS, 128), field(4), field(4)),
         [table, table, spreads, spreads, scr(2, 128, 128)] + [wide(EXT)] * 4
         + [scr(16, 2, 128, 128)] + [wide(EXT)] * 3, 40)(
-            ids, pv, qv, ph_e, ph_o, cos_own, sin_own, w1)
+            ids, angles, ph_e, ph_o, cos_own, sin_own, w1)
     parts = exchange(terms).reshape(PLANE, 2, LAYERS, ROWS, 128)
     half = call(sum_kernel, [vm()], shape(2, LAYERS, ROWS, 128), [], 2)(parts)
     half_z = lax.ppermute(half, "illum", swap)

time: 125 us -> 139 us (1.11)
  waiting for transfers between devices: 17 us -> 39.2 us
  starting transfers between devices: 35.1 us -> 28.5 us
    ppermute x1, waiting for transfers between devices: 2.34 us -> 16.4 us  [forward_and_back(): other = lax.ppermute(mine, 'illum', swap)]
    ppermute x4, starting transfers between devices: 4.8 us -> 0.6 us  [meet(): got_e = lax.ppermute(x_e, 'row', even)]
    ppermute x1, waiting for transfers between devices: 3.03 us -> 6.7 us  [forward_and_back(): half_z = lax.ppermute(half, 'illum', swap)]
    ppermute x1, starting transfers between devices: 4.79 us -> 1.12 us  [forward_and_back(): half_z = lax.ppermute(half, 'illum', swap)]
    all_to_all x2, waiting for transfers between devices: 9.48 us -> 12.1 us  [exchange(): lax.all_to_all(flat, 'illum', 0, 0, axis_index_groups=groups, tiled=True)]
    ppermute x4, waiting for transfers between devices: 2.16 us -> 3.98 us  [meet(): got_o = lax.ppermute(x_o, 'row', odd)]
    pallas_call x4 -> x3, Pallas kernels: 20.8 us -> 20 us  [the longest x1 18.6 us: forward_and_back(): call(main_kernel, [sm()] * 2 + [vm()] * 5, (shape(TILES * LAYERS * ROWS,...]
    unnamed x14 -> x17, local copies, waits for them, and re-layouts: 2.55 us -> 3.34 us
  transfers between devices with their start and end apart: 12 -> 12, of which waited for: 5 -> 5; matrix products, arithmetic and copies ran while one was open for 0% -> 0% of each run, Pallas kernels for 12% -> 11%
where the time goes in v5:
time: 139 us; the launch traced here: 138 us
  waiting for transfers between devices  39.2 us (28%)
  Pallas kernels  37.6 us (27%)
  blocking collectives  28.7 us (21%)
  starting transfers between devices  28.5 us (21%)
  local copies, waits for them, and re-layouts  3.34 us (2%)
    all_to_all x2, blocking collectives, exchange(): lax.all_to_all(flat, 'illum', 0, 0, axis_index_groups=groups, tiled=True)  28.7 us
    pallas_call x1, Pallas kernels, forward_and_back(): call(main_kernel, [sm()] * 2 + [vm()] * 5, (shape(TILES * LAYERS * ROWS,...  18.6 us
    ppermute x1, waiting for transfers between devices, forward_and_back(): other = lax.ppermute(mine, 'illum', swap)  16.4 us
    all_to_all x2, waiting for transfers between devices, exchange(): lax.all_to_all(flat, 'illum', 0, 0, axis_index_groups=groups, tiled=True)  12.1 us
    all_to_all x2, starting transfers between devices, exchange(): lax.all_to_all(flat, 'illum', 0, 0, axis_index_groups=groups, tiled=True)  11 us
    ppermute x4, starting transfers between devices, meet(): got_o = lax.ppermute(x_o, 'row', odd)  8.99 us
    ppermute x1, starting transfers between devices, forward_and_back(): other = lax.ppermute(mine, 'illum', swap)  6.81 us
    ppermute x1, waiting for transfers between devices, forward_and_back(): half_z = lax.ppermute(half, 'illum', swap)  6.7 us
  transfers between devices with their start and end apart: 12, of which 5 were waited for; matrix products, arithmetic and copies ran while one was open for 0% of the time, Pallas kernels for 11%

profile of v5, /device:TPU:32, one launch (start us, length us, event | category | flops | bytes accessed | tf_op | source)
XLA Modules:
  0.0 138.3 jit_solution(15008930259881984673)
XLA Ops:
  0.6 0.0 copy-start
  0.6 2.1 %collective-permute-start.4 = (f32[4,2,8,4096]{3,2,1,0:T(8,128)}, f32[4,2,8,4096]{3,2,1,0:T(8,128)S(1)}, u32[]{:S(2)}, u32[]{:S(2)}) collective-permute-start(f32[4,2,8,4096]{3,2,1,0:T(8,128)} %param.7), channel_id=1, source_target_pairs={{1,2},{3,4},{5,6},{2,1},{4,3},{6,5},{9,10},{11,12},{13,14},{10,9},... | collective-permute-start | bytes 3145736 | tf_op jit(solution)/shard_map/ppermute | solution.py:433
  2.7 6.8 %collective-permute-start = (f32[32,8,128]{2,1,0:T(8,128)}, f32[32,8,128]{2,1,0:T(8,128)S(1)}, u32[]{:S(2)}, u32[]{:S(2)}) collective-permute-start(f32[32,8,128]{2,1,0:T(8,128)} %bitcast.46), channel_id=1, source_target_pairs={{0,128},{8,136},{16,144},{24,152},{32,160},{40,168},{48,176},{56,1... | collective-permute-start | bytes 393224 | tf_op jit(solution)/shard_map/ppermute | solution.py:446
  9.5 0.4 collective-permute-start.3
  9.9 16.4 %collective-permute-done.other = f32[32,8,128]{2,1,0:T(8,128)S(1)} collective-permute-done((f32[32,8,128]{2,1,0:T(8,128)}, f32[32,8,128]{2,1,0:T(8,128)S(1)}, u32[]{:S(2)}, u32[]{:S(2)}) %collective-permute-start) | collective-permute-done | bytes 131104 | tf_op jit(solution)/shard_map/ppermute | solution.py:446
  26.3 0.9 copy-done.4
  27.2 0.0 copy-start.1
  27.2 0.7 copy-done.1
  27.9 7.2 %all-to-all-start = ((f32[16,32,128]{2,1,0:T(8,128)}), f32[16,32,128]{2,1,0:T(8,128)S(1)}, u32[]{:S(2)}, u32[]{:S(2)}) async-start(f32[16,32,128]{2,1,0:T(8,128)} %bitcast.42), calls=%async_computation | async-start | bytes 524288 | tf_op jit(solution)/shard_map/all_to_all | solution.py:439
  35.1 0.1 pad_add_fusion.ids
  35.2 9.6 %all-to-all-done = f32[16,32,128]{2,1,0:T(8,128)S(1)} async-done(((f32[16,32,128]{2,1,0:T(8,128)}), f32[16,32,128]{2,1,0:T(8,128)S(1)}, u32[]{:S(2)}, u32[]{:S(2)}) %all-to-all-start) | async-done | bytes 262176 | tf_op jit(solution)/shard_map/all_to_all | solution.py:439
  44.8 0.7 copy-done.5
  45.4 1.3 shard_map.60
  46.7 3.8 %all-to-all-start.1 = ((f32[16,48,128]{2,1,0:T(8,128)}), f32[16,48,128]{2,1,0:T(8,128)S(1)}, u32[]{:S(2)}, u32[]{:S(2)}) async-start(f32[16,48,128]{2,1,0:T(8,128)} %bitcast.7), calls=%async_computation.1 | async-start | bytes 786432 | tf_op jit(solution)/shard_map/all_to_all | solution.py:439
  50.6 0.0 copy-done
  50.6 2.4 %shard_map.62 = (f32[8,2,128,128]{3,2,1,0:T(8,128)S(1)}, f32[4,2,128,128]{3,2,1,0:T(8,128)}, f32[4,2,128,128]{3,2,1,0:T(8,128)}) custom-call(s32[2]{0:T(128)S(1)} %pad_add_fusion.ids, f32[2048,128]{1,0:T(8,128)S(1)} %bitcast.39), custom_call_target="tpu_custom_call" | custom-call | flops 20000000 | bytes 4194304 | tf_op jit(solution)/shard_map/pallas_call | solution.py:448
  53.0 1.0 copy-done.2
  54.0 0.0 collective-permute-start.5
  54.0 3.1 %collective-permute-start.6 = (f32[4,2,128,128]{3,2,1,0:T(8,128)}, f32[4,2,128,128]{3,2,1,0:T(8,128)}, u32[]{:S(2)}, u32[]{:S(2)}) collective-permute-start(f32[4,2,128,128]{3,2,1,0:T(8,128)} %get-tuple-element.18), channel_id=1, source_target_pairs={{2,4},{3,5},{4,2},{5,3},{10,12},{11,13},{12,10},{13,11},{18,20},{1... | collective-permute-start | bytes 1572872 | tf_op jit(solution)/shard_map/ppermute | solution.py:433
  57.1 2.6 %all-to-all-done.1 = f32[16,48,128]{2,1,0:T(8,128)S(1)} async-done(((f32[16,48,128]{2,1,0:T(8,128)}), f32[16,48,128]{2,1,0:T(8,128)S(1)}, u32[]{:S(2)}, u32[]{:S(2)}) %all-to-all-start.1) | async-done | bytes 393248 | tf_op jit(solution)/shard_map/all_to_all | solution.py:439
  59.7 1.9 %collective-permute-start.2 = (f32[768,128]{1,0:T(8,128)S(1)}, f32[768,128]{1,0:T(8,128)}, u32[]{:S(2)}, u32[]{:S(2)}) collective-permute-start(f32[768,128]{1,0:T(8,128)S(1)} %bitcast.34), channel_id=1, source_target_pairs={{1,2},{3,4},{5,6},{2,1},{4,3},{6,5},{9,10},{11,12},{13,14},{10,9},... | collective-permute-start | bytes 1179656 | tf_op jit(solution)/shard_map/ppermute | solution.py:433
  61.6 0.0 collective-permute-done.4
  61.6 0.1 collective-permute-start.1
  61.7 0.0 copy-done.7
  61.7 0.1 copy.6.angles
  61.8 2.2 %shard_map.61 = (f32[24,128,128]{2,1,0:T(8,128)S(1)}, f32[24,128,128]{2,1,0:T(8,128)S(1)}) custom-call(f32[768,128]{1,0:T(8,128)S(1)} %bitcast.36), custom_call_target="tpu_custom_call" | custom-call | flops 20000000 | bytes 4194304 | tf_op jit(solution)/shard_map/pallas_call | solution.py:465
  64.1 0.0 collective-permute-done.3
  64.1 1.6 %shard_map.63 = (f32[8,2,128,128]{3,2,1,0:T(8,128)S(1)}, f32[8,2,128,128]{3,2,1,0:T(8,128)S(1)}) custom-call(f32[2048,128]{1,0:T(8,128)S(1)} %bitcast.41, f32[2048,128]{1,0:T(8,128)S(1)} %bitcast.40), custom_call_target="tpu_custom_call" | custom-call | flops 20000000 | bytes 4194304 | tf_op jit(solution)/shard_map/pallas_call | solution.py:455
  65.7 0.0 collective-permute-done.5.far_e
  65.7 4.0 %collective-permute-done.6.far_o = f32[4,2,128,128]{3,2,1,0:T(8,128)} collective-permute-done((f32[4,2,128,128]{3,2,1,0:T(8,128)}, f32[4,2,128,128]{3,2,1,0:T(8,128)}, u32[]{:S(2)}, u32[]{:S(2)}) %collective-permute-start.6) | collective-permute-done | bytes 524320 | tf_op jit(solution)/shard_map/ppermute | solution.py:433
  69.7 0.0 copy-done.3
  69.7 5.7 %shard_map.64.w1 = f32[24,2,128,128]{3,2,1,0:T(8,128)S(1)} custom-call(s32[2]{0:T(128)S(1)} %pad_add_fusion.ids, f32[8,2,128,128]{3,2,1,0:T(8,128)S(1)} %copy-done.3, f32[8,2,128,128]{3,2,1,0:T(8,128)S(1)} %get-tuple-element.15.halo_e, f32[8,2,128,128]{3,2,1,0:T(8,128)S(1)} %get-tuple-element.16.halo_o, f32[4,2,128,128]{3,2,1,0:T(8,128)} %collective-permute-done.5.far_e, ...), custom_call_target="tpu_custom_call" | custom-call | flops 20000000 | bytes 4194304 | tf_op jit(solution)/shard_map/pallas_call | solution.py:463
  75.4 0.0 collective-permute-done.2.ph_o
  75.4 0.0 collective-permute-done.1.ph_e
  75.4 0.0 copy-start.6
  75.4 18.6 %shard_map.65 = (f32[768,128]{1,0:T(8,128)S(1)}, f32[4,2,128,128]{3,2,1,0:T(8,128)S(1)}, f32[4,2,128,128]{3,2,1,0:T(8,128)S(1)}) custom-call(s32[2]{0:T(128)S(1)} %pad_add_fusion.ids, s32[4,2]{1,0:T(4,128)S(1)} %copy.6.angles, f32[768,128]{1,0:T(8,128)} %collective-permute-done.1.ph_e, f32[768,128]{1,0:T(8,128)} %collective-permute-done.2.ph_o, ...), custom_call_target="tpu_custom_call" | custom-call | flops 20000000 | bytes 4194304 | tf_op jit(solution)/shard_map/pallas_call | solution.py:469
  94.1 0.1 collective-permute-start.7
  94.2 1.9 %collective-permute-start.8 = (f32[4,2,128,128]{3,2,1,0:T(8,128)S(1)}, f32[4,2,128,128]{3,2,1,0:T(8,128)S(1)}, u32[]{:S(2)}, u32[]{:S(2)}) collective-permute-start(f32[4,2,128,128]{3,2,1,0:T(8,128)S(1)} %get-tuple-element.20.sent_o), channel_id=1, source_target_pairs={{1,2},{3,4},{5,6},{2,1},{4,3},{6,5},{9,10},{11,12},{13,14},{10,9},... | collective-permute-start | bytes 1572872 | tf_op jit(solution)/shard_map/ppermute | solution.py:433
  96.1 16.4 %all_to_all.38 = f32[16,48,128]{2,1,0:T(8,128)S(1)} all-to-all(f32[16,48,128]{2,1,0:T(8,128)S(1)} %bitcast.45), channel_id=1, replica_groups={{0,8,16,24,32,40,48,56,64,72,80,88,96,104,112,120},{128,136,144,152,160..., dimensions={0} | all-to-all | bytes 786432 | tf_op jit(solution)/shard_map/all_to_all | solution.py:439
  112.6 1.1 collective-permute-start.9
  113.7 6.7 %collective-permute-done.9.other = f32[2,3,8,128]{3,2,1,0:T(8,128)S(1)} collective-permute-done((f32[2,3,8,128]{3,2,1,0:T(8,128)S(1)}, f32[2,3,8,128]{3,2,1,0:T(8,128)S(1)}, u32[]{:S(2)}, u32[]{:S(2)}) %collective-permute-start.9) | collective-permute-done | bytes 24608 | tf_op jit(solution)/shard_map/ppermute | solution.py:477
  120.4 0.0 copy-done.6
  120.4 0.6 shard_map.68
  121.0 12.3 %all_to_all.39 = f32[16,16,128]{2,1,0:T(8,128)S(1)} all-to-all(f32[16,16,128]{2,1,0:T(8,128)S(1)} %bitcast.43), channel_id=1, replica_groups={{0,8,16,24,32,40,48,56,64,72,80,88,96,104,112,120},{128,136,144,152,160..., dimensions={0} | all-to-all | bytes 262144 | tf_op jit(solution)/shard_map/all_to_all | solution.py:439
  133.3 0.7 shard_map.69
  133.9 0.0 collective-permute-done.7.got_e
  133.9 0.0 collective-permute-done.8.got_o
  133.9 4.3 %shard_map.66 = f32[2048,128]{1,0:T(8,128)} custom-call(s32[2]{0:T(128)S(1)} %pad_add_fusion.ids, f32[4,2,128,128]{3,2,1,0:T(8,128)S(1)} %get-tuple-element.19.sent_e, f32[4,2,128,128]{3,2,1,0:T(8,128)S(1)} %get-tuple-element.20.sent_o, f32[4,2,128,128]{3,2,1,0:T(8,128)S(1)} %collective-permute-done.7.got_e, f32[4,2,128,128]{3,2,1,0:T(8,128)S(1)} %collective-permute-done.8.got_o), custom_call_target="tpu_custom_call" | custom-call | flops 20000000 | bytes 4194304 | tf_op jit(solution)/shard_map/pallas_call | solution.py:482
  (7 shorter events, 0.0 us)
Async XLA Ops:
  0.6 49.9 %copy-start = (f32[4,2,8,4096]{3,2,1,0:T(8,128)S(1)}, f32[4,2,8,4096]{3,2,1,0:T(8,128)}, u32[]{:S(2)}) copy-start(f32[4,2,8,4096]{3,2,1,0:T(8,128)} %param.7) | copy-start | bytes 3145732
  0.6 61.0 %collective-permute-start.4 = (f32[4,2,8,4096]{3,2,1,0:T(8,128)}, f32[4,2,8,4096]{3,2,1,0:T(8,128)S(1)}, u32[]{:S(2)}, u32[]{:S(2)}) collective-permute-start(f32[4,2,8,4096]{3,2,1,0:T(8,128)} %param.7), channel_id=1, source_target_pairs={{1,2},{3,4},{5,6},{2,1},{4,3},{6,5},{9,10},{11,12},{13,14},{10,9},... | collective-permute-start | bytes 3145736 | tf_op jit(solution)/shard_map/ppermute | solution.py:433
  2.7 23.6 %collective-permute-start = (f32[32,8,128]{2,1,0:T(8,128)}, f32[32,8,128]{2,1,0:T(8,128)S(1)}, u32[]{:S(2)}, u32[]{:S(2)}) collective-permute-start(f32[32,8,128]{2,1,0:T(8,128)} %bitcast.46), channel_id=1, source_target_pairs={{0,128},{8,136},{16,144},{24,152},{32,160},{40,168},{48,176},{56,1... | collective-permute-start | bytes 393224 | tf_op jit(solution)/shard_map/ppermute | solution.py:446
  9.5 54.6 %collective-permute-start.3 = (f32[4,2,8,4096]{3,2,1,0:T(8,128)}, f32[4,2,8,4096]{3,2,1,0:T(8,128)S(1)}, u32[]{:S(2)}, u32[]{:S(2)}) collective-permute-start(f32[4,2,8,4096]{3,2,1,0:T(8,128)} %param.7), channel_id=1, source_target_pairs={{0,1},{1,0},{2,3},{3,2},{4,5},{5,4},{6,7},{7,6},{8,9},{9,8},{10,11... | collective-permute-start | bytes 3145736 | tf_op jit(solution)/shard_map/ppermute | solution.py:434
  26.3 0.9 copy-start.4
  27.2 0.7 copy-start.1
  27.9 33.8 %copy-start.7 = (s32[4,2]{0,1:T(2,128)S(1)}, s32[4,2]{0,1:T(2,128)}, u32[]{:S(2)}) copy-start(s32[4,2]{0,1:T(2,128)} %param.4) | copy-start | bytes 100
  27.9 16.8 %all-to-all-start = ((f32[16,32,128]{2,1,0:T(8,128)}), f32[16,32,128]{2,1,0:T(8,128)S(1)}, u32[]{:S(2)}, u32[]{:S(2)}) async-start(f32[16,32,128]{2,1,0:T(8,128)} %bitcast.42), calls=%async_computation | async-start | bytes 524288 | tf_op jit(solution)/shard_map/all_to_all | solution.py:439
  44.8 0.7 copy-start.5
  46.7 12.9 %all-to-all-start.1 = ((f32[16,48,128]{2,1,0:T(8,128)}), f32[16,48,128]{2,1,0:T(8,128)S(1)}, u32[]{:S(2)}, u32[]{:S(2)}) async-start(f32[16,48,128]{2,1,0:T(8,128)} %bitcast.7), calls=%async_computation.1 | async-start | bytes 786432 | tf_op jit(solution)/shard_map/all_to_all | solution.py:439
  53.0 1.0 copy-start.2
  54.0 15.7 %copy-start.3 = (f32[8,2,128,128]{3,2,1,0:T(8,128)S(1)}, f32[8,2,128,128]{3,2,1,0:T(8,128)}, u32[]{:S(2)}) copy-start(f32[8,2,128,128]{3,2,1,0:T(8,128)} %copy-done.2) | copy-start | bytes 3145732
  54.0 11.8 %collective-permute-start.5 = (f32[4,2,128,128]{3,2,1,0:T(8,128)}, f32[4,2,128,128]{3,2,1,0:T(8,128)}, u32[]{:S(2)}, u32[]{:S(2)}) collective-permute-start(f32[4,2,128,128]{3,2,1,0:T(8,128)} %get-tuple-element.17), channel_id=1, source_target_pairs={{0,2},{1,3},{2,0},{3,1},{4,6},{5,7},{6,4},{7,5},{8,10},{9,11},{10,... | collective-permute-start | bytes 1572872 | tf_op jit(solution)/shard_map/ppermute | solution.py:434
  54.0 15.7 %collective-permute-start.6 = (f32[4,2,128,128]{3,2,1,0:T(8,128)}, f32[4,2,128,128]{3,2,1,0:T(8,128)}, u32[]{:S(2)}, u32[]{:S(2)}) collective-permute-start(f32[4,2,128,128]{3,2,1,0:T(8,128)} %get-tuple-element.18), channel_id=1, source_target_pairs={{2,4},{3,5},{4,2},{5,3},{10,12},{11,13},{12,10},{13,11},{18,20},{1... | collective-permute-start | bytes 1572872 | tf_op jit(solution)/shard_map/ppermute | solution.py:433
  59.7 15.7 %collective-permute-start.2 = (f32[768,128]{1,0:T(8,128)S(1)}, f32[768,128]{1,0:T(8,128)}, u32[]{:S(2)}, u32[]{:S(2)}) collective-permute-start(f32[768,128]{1,0:T(8,128)S(1)} %bitcast.34), channel_id=1, source_target_pairs={{1,2},{3,4},{5,6},{2,1},{4,3},{6,5},{9,10},{11,12},{13,14},{10,9},... | collective-permute-start | bytes 1179656 | tf_op jit(solution)/shard_map/ppermute | solution.py:433
  61.6 13.8 %collective-permute-start.1 = (f32[768,128]{1,0:T(8,128)S(1)}, f32[768,128]{1,0:T(8,128)}, u32[]{:S(2)}, u32[]{:S(2)}) collective-permute-start(f32[768,128]{1,0:T(8,128)S(1)} %bitcast.35), channel_id=1, source_target_pairs={{0,1},{1,0},{2,3},{3,2},{4,5},{5,4},{6,7},{7,6},{8,9},{9,8},{10,11... | collective-permute-start | bytes 1179656 | tf_op jit(solution)/shard_map/ppermute | solution.py:434
  75.4 45.0 %copy-start.6 = (s32[3]{0:T(128)S(1)}, s32[3]{0:T(128)}, u32[]{:S(2)}) copy-start(s32[3]{0:T(128)} %order.3) | copy-start | bytes 40
  94.1 39.8 %collective-permute-start.7 = (f32[4,2,128,128]{3,2,1,0:T(8,128)S(1)}, f32[4,2,128,128]{3,2,1,0:T(8,128)S(1)}, u32[]{:S(2)}, u32[]{:S(2)}) collective-permute-start(f32[4,2,128,128]{3,2,1,0:T(8,128)S(1)} %get-tuple-element.19.sent_e), channel_id=1, source_target_pairs={{0,1},{1,0},{2,3},{3,2},{4,5},{5,4},{6,7},{7,6},{8,9},{9,8},{10,11... | collective-permute-start | bytes 1572872 | tf_op jit(solution)/shard_map/ppermute | solution.py:434
  94.2 39.8 %collective-permute-start.8 = (f32[4,2,128,128]{3,2,1,0:T(8,128)S(1)}, f32[4,2,128,128]{3,2,1,0:T(8,128)S(1)}, u32[]{:S(2)}, u32[]{:S(2)}) collective-permute-start(f32[4,2,128,128]{3,2,1,0:T(8,128)S(1)} %get-tuple-element.20.sent_o), channel_id=1, source_target_pairs={{1,2},{3,4},{5,6},{2,1},{4,3},{6,5},{9,10},{11,12},{13,14},{10,9},... | collective-permute-start | bytes 1572872 | tf_op jit(solution)/shard_map/ppermute | solution.py:433
  112.6 7.8 %collective-permute-start.9 = (f32[2,3,8,128]{3,2,1,0:T(8,128)S(1)}, f32[2,3,8,128]{3,2,1,0:T(8,128)S(1)}, u32[]{:S(2)}, u32[]{:S(2)}) collective-permute-start(f32[2,3,8,128]{3,2,1,0:T(8,128)S(1)} %shard_map.67.mine), channel_id=1, source_target_pairs={{0,128},{8,136},{16,144},{24,152},{32,160},{40,168},{48,176},{56,1... | collective-permute-start | bytes 73736 | tf_op jit(solution)/shard_map/ppermute | solution.py:477

commit v6 on v5

--- a/solution.py
+++ b/solution.py
@@ -76,7 +76,7 @@
     return out
 
 
-def step(row, src, rows, base, h, powers, factor, write):
+def step(row, src, rows, base, h, powers, factor, write, outs=()):
     prev = src
     for n, dst in enumerate(powers):
         lo, count = base - h + 1 + n, ROWS + 2 * (h - 1 - n)
@@ -111,33 +111,36 @@
                 write(r + q, j, even[0] - odd[1], even[1] + odd[0])
         return 0
 
-    lax.fori_loop(0, (ROWS + 2 * (h - 4)) // 2, last, 0)
+    pairs = (ROWS + 2 * (h - 4)) // 2
+    parts = len(outs) or 1
+    for n in range(parts):
+        lax.fori_loop(n * pairs // parts, (n + 1) * pairs // parts, last, 0)
+        if outs:
+            outs[n].start()
 
 
 def natural(g, k, r):
     return pl.ds((g * 2 + k) * TILES * ROWS + r, TILES, stride=ROWS)
 
 
-def turn_rows(cot, out):
+def turned(cot, k, r):
+    return jnp.concatenate([cot[natural(g, k, r), :] for g in range(4)], axis=0).T
+
+
+def split_kernel(ids, cot, out, send_e, send_o, own, sem):
     def body(r, _):
         for k in range(2):
-            out[r, k] = jnp.concatenate([cot[natural(g, k, r), :] for g in range(4)], axis=0).T
+            own[r, k] = turned(cot, k, r)
         return 0
 
     lax.fori_loop(0, ROWS, body, 0)
-
-
-def split_kernel(ids, cot, out, send_e, send_o):
-    turn_rows(cot, out)
+    keep = pltpu.make_async_copy(own, out, sem)
+    keep.start()
     upper = (ids[0] >> 1) & 1
     for r in range(4):
-        send_e[r] = out[r + 4 * (1 - upper)]
-        send_o[r] = out[r + 4 * upper]
-
-
-def halo_kernel(cot_e, cot_o, out_e, out_o):
-    turn_rows(cot_e, out_e)
-    turn_rows(cot_o, out_o)
+        send_e[r] = own[r + 4 * (1 - upper)]
+        send_o[r] = own[r + 4 * upper]
+    keep.wait()
 
 
 def put(dst, at, src, n):
@@ -149,21 +152,42 @@
     lax.fori_loop(0, n, body, 0)
 
 
-def adjoint_kernel(ids, own, halo_e, halo_o, far_e, far_o, out, u, l1, l2, l3):
+def adjoint_kernel(ids, own, cot_e, cot_o, far_e, far_o, out,
+                   own_v, near_e, near_o, res, u, l1, l2, l3, sems):
     row = ids[0]
     odd, upper = row & 1, (row >> 1) & 1
-    put(u, 12, own, 8)
-    put(u, 20 - 16 * odd, halo_e, 8)
-    put(u, 4 + 16 * odd, halo_o, 8)
+    ins = [
+        pltpu.make_async_copy(a, b, sems.at[n])
+        for n, (a, b) in enumerate(((cot_e, near_e), (cot_o, near_o), (own, own_v)))
+    ]
+    for c in ins:
+        c.start()
+    for c, near, at in ((ins[0], near_e, 20 - 16 * odd), (ins[1], near_o, 4 + 16 * odd)):
+        c.wait()
+
+        def turn(r, _, near=near, at=at):
+            for k in range(2):
+                u[at + r, k, 8:136, :] = turned(near, k, r)
+            return 0
+
+        lax.fori_loop(0, ROWS, turn, 0)
+    ins[2].wait()
+    put(u, 12, own_v, 8)
     put(u, 28 - 28 * upper, far_e, 4)
     put(u, 28 * upper, far_o, 4)
     fill_pads(u, 32)
 
     def write(r, j, re, im):
-        out[r - 4, 0, chunk(j), :] = re
-        out[r - 4, 1, chunk(j), :] = im
-
-    step(row, u, 32, 12, 12, (l1, l2, l3), -rate_scale, write)
+        res[r - 4, 0, chunk(j), :] = re
+        res[r - 4, 1, chunk(j), :] = im
+
+    outs = [
+        pltpu.make_async_copy(res.at[8 * n:8 * n + 8], out.at[8 * n:8 * n + 8], sems.at[3 + n])
+        for n in range(3)
+    ]
+    step(row, u, 32, 12, 12, (l1, l2, l3), -rate_scale, write, outs)
+    for c in outs:
+        c.wait()
 
 
 def exit_kernel(ids, sent_e, sent_o, got_e, got_o, out, u, l1, l2, l3, res):
@@ -219,11 +243,13 @@
     lax.fori_loop(0, LAYERS * ROWS // 2, body, 0)
 
 
-def main_kernel(ids, angles, ph_e, ph_o, cos_own, sin_own, w1,
+def main_kernel(ids, angles, ph_e, ph_o, cos_own, sin_own, w1_far,
                 terms, last_e, last_o,
-                cos_n, sin_n, cosr, sinr, beam, u, v, w, w2, raw, l1, l2, l3):
+                cos_n, sin_n, cosr, sinr, beam, u, v, w, w2, raw, l1, l2, l3, w1, sem):
     row = ids[0]
     odd = row & 1
+    fetch = pltpu.make_async_copy(w1_far, w1, sem)
+    fetch.start()
     for ph, above in ((ph_e, odd), (ph_o, 1 - odd)):
         trig_tables(ph, cos_n, sin_n)
         first = (HALO + ROWS) * (1 - above)
@@ -315,6 +341,7 @@
     def own(ref):
         return lambda r, k: ref[HALO + r, k, 8:136, :]
 
+    fetch.wait()
     term(2, lambda r, k: w1[HALO + r, k], own(w2))
 
     def back(r, _):
@@ -390,6 +417,14 @@
     return pl.BlockSpec(memory_space=pltpu.VMEM)
 
 
+def hbm():
+    return pl.BlockSpec(memory_space=pltpu.HBM)
+
+
+def in_hbm(x):
+    return pltpu.with_memory_space_constraint(x, pltpu.HBM)
+
+
 def sm():
     return pl.BlockSpec(memory_space=pltpu.SMEM)
 
@@ -402,6 +437,10 @@
     return shape(rows, 2, 128, 128)
 
 
+def field_hbm(rows):
+    return pltpu.HBM((rows, 2, 128, 128), jnp.float32)
+
+
 def scr(*dims):
     return pltpu.VMEM(dims, jnp.float32)
 
@@ -410,9 +449,10 @@
     return scr(rows, 2, PAD, 128)
 
 
-def call(kernel, ins, outs, scratch, mib):
+def call(kernel, ins, outs, scratch, mib, out_specs=None):
     return pl.pallas_call(
-        kernel, out_shape=outs, in_specs=ins, out_specs=jax.tree.map(lambda _: vm(), outs),
+        kernel, out_shape=outs, in_specs=ins,
+        out_specs=out_specs or jax.tree.map(lambda _: vm(), outs),
         scratch_shapes=scratch,
         compiler_params=pltpu.CompilerParams(vmem_limit_bytes=mib << 20),
         cost_estimate=pl.CostEstimate(flops=20_000_000, bytes_accessed=4 << 20, transcendentals=0),
@@ -446,32 +486,35 @@
     other = lax.ppermute(mine, "illum", swap)
     cot_e, cot_o = meet(cotangent, cotangent, 1)
     own, send_e, send_o = call(
-        split_kernel, [sm(), vm()], (field(8), field(4), field(4)), [], 6)(
+        split_kernel, [sm(), vm()], (field_hbm(8), field(4), field(4)),
+        [scr(8, 2, 128, 128), pltpu.SemaphoreType.DMA], 6, (hbm(), vm(), vm()))(
             ids, rows_first(cotangent))
     far_e, far_o = meet(send_e, send_o, 2)
     dealt = call(deal_kernel, [vm()] * 2, shape(PLANE, 2, 2, ROWS, 128), [], 2)(
         mine, other)
     got = exchange(dealt)
-    halo_e, halo_o = call(halo_kernel, [vm()] * 2, (field(8),) * 2, [], 6)(
-        rows_first(cot_e), rows_first(cot_o))
     whole = call(pick_kernel, [sm(), sm(), vm()], shape(PLANE, 2, LAYERS, ROWS, 128), [],
                  2)(ids, depth_order, got)
     phases = exchange(whole).reshape(-1, 128)
     ph_e, ph_o = meet(phases, phases, 1)
 
     table = scr(TILES * LAYERS * ROWS, 128)
-    w1 = call(adjoint_kernel, [sm()] + [vm()] * 5, field(EXT), [wide(32)] * 4,
-              20)(ids, own, halo_e, halo_o, far_e, far_o)
+    w1 = call(
+        adjoint_kernel, [sm()] + [hbm()] * 3 + [vm()] * 2, field_hbm(EXT),
+        [scr(8, 2, 128, 128), scr(2048, 128), scr(2048, 128), scr(EXT, 2, 128, 128)]
+        + [wide(32)] * 4 + [pltpu.SemaphoreType.DMA((6,))], 27, hbm())(
+            ids, *map(in_hbm, (own, rows_first(cot_e), rows_first(cot_o))), far_e, far_o)
     cos_own, sin_own = call(
         phase_kernel, [vm()], (shape(LAYERS * ROWS, 128, 128),) * 2, [table] * 2,
         5)(phases)
     spreads = scr(LAYERS * EXT, 128, 128)
     terms, last_e, last_o = call(
-        main_kernel, [sm()] * 2 + [vm()] * 5,
+        main_kernel, [sm()] * 2 + [vm()] * 4 + [hbm()],
         (shape(TILES * LAYERS * ROWS, 128), field(4), field(4)),
         [table, table, spreads, spreads, scr(2, 128, 128)] + [wide(EXT)] * 4
-        + [scr(16, 2, 128, 128)] + [wide(EXT)] * 3, 40)(
-            ids, angles, ph_e, ph_o, cos_own, sin_own, w1)
+        + [scr(16, 2, 128, 128)] + [wide(EXT)] * 3
+        + [scr(EXT, 2, 128, 128), pltpu.SemaphoreType.DMA], 43)(
+            ids, angles, ph_e, ph_o, cos_own, sin_own, in_hbm(w1))
     parts = exchange(terms).reshape(PLANE, 2, LAYERS, ROWS, 128)
     half = call(sum_kernel, [vm()], shape(2, LAYERS, ROWS, 128), [], 2)(parts)
     half_z = lax.ppermute(half, "illum", swap)

time: 139 us -> 122 us (0.88)
  waiting for transfers between devices: 39.2 us -> 18.1 us
  starting transfers between devices: 28.5 us -> 35.2 us
  local copies, waits for them, and re-layouts: 3.34 us -> 1.01 us
  blocking collectives: 28.7 us -> 27 us
  Pallas kernels: 37.6 us -> 39.1 us
    ppermute x1, waiting for transfers between devices: 16.4 us -> 3.54 us  [forward_and_back(): other = lax.ppermute(mine, 'illum', swap)]
    ppermute x4, waiting for transfers between devices: 3.98 us -> 0.01 us  [meet(): got_o = lax.ppermute(x_o, 'row', odd)]
    ppermute x1, waiting for transfers between devices: 6.7 us -> 3.24 us  [forward_and_back(): half_z = lax.ppermute(half, 'illum', swap)]
    ppermute x1, starting transfers between devices: 1.12 us -> 4.58 us  [forward_and_back(): half_z = lax.ppermute(half, 'illum', swap)]
    ppermute x4, starting transfers between devices: 0.6 us -> 3.31 us  [meet(): got_e = lax.ppermute(x_e, 'row', even)]
    unnamed x17 -> x9, local copies, waits for them, and re-layouts: 3.34 us -> 1.01 us
    all_to_all x2, blocking collectives: 28.7 us -> 27 us  [exchange(): lax.all_to_all(flat, 'illum', 0, 0, axis_index_groups=groups, tiled=True)]
    pallas_call x4 -> x3, Pallas kernels: 28.4 us -> 29.2 us  [the longest x1 18.1 us: forward_and_back(): call(main_kernel, [sm()] * 2 + [vm()] * 4 + [hbm()], (shape(TILES * LAYER...]
  transfers between devices with their start and end apart: 12 -> 12, of which waited for: 5 -> 4; matrix products, arithmetic and copies ran while one was open for 0% -> 0% of each run, Pallas kernels for 11% -> 14%
where the time goes in v6:
time: 122 us; the launch traced here: 121 us
  Pallas kernels  39.1 us (32%)
  starting transfers between devices  35.2 us (29%)
  blocking collectives  27 us (22%)
  waiting for transfers between devices  18.1 us (15%)
    all_to_all x2, blocking collectives, exchange(): lax.all_to_all(flat, 'illum', 0, 0, axis_index_groups=groups, tiled=True)  27 us
    pallas_call x1, Pallas kernels, forward_and_back(): call(main_kernel, [sm()] * 2 + [vm()] * 4 + [hbm()], (shape(TILES * LAYER...  18.1 us
    all_to_all x2, waiting for transfers between devices, exchange(): lax.all_to_all(flat, 'illum', 0, 0, axis_index_groups=groups, tiled=True)  11.3 us
    all_to_all x2, starting transfers between devices, exchange(): lax.all_to_all(flat, 'illum', 0, 0, axis_index_groups=groups, tiled=True)  10.8 us
    ppermute x4, starting transfers between devices, meet(): got_o = lax.ppermute(x_o, 'row', odd)  10.1 us
    pallas_call x1, Pallas kernels, forward_and_back(): call(adjoint_kernel, [sm()] + [hbm()] * 3 + [vm()] * 2, field_hbm(EXT), [...  8.75 us
    ppermute x1, starting transfers between devices, forward_and_back(): other = lax.ppermute(mine, 'illum', swap)  6.38 us
    ppermute x1, starting transfers between devices, forward_and_back(): half_z = lax.ppermute(half, 'illum', swap)  4.58 us
  transfers between devices with their start and end apart: 12, of which 4 were waited for; matrix products, arithmetic and copies ran while one was open for 0% of the time, Pallas kernels for 14%

profile of v6, /device:TPU:32, one launch (start us, length us, event | category | flops | bytes accessed | tf_op | source)
XLA Modules:
  0.0 121.3 jit_solution(11030768728244920234)
XLA Ops:
  0.6 0.0 copy-start
  0.6 6.4 %collective-permute-start = (f32[32,8,128]{2,1,0:T(8,128)}, f32[32,8,128]{2,1,0:T(8,128)S(1)}, u32[]{:S(2)}, u32[]{:S(2)}) collective-permute-start(f32[32,8,128]{2,1,0:T(8,128)} %bitcast.43), channel_id=1, source_target_pairs={{0,128},{8,136},{16,144},{24,152},{32,160},{40,168},{48,176},{56,1... | collective-permute-start | bytes 393224 | tf_op jit(solution)/shard_map/ppermute | solution.py:486
  7.0 2.1 %collective-permute-start.4 = (f32[4,2,8,4096]{3,2,1,0:T(8,128)}, f32[4,2,8,4096]{3,2,1,0:T(8,128)}, u32[]{:S(2)}, u32[]{:S(2)}) collective-permute-start(f32[4,2,8,4096]{3,2,1,0:T(8,128)} %param.7), channel_id=1, source_target_pairs={{1,2},{3,4},{5,6},{2,1},{4,3},{6,5},{9,10},{11,12},{13,14},{10,9},... | collective-permute-start | bytes 3145736 | tf_op jit(solution)/shard_map/ppermute | solution.py:473
  9.1 1.1 collective-permute-start.3
  10.1 3.5 %collective-permute-done.other = f32[32,8,128]{2,1,0:T(8,128)S(1)} collective-permute-done((f32[32,8,128]{2,1,0:T(8,128)}, f32[32,8,128]{2,1,0:T(8,128)S(1)}, u32[]{:S(2)}, u32[]{:S(2)}) %collective-permute-start) | collective-permute-done | bytes 131104 | tf_op jit(solution)/shard_map/ppermute | solution.py:486
  13.7 0.0 copy-start.1
  13.7 0.9 copy-done.1
  14.6 0.0 copy-start.2
  14.6 0.7 shard_map.59
  15.3 0.0 copy-start.3
  15.3 7.2 %all-to-all-start = ((f32[16,32,128]{2,1,0:T(8,128)}), f32[16,32,128]{2,1,0:T(8,128)S(1)}, u32[]{:S(2)}, u32[]{:S(2)}) async-start(f32[16,32,128]{2,1,0:T(8,128)} %bitcast.5), calls=%async_computation | async-start | bytes 524288 | tf_op jit(solution)/shard_map/all_to_all | solution.py:479
  22.5 0.1 pad_add_fusion.ids
  22.6 0.0 copy-done
  22.6 2.3 %shard_map.62 = (f32[8,2,128,128]{3,2,1,0:T(8,128)}, f32[4,2,128,128]{3,2,1,0:T(8,128)S(1)}, f32[4,2,128,128]{3,2,1,0:T(8,128)S(1)}) custom-call(s32[2]{0:T(128)S(1)} %pad_add_fusion.ids, f32[2048,128]{1,0:T(8,128)S(1)} %bitcast.39), custom_call_target="tpu_custom_call" | custom-call | flops 20000000 | bytes 4194304 | tf_op jit(solution)/shard_map/pallas_call | solution.py:488
  24.9 0.1 collective-permute-start.5
  25.0 5.9 %all-to-all-done = f32[16,32,128]{2,1,0:T(8,128)S(1)} async-done(((f32[16,32,128]{2,1,0:T(8,128)}), f32[16,32,128]{2,1,0:T(8,128)S(1)}, u32[]{:S(2)}, u32[]{:S(2)}) %all-to-all-start) | async-done | bytes 262176 | tf_op jit(solution)/shard_map/all_to_all | solution.py:479
  31.0 0.0 copy-done.2
  31.0 1.3 %shard_map.60 = f32[16,2,3,8,128]{4,3,2,1,0:T(8,128)} custom-call(s32[2]{0:T(128)S(1)} %pad_add_fusion.ids, s32[3]{0:T(128)S(1)} %copy-done.2, f32[16,2,2,8,128]{4,3,2,1,0:T(8,128)S(1)} %bitcast.38), custom_call_target="tpu_custom_call" | custom-call | flops 20000000 | bytes 4194304 | tf_op jit(solution)/shard_map/pallas_call | solution.py:496
  32.3 3.7 %all-to-all-start.1 = ((f32[16,48,128]{2,1,0:T(8,128)}), f32[16,48,128]{2,1,0:T(8,128)S(1)}, u32[]{:S(2)}, u32[]{:S(2)}) async-start(f32[16,48,128]{2,1,0:T(8,128)} %bitcast.7), calls=%async_computation.1 | async-start | bytes 786432 | tf_op jit(solution)/shard_map/all_to_all | solution.py:479
  36.0 3.8 %collective-permute-start.6 = (f32[4,2,128,128]{3,2,1,0:T(8,128)S(1)}, f32[4,2,128,128]{3,2,1,0:T(8,128)S(1)}, u32[]{:S(2)}, u32[]{:S(2)}) collective-permute-start(f32[4,2,128,128]{3,2,1,0:T(8,128)S(1)} %get-tuple-element.14), channel_id=1, source_target_pairs={{2,4},{3,5},{4,2},{5,3},{10,12},{11,13},{12,10},{13,11},{18,20},{1... | collective-permute-start | bytes 1572872 | tf_op jit(solution)/shard_map/ppermute | solution.py:473
  39.7 5.3 %all-to-all-done.1 = f32[16,48,128]{2,1,0:T(8,128)S(1)} async-done(((f32[16,48,128]{2,1,0:T(8,128)}), f32[16,48,128]{2,1,0:T(8,128)S(1)}, u32[]{:S(2)}, u32[]{:S(2)}) %all-to-all-start.1) | async-done | bytes 393248 | tf_op jit(solution)/shard_map/all_to_all | solution.py:479
  45.1 1.9 %collective-permute-start.2 = (f32[768,128]{1,0:T(8,128)S(1)}, f32[768,128]{1,0:T(8,128)S(1)}, u32[]{:S(2)}, u32[]{:S(2)}) collective-permute-start(f32[768,128]{1,0:T(8,128)S(1)} %bitcast.34), channel_id=1, source_target_pairs={{1,2},{3,4},{5,6},{2,1},{4,3},{6,5},{9,10},{11,12},{13,14},{10,9},... | collective-permute-start | bytes 1179656 | tf_op jit(solution)/shard_map/ppermute | solution.py:473
  47.0 0.0 collective-permute-done.5.far_e
  47.0 2.1 %collective-permute-start.1 = (f32[768,128]{1,0:T(8,128)S(1)}, f32[768,128]{1,0:T(8,128)S(1)}, u32[]{:S(2)}, u32[]{:S(2)}) collective-permute-start(f32[768,128]{1,0:T(8,128)S(1)} %bitcast.35), channel_id=1, source_target_pairs={{0,1},{1,0},{2,3},{3,2},{4,5},{5,4},{6,7},{7,6},{8,9},{9,8},{10,11... | collective-permute-start | bytes 1179656 | tf_op jit(solution)/shard_map/ppermute | solution.py:474
  49.1 0.0 copy-done.3
  49.1 0.1 copy.6.angles
  49.2 2.2 %shard_map.61 = (f32[24,128,128]{2,1,0:T(8,128)S(1)}, f32[24,128,128]{2,1,0:T(8,128)S(1)}) custom-call(f32[768,128]{1,0:T(8,128)S(1)} %bitcast.36), custom_call_target="tpu_custom_call" | custom-call | flops 20000000 | bytes 4194304 | tf_op jit(solution)/shard_map/pallas_call | solution.py:507
  51.4 0.0 collective-permute-done.6.far_o
  51.4 0.0 collective-permute-done.4
  51.4 0.0 collective-permute-done.3
  51.4 8.8 %shard_map.63.w1_far = f32[24,2,128,128]{3,2,1,0:T(8,128)} custom-call(s32[2]{0:T(128)S(1)} %pad_add_fusion.ids, f32[8,2,128,128]{3,2,1,0:T(8,128)} %get-tuple-element.12.own, f32[2048,128]{1,0:T(8,128)} %bitcast.14.cot_e, f32[2048,128]{1,0:T(8,128)} %bitcast.17.cot_o, f32[4,2,128,128]{3,2,1,0:T(8,128)S(1)} %collective-permute-done.5.far_e, ...), custom_call_target="tpu_custom_call" | custom-call | flops 20000000 | bytes 4194304 | tf_op jit(solution)/shard_map/pallas_call | solution.py:502
  60.2 0.0 collective-permute-done.2.ph_o
  60.2 0.0 collective-permute-done.1.ph_e
  60.2 18.1 %shard_map.64 = (f32[768,128]{1,0:T(8,128)S(1)}, f32[4,2,128,128]{3,2,1,0:T(8,128)S(1)}, f32[4,2,128,128]{3,2,1,0:T(8,128)S(1)}) custom-call(s32[2]{0:T(128)S(1)} %pad_add_fusion.ids, s32[4,2]{1,0:T(4,128)S(1)} %copy.6.angles, f32[768,128]{1,0:T(8,128)S(1)} %collective-permute-done.1.ph_e, f32[768,128]{1,0:T(8,128)S(1)} %collective-permute-done.2.ph_o, ...), custom_call_target="tpu_custom_call" | custom-call | flops 20000000 | bytes 4194304 | tf_op jit(solution)/shard_map/pallas_call | solution.py:511
  78.3 0.1 collective-permute-start.7
  78.4 2.4 %collective-permute-start.8 = (f32[4,2,128,128]{3,2,1,0:T(8,128)S(1)}, f32[4,2,128,128]{3,2,1,0:T(8,128)S(1)}, u32[]{:S(2)}, u32[]{:S(2)}) collective-permute-start(f32[4,2,128,128]{3,2,1,0:T(8,128)S(1)} %get-tuple-element.16.sent_o), channel_id=1, source_target_pairs={{1,2},{3,4},{5,6},{2,1},{4,3},{6,5},{9,10},{11,12},{13,14},{10,9},... | collective-permute-start | bytes 1572872 | tf_op jit(solution)/shard_map/ppermute | solution.py:473
  80.8 14.7 %all_to_all.38 = f32[16,48,128]{2,1,0:T(8,128)S(1)} all-to-all(f32[16,48,128]{2,1,0:T(8,128)S(1)} %bitcast.42), channel_id=1, replica_groups={{0,8,16,24,32,40,48,56,64,72,80,88,96,104,112,120},{128,136,144,152,160..., dimensions={0} | all-to-all | bytes 786432 | tf_op jit(solution)/shard_map/all_to_all | solution.py:479
  95.6 4.6 %collective-permute-start.9 = (f32[2,3,8,128]{3,2,1,0:T(8,128)S(1)}, f32[2,3,8,128]{3,2,1,0:T(8,128)S(1)}, u32[]{:S(2)}, u32[]{:S(2)}) collective-permute-start(f32[2,3,8,128]{3,2,1,0:T(8,128)S(1)} %shard_map.66.mine), channel_id=1, source_target_pairs={{0,128},{8,136},{16,144},{24,152},{32,160},{40,168},{48,176},{56,1... | collective-permute-start | bytes 73736 | tf_op jit(solution)/shard_map/ppermute | solution.py:520
  100.1 3.2 %collective-permute-done.9.other = f32[2,3,8,128]{3,2,1,0:T(8,128)S(1)} collective-permute-done((f32[2,3,8,128]{3,2,1,0:T(8,128)S(1)}, f32[2,3,8,128]{3,2,1,0:T(8,128)S(1)}, u32[]{:S(2)}, u32[]{:S(2)}) %collective-permute-start.9) | collective-permute-done | bytes 24608 | tf_op jit(solution)/shard_map/ppermute | solution.py:520
  103.4 0.6 shard_map.67
  104.0 12.3 %all_to_all.39 = f32[16,16,128]{2,1,0:T(8,128)S(1)} all-to-all(f32[16,16,128]{2,1,0:T(8,128)S(1)} %bitcast.40), channel_id=1, replica_groups={{0,8,16,24,32,40,48,56,64,72,80,88,96,104,112,120},{128,136,144,152,160..., dimensions={0} | all-to-all | bytes 262144 | tf_op jit(solution)/shard_map/all_to_all | solution.py:479
  116.3 0.7 shard_map.68
  116.9 0.0 collective-permute-done.7.got_e
  116.9 0.0 collective-permute-done.8.got_o
  116.9 4.3 %shard_map.65 = f32[2048,128]{1,0:T(8,128)} custom-call(s32[2]{0:T(128)S(1)} %pad_add_fusion.ids, f32[4,2,128,128]{3,2,1,0:T(8,128)S(1)} %get-tuple-element.15.sent_e, f32[4,2,128,128]{3,2,1,0:T(8,128)S(1)} %get-tuple-element.16.sent_o, f32[4,2,128,128]{3,2,1,0:T(8,128)S(1)} %collective-permute-done.7.got_e, f32[4,2,128,128]{3,2,1,0:T(8,128)S(1)} %collective-permute-done.8.got_o), custom_call_target="tpu_custom_call" | custom-call | flops 20000000 | bytes 4194304 | tf_op jit(solution)/shard_map/pallas_call | solution.py:525
  (1 shorter events, 0.0 us)
Async XLA Ops:
  0.6 21.9 %copy-start = (f32[4,2,8,4096]{3,2,1,0:T(8,128)S(1)}, f32[4,2,8,4096]{3,2,1,0:T(8,128)}, u32[]{:S(2)}) copy-start(f32[4,2,8,4096]{3,2,1,0:T(8,128)} %param.7) | copy-start | bytes 3145732
  0.6 13.0 %collective-permute-start = (f32[32,8,128]{2,1,0:T(8,128)}, f32[32,8,128]{2,1,0:T(8,128)S(1)}, u32[]{:S(2)}, u32[]{:S(2)}) collective-permute-start(f32[32,8,128]{2,1,0:T(8,128)} %bitcast.43), channel_id=1, source_target_pairs={{0,128},{8,136},{16,144},{24,152},{32,160},{40,168},{48,176},{56,1... | collective-permute-start | bytes 393224 | tf_op jit(solution)/shard_map/ppermute | solution.py:486
  7.0 44.4 %collective-permute-start.4 = (f32[4,2,8,4096]{3,2,1,0:T(8,128)}, f32[4,2,8,4096]{3,2,1,0:T(8,128)}, u32[]{:S(2)}, u32[]{:S(2)}) collective-permute-start(f32[4,2,8,4096]{3,2,1,0:T(8,128)} %param.7), channel_id=1, source_target_pairs={{1,2},{3,4},{5,6},{2,1},{4,3},{6,5},{9,10},{11,12},{13,14},{10,9},... | collective-permute-start | bytes 3145736 | tf_op jit(solution)/shard_map/ppermute | solution.py:473
  9.1 42.3 %collective-permute-start.3 = (f32[4,2,8,4096]{3,2,1,0:T(8,128)}, f32[4,2,8,4096]{3,2,1,0:T(8,128)}, u32[]{:S(2)}, u32[]{:S(2)}) collective-permute-start(f32[4,2,8,4096]{3,2,1,0:T(8,128)} %param.7), channel_id=1, source_target_pairs={{0,1},{1,0},{2,3},{3,2},{4,5},{5,4},{6,7},{7,6},{8,9},{9,8},{10,11... | collective-permute-start | bytes 3145736 | tf_op jit(solution)/shard_map/ppermute | solution.py:474
  13.7 0.9 copy-start.1
  14.6 16.4 %copy-start.2 = (s32[3]{0:T(128)S(1)}, s32[3]{0:T(128)}, u32[]{:S(2)}) copy-start(s32[3]{0:T(128)} %order.3) | copy-start | bytes 40
  15.3 33.8 %copy-start.3 = (s32[4,2]{0,1:T(2,128)S(1)}, s32[4,2]{0,1:T(2,128)}, u32[]{:S(2)}) copy-start(s32[4,2]{0,1:T(2,128)} %param.4) | copy-start | bytes 100
  15.3 15.6 %all-to-all-start = ((f32[16,32,128]{2,1,0:T(8,128)}), f32[16,32,128]{2,1,0:T(8,128)S(1)}, u32[]{:S(2)}, u32[]{:S(2)}) async-start(f32[16,32,128]{2,1,0:T(8,128)} %bitcast.5), calls=%async_computation | async-start | bytes 524288 | tf_op jit(solution)/shard_map/all_to_all | solution.py:479
  24.9 22.1 %collective-permute-start.5 = (f32[4,2,128,128]{3,2,1,0:T(8,128)S(1)}, f32[4,2,128,128]{3,2,1,0:T(8,128)S(1)}, u32[]{:S(2)}, u32[]{:S(2)}) collective-permute-start(f32[4,2,128,128]{3,2,1,0:T(8,128)S(1)} %get-tuple-element.13), channel_id=1, source_target_pairs={{0,2},{1,3},{2,0},{3,1},{4,6},{5,7},{6,4},{7,5},{8,10},{9,11},{10,... | collective-permute-start | bytes 1572872 | tf_op jit(solution)/shard_map/ppermute | solution.py:474
  32.3 12.8 %all-to-all-start.1 = ((f32[16,48,128]{2,1,0:T(8,128)}), f32[16,48,128]{2,1,0:T(8,128)S(1)}, u32[]{:S(2)}, u32[]{:S(2)}) async-start(f32[16,48,128]{2,1,0:T(8,128)} %bitcast.7), calls=%async_computation.1 | async-start | bytes 786432 | tf_op jit(solution)/shard_map/all_to_all | solution.py:479
  36.0 15.5 %collective-permute-start.6 = (f32[4,2,128,128]{3,2,1,0:T(8,128)S(1)}, f32[4,2,128,128]{3,2,1,0:T(8,128)S(1)}, u32[]{:S(2)}, u32[]{:S(2)}) collective-permute-start(f32[4,2,128,128]{3,2,1,0:T(8,128)S(1)} %get-tuple-element.14), channel_id=1, source_target_pairs={{2,4},{3,5},{4,2},{5,3},{10,12},{11,13},{12,10},{13,11},{18,20},{1... | collective-permute-start | bytes 1572872 | tf_op jit(solution)/shard_map/ppermute | solution.py:473
  45.1 15.1 %collective-permute-start.2 = (f32[768,128]{1,0:T(8,128)S(1)}, f32[768,128]{1,0:T(8,128)S(1)}, u32[]{:S(2)}, u32[]{:S(2)}) collective-permute-start(f32[768,128]{1,0:T(8,128)S(1)} %bitcast.34), channel_id=1, source_target_pairs={{1,2},{3,4},{5,6},{2,1},{4,3},{6,5},{9,10},{11,12},{13,14},{10,9},... | collective-permute-start | bytes 1179656 | tf_op jit(solution)/shard_map/ppermute | solution.py:473
  47.0 13.2 %collective-permute-start.1 = (f32[768,128]{1,0:T(8,128)S(1)}, f32[768,128]{1,0:T(8,128)S(1)}, u32[]{:S(2)}, u32[]{:S(2)}) collective-permute-start(f32[768,128]{1,0:T(8,128)S(1)} %bitcast.35), channel_id=1, source_target_pairs={{0,1},{1,0},{2,3},{3,2},{4,5},{5,4},{6,7},{7,6},{8,9},{9,8},{10,11... | collective-permute-start | bytes 1179656 | tf_op jit(solution)/shard_map/ppermute | solution.py:474
  78.3 38.6 %collective-permute-start.7 = (f32[4,2,128,128]{3,2,1,0:T(8,128)S(1)}, f32[4,2,128,128]{3,2,1,0:T(8,128)S(1)}, u32[]{:S(2)}, u32[]{:S(2)}) collective-permute-start(f32[4,2,128,128]{3,2,1,0:T(8,128)S(1)} %get-tuple-element.15.sent_e), channel_id=1, source_target_pairs={{0,1},{1,0},{2,3},{3,2},{4,5},{5,4},{6,7},{7,6},{8,9},{9,8},{10,11... | collective-permute-start | bytes 1572872 | tf_op jit(solution)/shard_map/ppermute | solution.py:474
  78.4 38.5 %collective-permute-start.8 = (f32[4,2,128,128]{3,2,1,0:T(8,128)S(1)}, f32[4,2,128,128]{3,2,1,0:T(8,128)S(1)}, u32[]{:S(2)}, u32[]{:S(2)}) collective-permute-start(f32[4,2,128,128]{3,2,1,0:T(8,128)S(1)} %get-tuple-element.16.sent_o), channel_id=1, source_target_pairs={{1,2},{3,4},{5,6},{2,1},{4,3},{6,5},{9,10},{11,12},{13,14},{10,9},... | collective-permute-start | bytes 1572872 | tf_op jit(solution)/shard_map/ppermute | solution.py:473
  95.6 7.8 %collective-permute-start.9 = (f32[2,3,8,128]{3,2,1,0:T(8,128)S(1)}, f32[2,3,8,128]{3,2,1,0:T(8,128)S(1)}, u32[]{:S(2)}, u32[]{:S(2)}) collective-permute-start(f32[2,3,8,128]{3,2,1,0:T(8,128)S(1)} %shard_map.66.mine), channel_id=1, source_target_pairs={{0,128},{8,136},{16,144},{24,152},{32,160},{40,168},{48,176},{56,1... | collective-permute-start | bytes 73736 | tf_op jit(solution)/shard_map/ppermute | solution.py:520
